TPU v7x, 128 devices: a whole 4x4x4 slice. The times are simulated.
128 devices in a mesh: dp: 8 (over z, y_lo), cp: 16 (over x, y_hi, core).
Axes of the slice: x: 4, y: 4 (y_hi: 2, y_lo: 2; y = y_hi * 2 + y_lo), z: 4, core: 2. Of those that a mesh axis runs over, the one named last changes fastest.
Arguments:
- table_rows: bfloat16 [262144, 1024], P(('dp', 'cp')), may hold values from -6 to 6
- row_scales: float32 [262144], P(('dp', 'cp')), may hold values from 0.25 to 4
- owners: int32 [16384, 1], P(('dp', 'cp')), may hold values from 0 to 127; in each aligned block of 128 rows (0 to 127, 128 to 255, ...) at most 2 rows name the same one
- shard_rows: int32 [16384], P(('dp', 'cp')), may hold values from 0 to 2047
- history_lengths: int32 [8, 3], P('dp'), may hold values from 1 to 1024, 2048 in all within a row
- input_weight: bfloat16 [1024, 4096], replicated, may hold values from -0.1875 to 0.1875
- output_weight: bfloat16 [1024, 1024], replicated, may hold values from -0.1875 to 0.1875
- cotangent: bfloat16 [16384, 1024], P(('dp', 'cp')), may hold values from -6 to 6
Outputs:
- layer_out: bfloat16 [16384, 1024], P(('dp', 'cp'))
- table_grad: float32 [262144, 1024], P(('dp', 'cp'))
Inputs may be any that keep to these rules, and one draw needn't show every extreme that they name: `owners`: among the events of one device no shard is named more than 2 times, and some device names one shard exactly 2 times. `history_lengths`: the 3 lengths of a cycle group sum to 2048; the longest is exactly 1024.
All inputs are finite; a program needn't handle non-finite values.
Results may differ from a plain program's by a relative error of at most 0.0043.
Values may be sent and summed in bfloat16 or wider, within the bound.
No kernel may reach another device: no remote copies, remote signals or barrier semaphores. Data moves between devices by JAX's collectives and lax.ppermute only.
A program may use at most 128 MiB of HBM per device.

v0:
```python
import jax
import jax.numpy as jnp
from jax import lax
from jax.sharding import PartitionSpec as P

HEADS = 8


EPSILON = 1e-05


def doc_bounds(lengths, positions):
    ends_at = jnp.cumsum(lengths)
    begins_at = ends_at - lengths
    inside = (positions[:, None] >= begins_at[None, :]) & (positions[:, None] < ends_at[None, :])
    doc_first = jnp.sum(jnp.where(inside, begins_at[None, :], 0), axis=1)
    doc_length = jnp.sum(jnp.where(inside, lengths[None, :], 0), axis=1).astype(jnp.float32)
    return (doc_first, doc_length)


def normalize(values):
    center = jnp.mean(values, axis=-1, keepdims=True)
    shifted = values - center
    inv_spread = lax.rsqrt(jnp.mean(shifted * shifted, axis=-1, keepdims=True) + EPSILON)
    return (shifted * inv_spread, inv_spread)


def normalize_back(grad_in, normed, inv_spread):
    return inv_spread * (
        grad_in
        - jnp.mean(grad_in, axis=-1, keepdims=True)
        - normed * jnp.mean(grad_in * normed, axis=-1, keepdims=True)
    )


def score_block(queries, key_block, query_pos, query_first, key_pos):
    scaling = queries.shape[-1] ** (-0.5)
    scores = (
        jnp.einsum("qhe,khe->hqk", queries, key_block, preferred_element_type=jnp.float32) * scaling
    )
    allowed = (key_pos[None, :] >= query_first[:, None]) & (key_pos[None, :] <= query_pos[:, None])
    return (scores, allowed[None])


def forward_part(queries, key_block, value_block, query_pos, query_first, query_length, key_pos):
    scores, allowed = score_block(queries, key_block, query_pos, query_first, key_pos)
    weights = jnp.where(
        allowed, scores * jax.nn.sigmoid(scores) / query_length[None, :, None], 0.0
    ).astype(jnp.bfloat16)
    return jnp.einsum("hqk,khe->qhe", weights, value_block, preferred_element_type=jnp.float32)


def backward_part(
    queries, key_block, value_block, grad_out, query_pos, query_first, query_length, key_pos
):
    scores, allowed = score_block(queries, key_block, query_pos, query_first, key_pos)
    sigmoid_part = jax.nn.sigmoid(scores)
    weights = jnp.where(allowed, scores * sigmoid_part / query_length[None, :, None], 0.0).astype(
        jnp.bfloat16
    )
    grad_weights = jnp.einsum(
        "qhe,khe->hqk", grad_out, value_block, preferred_element_type=jnp.float32
    )
    silu_slope = sigmoid_part * (1.0 + scores * (1.0 - sigmoid_part))
    scaling = queries.shape[-1] ** (-0.5)
    grad_scores = jnp.where(
        allowed, grad_weights * silu_slope / query_length[None, :, None] * scaling, 0.0
    ).astype(jnp.bfloat16)
    grad_query = jnp.einsum(
        "hqk,khe->qhe", grad_scores, key_block, preferred_element_type=jnp.float32
    )
    grad_key = jnp.einsum("hqk,qhe->khe", grad_scores, queries, preferred_element_type=jnp.float32)
    grad_value = jnp.einsum("hqk,qhe->khe", weights, grad_out, preferred_element_type=jnp.float32)
    return (grad_query, grad_key, grad_value)


def sweep(kernel, running, key_total, block_size, lowest, highest):

    def advance(block_index, current):
        block_start = block_index * block_size
        needed = (block_start <= highest) & (block_start + block_size > lowest)
        return lax.cond(
            needed,
            lambda state: kernel(state, block_start, block_size),
            lambda state: state,
            current,
        )

    return lax.fori_loop(0, key_total // block_size, advance, running)


def per_device(
    table_rows,
    row_scales,
    owners,
    shard_rows,
    history_lengths,
    input_weight,
    output_weight,
    cotangent,
):
    row_count = owners.shape[0]
    model_width = table_rows.shape[1]
    head_count = HEADS
    head_size = model_width // head_count
    devices = lax.axis_size(("dp", "cp"))
    capacity = max(2, 2 * row_count // devices)
    target = owners[:, 0]
    matches = (target[:, None] == jnp.arange(devices, dtype=jnp.int32)[None, :]).astype(jnp.int32)
    before = jnp.cumsum(matches, axis=0) - matches
    ranked = jnp.sum(before * matches, axis=1)
    placed = target * capacity + ranked
    requests = jnp.zeros((devices * capacity,), jnp.int32).at[placed].set(shard_rows + 1)
    incoming = lax.all_to_all(
        requests.reshape(devices, capacity), ("dp", "cp"), split_axis=0, concat_axis=0, tiled=True
    ).reshape(-1)
    wanted = incoming > 0
    lookup = jnp.maximum(incoming - 1, 0)
    fetched = jnp.where(
        wanted[:, None], table_rows[lookup].astype(jnp.float32) * row_scales[lookup][:, None], 0.0
    )
    returned = lax.all_to_all(
        fetched.reshape(devices, capacity, model_width),
        ("dp", "cp"),
        split_axis=0,
        concat_axis=0,
        tiled=True,
    )
    embedded = returned.reshape(devices * capacity, model_width)[placed]
    normed, inv_embed = normalize(embedded)
    projected = jnp.dot(
        normed.astype(jnp.bfloat16), input_weight, preferred_element_type=jnp.float32
    )
    activated = (projected * jax.nn.sigmoid(projected)).astype(jnp.bfloat16)
    gate_rows = activated[:, :model_width]
    value_rows = activated[:, model_width : 2 * model_width]
    query_rows = activated[:, 2 * model_width : 3 * model_width]
    key_rows = activated[:, 3 * model_width :]
    lengths = history_lengths[0]
    cycle_pos = lax.axis_index("cp") * row_count + jnp.arange(row_count, dtype=jnp.int32)
    query_first, query_length = doc_bounds(lengths, cycle_pos)
    lowest = jnp.min(query_first)
    highest = cycle_pos[row_count - 1]
    key_all, value_all = (
        lax.all_gather(key_rows, "cp", axis=0, tiled=True),
        lax.all_gather(value_rows, "cp", axis=0, tiled=True),
    )
    key_total = key_all.shape[0]
    queries = query_rows.reshape(row_count, head_count, head_size)

    def key_slices(block_start, piece_size):
        key_block = key_all.reshape(piece_size, head_count, head_size)
        value_block = value_all.reshape(piece_size, head_count, head_size)
        key_pos = block_start + jnp.arange(piece_size, dtype=jnp.int32)
        return (key_block, value_block, key_pos)

    def forward_kernel(running, block_start, piece_size):
        key_block, value_block, key_pos = key_slices(block_start, piece_size)
        return running + forward_part(
            queries, key_block, value_block, cycle_pos, query_first, query_length, key_pos
        )

    zeros_local = jnp.zeros((row_count, head_count, head_size), jnp.float32)
    attention = sweep(forward_kernel, zeros_local, key_total, key_total, lowest, highest).reshape(
        row_count, model_width
    )
    attn_norm, inv_attn = normalize(attention)
    mixed = attn_norm * gate_rows.astype(jnp.float32)
    output = embedded + jnp.dot(
        mixed.astype(jnp.bfloat16), output_weight, preferred_element_type=jnp.float32
    )
    layer_out = output.astype(jnp.bfloat16)
    grad_mixed = jnp.einsum(
        "rk,dk->rd", cotangent, output_weight, preferred_element_type=jnp.float32
    )
    grad_gate = grad_mixed * attn_norm
    grad_attn = normalize_back(
        grad_mixed * gate_rows.astype(jnp.float32), attn_norm, inv_attn
    ).astype(jnp.bfloat16)
    grad_heads = grad_attn.reshape(row_count, head_count, head_size)
    zeros_all = jnp.zeros((key_total, head_count, head_size), jnp.float32)

    def backward_kernel(running, block_start, piece_size):
        key_block, value_block, key_pos = key_slices(block_start, piece_size)
        grad_query, grad_key, grad_value = backward_part(
            queries,
            key_block,
            value_block,
            grad_heads,
            cycle_pos,
            query_first,
            query_length,
            key_pos,
        )
        return (running[0] + grad_query, grad_key, grad_value)

    grad_query, grad_key_all, grad_value_all = sweep(
        backward_kernel, (zeros_local, zeros_all, zeros_all), key_total, key_total, lowest, highest
    )
    grad_key, grad_value = (
        lax.psum_scatter(
            grad_key_all.reshape(key_total, model_width), "cp", scatter_dimension=0, tiled=True
        ),
        lax.psum_scatter(
            grad_value_all.reshape(key_total, model_width), "cp", scatter_dimension=0, tiled=True
        ),
    )
    grad_act = jnp.concatenate(
        [grad_gate, grad_value, grad_query.reshape(row_count, model_width), grad_key], axis=1
    )
    sigmoid_part = jax.nn.sigmoid(projected)
    grad_proj = (grad_act * sigmoid_part * (1.0 + projected * (1.0 - sigmoid_part))).astype(
        jnp.bfloat16
    )
    grad_norm = jnp.einsum("rk,dk->rd", grad_proj, input_weight, preferred_element_type=jnp.float32)
    grad_embed = cotangent.astype(jnp.float32) + normalize_back(grad_norm, normed, inv_embed)
    outgoing = jnp.zeros((devices * capacity, model_width), jnp.float32).at[placed].set(grad_embed)
    arrived = lax.all_to_all(
        outgoing.reshape(devices, capacity, model_width),
        ("dp", "cp"),
        split_axis=0,
        concat_axis=0,
        tiled=True,
    ).reshape(devices * capacity, model_width)
    summed = (
        jnp.zeros(table_rows.shape, jnp.float32)
        .at[lookup]
        .add(jnp.where(wanted[:, None], arrived, 0.0))
    )
    table_grad = summed * row_scales[:, None]
    return (layer_out, table_grad)


def solution(mesh):
    return jax.shard_map(
        per_device,
        mesh=mesh,
        in_specs=(
            P(("dp", "cp"), None),
            P(("dp", "cp")),
            P(("dp", "cp"), None),
            P(("dp", "cp")),
            P("dp", None),
            P(),
            P(),
            P(("dp", "cp"), None),
        ),
        out_specs=(P(("dp", "cp"), None), P(("dp", "cp"), None)),
        check_vma=False,
    )
```

profile of v0, /device:TPU:1, one launch (start us, length us, event | category | flops | bytes accessed | tf_op | source)
XLA Modules:
  0.0 501.4 jit_solution(9689500098973985464)
XLA Ops:
  11.5 20.8 %all_to_all.19 = s32[128,1,2]{2,1,0:T(1,128)S(1)} all-to-all(s32[128,1,2]{2,1,0:T(1,128)S(1)} %bitcast.137), channel_id=1, replica_groups=mesh['dp'=8,'cp'=16] {'dp','cp'}, dimensions={0} | all-to-all | bytes 2048 | tf_op jit(solution)/shard_map/all_to_all | solution.py:114
  33.2 1.9 gather_fusion.1
  35.3 5.1 %gather_fusion = bf16[256,1024]{1,0:T(8,128)(2,1)} fusion(bf16[2048,1024]{1,0:T(8,128)(2,1)} %param.12, s32[1024]{0:T(1024)S(1)} %pad_clamp_fusion.1), kind=kCustom, calls=%fused_computation | custom fusion | bytes 1049600 | tf_op jit(solution)/shard_map/gather | solution.py:120
  43.6 5.6 %all-to-all-start.1 = ((f32[128,2,1024]{2,1,0:T(2,128)}), f32[128,2,1024]{2,1,0:T(2,128)}, u32[]{:S(2)}, u32[]{:S(2)}) async-start(f32[128,2,1024]{2,1,0:T(2,128)} %multiply_select_fusion), calls=%async_computation.1 | async-start | bytes 2097152 | tf_op jit(solution)/shard_map/all_to_all | solution.py:122
  49.2 18.6 %all-to-all-done.1 = f32[128,2,1024]{2,1,0:T(2,128)} async-done(((f32[128,2,1024]{2,1,0:T(2,128)}), f32[128,2,1024]{2,1,0:T(2,128)}, u32[]{:S(2)}, u32[]{:S(2)}) %all-to-all-start.1) | async-done | bytes 1048608 | tf_op jit(solution)/shard_map/all_to_all | solution.py:122
  67.9 1.9 reshape.277
  73.8 6.3 %multiply_convert_fusion = (bf16[128,4096]{1,0:T(8,128)(2,1)S(1)}, f32[128,4096]{1,0:T(8,128)}) fusion(bf16[1024,4096]{1,0:T(8,128)(2,1)} %param.17, f32[128,1024]{1,0:T(8,128)} %gather_fusion.2, f32[128]{0:T(128)S(1)} %add_rsqrt_fusion.1, f32[128]{0:T(128)S(1)} %broadcast_multiply_fusion.6), kind=kOutput, calls=%fused_computation.60 | convolution fusion | flops 1076756480 | bytes 12059648 | tf_op jit(solution)/shard_map/dot_general | solution.py:131
  85.7 49.2 %all-gather.5.cloned.1.call-done = bf16[2048,1024]{1,0:T(8,128)(2,1)} async-done(((bf16[128,1024]{1,0:T(8,128)(2,1)}), bf16[2048,1024]{1,0:T(8,128)(2,1)}) %all-gather.5.cloned.1.call-update) | async-done | bytes 4194320 | tf_op jit(solution)/shard_map/all_gather | solution.py:146
  134.9 57.9 %all-gather.3.cloned.1.call-done = bf16[2048,1024]{1,0:T(8,128)(2,1)} async-done(((bf16[128,1024]{1,0:T(8,128)(2,1)}), bf16[2048,1024]{1,0:T(8,128)(2,1)}) %all-gather.3.cloned.1.call-update) | async-done | bytes 4194320 | tf_op jit(solution)/shard_map/all_gather | solution.py:145
  192.9 8.3 %conditional.2 = (f32[128,8,128]{2,0,1:T(8,128)S(1)}) conditional(s32[]{:T(128)} %convert_element_type.56, f32[128,8,128]{2,0,1:T(8,128)S(1)} %broadcast_in_dim.116, (s32[128]{0:T(128)S(1)}, s32[128]{0:T(128)S(1)}, bf16[2048,1024]{1,0:T(8,128)(2,1)}, bf16[128,8,128]{2,1,0:T(8,128)(2,1)S(1)}, f32[128]{0:T(128)S(1)}, ...), branch_computations={%region_9.10_spmd, %region_10.11_spmd} | conditional | flops 1091436544 | bytes 10225160 | solution.py:82
  194.2 7.0 %fusion.8 = f32[128,8,128]{2,0,1:T(8,128)S(1)} fusion(f32[128,8,128]{2,0,1:T(8,128)S(1)} %get-tuple-element.88, f32[128]{0:T(128)S(1)} %get-tuple-element.116, pred[128,2048]{1,0:T(8,128)(4,1)} %fusion.13, bf16[128,8,128]{2,1,0:T(8,128)(2,1)S(1)} %get-tuple-element.214, bf16[2048,1024]{1,0:T(8,128)(2,1)} %get-tuple-element.117, ...), kind=kOutput, calls=%fused_computation.15 | convolution fusion | flops 1090650112 | bytes 9961984 | tf_op jit(solution)/shard_map/while/body/eval_jaxpr/cond/branch_1_fun/hqk,khe->qhe/dot_general | solution.py:50
  201.6 2.1 fusion.79
  203.7 2.0 fusion.88
  205.7 22.3 %conditional.3 = (f32[2048,8,128]{2,0,1:T(8,128)}, f32[2048,8,128]{2,0,1:T(8,128)S(1)}, f32[128,8,128]{2,0,1:T(8,128)S(1)}) conditional(s32[]{:T(128)} %convert_element_type.56, f32[128,8,128]{2,0,1:T(8,128)S(1)} %broadcast_in_dim.116, (s32[128]{0:T(128)S(1)}, s32[128]{0:T(128)S(1)}, bf16[128,1024]{1,0:T(8,128)(2,1)S(1)}, ...), branch_computations={%region_15.16_spmd, %region_16.17_spmd} | conditional | flops 2729312256 | bytes 103549008 | solution.py:82
  208.4 5.5 %select_convert_fusion.2 = bf16[8,128,2048]{2,1,0:T(8,128)(2,1)S(1)} fusion(f32[8,128,2048]{2,1,0:T(8,128)S(1)} %fusion.21, f32[128]{0:T(128)S(1)} %get-tuple-element.124, pred[128,2048]{1,0:T(8,128)(4,1)S(1)} %fusion.37, bf16[2048,1024]{1,0:T(8,128)(2,1)S(1)} %copy-done.9, bf16[128,1024]{1,0:T(8,128)(2,1)S(1)} %get-tuple-element.120), kind=kOutput, calls=%fused_computation.22 | convolution fusion | flops 564133888 | bytes 17302016 | tf_op jit(solution)/shard_map/while/body/eval_jaxpr/cond/branch_1_fun/qhe,khe->hqk/dot_general | solution.py:61
  213.8 2.0 copy-done.5
  217.3 3.7 convolution_bitcast_fusion
  221.0 7.0 %convolution_bitcast_fusion.1 = f32[2048,8,128]{2,0,1:T(8,128)} fusion(bf16[8,128,2048]{2,1,0:T(8,128)(2,1)} %copy-done.5, bf16[128,8,128]{2,1,0:T(8,128)(2,1)S(1)} %get-tuple-element.223), kind=kOutput, calls=%fused_computation.25 | convolution fusion | flops 536870912 | bytes 12845056 | tf_op jit(solution)/shard_map/while/body/eval_jaxpr/cond/branch_1_fun/hqk,qhe->khe/dot_general | solution.py:72
  228.0 4.4 copy_bitcast_fusion.1
  232.7 7.8 %copy_bitcast_fusion = f32[2048,1024]{1,0:T(8,128)} fusion(f32[2048,8,128]{2,0,1:T(8,128)} %get-tuple-element.148), kind=kLoop, calls=%fused_computation.52 | loop fusion | bytes 16777216 | tf_op jit(solution)/shard_map/reshape | solution.py:202
  240.5 2.0 copy_bitcast_fusion.2
  242.5 89.3 %reduce-scatter.3.cloned.1.call-done = f32[128,1024]{1,0:T(8,128)} async-done(((f32[2048,1024]{1,0:T(8,128)}), f32[128,1024]{1,0:T(8,128)}) %reduce-scatter.3.cloned.1.call-update) | async-done | bytes 524304 | tf_op jit(solution)/shard_map/reduce_scatter | solution.py:204
  331.8 105.4 %reduce-scatter.5.cloned.1.call-done = f32[128,1024]{1,0:T(8,128)} async-done(((f32[2048,1024]{1,0:T(8,128)}), f32[128,1024]{1,0:T(8,128)}) %reduce-scatter.5.cloned.1.call-update) | async-done | bytes 524304 | tf_op jit(solution)/shard_map/reduce_scatter | solution.py:201
  437.2 8.4 %fusion.90 = (f32[128]{0:T(128)S(1)}, f32[128]{0:T(128)S(1)}, f32[128,1024]{1,0:T(8,128)}) fusion(f32[128]{0:T(128)S(1)} %add_rsqrt_fusion.1, f32[128,1024]{1,0:T(8,128)S(1)} %copy-done.2, f32[128]{0:T(128)S(1)} %broadcast_multiply_fusion.6, bf16[1024,4096]{1,0:T(8,128)(2,1)} %param.17, f32[128,1024]{1,0:T(8,128)} %reduce-scatter.5.cloned.1.call-done, ...), kind=kOutput, calls=%fused_computation.132 | convolution fusion | flops 1080688384 | bytes 13633536 | tf_op jit(solution)/shard_map/rk,dk->rd/dot_general | solution.py:215
  445.6 2.7 scatter_custom_fusion.1
  448.3 2.9 reshape.284
  451.2 9.1 %all-to-all-start.2 = ((f32[128,2,1024]{2,1,0:T(2,128)}), f32[128,2,1024]{2,1,0:T(2,128)}, u32[]{:S(2)}, u32[]{:S(2)}) async-start(f32[128,2,1024]{2,1,0:T(2,128)} %reshape.284), calls=%async_computation.4 | async-start | bytes 2097152 | tf_op jit(solution)/shard_map/all_to_all | solution.py:218
  460.5 2.2 fusion.51
  462.6 16.3 %all-to-all-done.2 = f32[128,2,1024]{2,1,0:T(2,128)} async-done(((f32[128,2,1024]{2,1,0:T(2,128)}), f32[128,2,1024]{2,1,0:T(2,128)}, u32[]{:S(2)}, u32[]{:S(2)}) %all-to-all-start.2) | async-done | bytes 1048608 | tf_op jit(solution)/shard_map/all_to_all | solution.py:218
  478.9 1.9 reshape.285
  480.9 6.6 %scatter_custom_fusion.2 = f32[2048,1024]{1,0:T(8,128)} fusion(s32[256]{0:T(256)S(1)} %reshape.290, f32[]{:T(128)} %constant.69.clone.1, f32[256,1024]{1,0:T(8,128)S(1)} %reshape.285, pred[256]{0:T(512)(128)(4,1)S(1)} %gt.23), kind=kCustom, calls=%fused_computation.55 | custom fusion | flops 524288 | bytes 9438720 | tf_op jit(solution)/shard_map/scatter-add | solution.py:228
  487.5 7.4 %broadcast_multiply_fusion = f32[2048,1024]{1,0:T(8,128)} fusion(f32[2048,1024]{1,0:T(8,128)} %scatter_custom_fusion.2, f32[2048]{0:T(1024)S(1)} %copy-done.1), kind=kLoop, calls=%fused_computation.54 | loop fusion | flops 2097152 | bytes 16785408 | tf_op jit(solution)/shard_map/mul | solution.py:230
  (71 shorter events, 22.9 us)
Async XLA Ops:
  7.2 194.4 %copy-start = (bf16[1024,1024]{1,0:T(8,128)(2,1)S(1)}, bf16[1024,1024]{1,0:T(8,128)(2,1)}, u32[]{:S(2)}) copy-start(bf16[1024,1024]{1,0:T(8,128)(2,1)} %param.18) | copy-start | bytes 6291460
  43.6 24.3 %all-to-all-start.1 = ((f32[128,2,1024]{2,1,0:T(2,128)}), f32[128,2,1024]{2,1,0:T(2,128)}, u32[]{:S(2)}, u32[]{:S(2)}) async-start(f32[128,2,1024]{2,1,0:T(2,128)} %multiply_select_fusion), calls=%async_computation.1 | async-start | bytes 2097152 | tf_op jit(solution)/shard_map/all_to_all | solution.py:122
  49.2 85.7 %all-gather.5.cloned.1.call-start = ((), (), s32[]{:S(2)}) async-start(), calls=%async_computation.6 | async-start | bytes 4456448 | tf_op jit(solution)/shard_map/all_gather | solution.py:146
  73.8 9.6 %copy-start.8 = (s32[1,3]{1,0:T(1,128)S(1)}, s32[1,3]{1,0:T(1,128)}, u32[]{:S(2)}) copy-start(s32[1,3]{1,0:T(1,128)} %param.16) | copy-start | bytes 40
  80.2 1.0 copy-start.6
  82.0 110.8 %all-gather.3.cloned.1.call-start = ((), (), s32[]{:S(2)}) async-start(), calls=%async_computation.5 | async-start | bytes 4456448 | tf_op jit(solution)/shard_map/all_gather | solution.py:145
  82.8 249.0 %reduce-scatter.3.cloned.1.call-start = ((), (), s32[]{:S(2)}) async-start(), calls=%async_computation.7 | async-start | bytes 8912896 | tf_op jit(solution)/shard_map/reduce_scatter | solution.py:204
  201.3 4.4 copy-start.4
  206.2 2.2 copy-start.9
  213.8 2.0 copy-start.5
  228.0 4.4 copy-start.3
  232.4 204.8 %reduce-scatter.5.cloned.1.call-start = ((), (), s32[]{:S(2)}) async-start(), calls=%async_computation.8 | async-start | bytes 8912896 | tf_op jit(solution)/shard_map/reduce_scatter | solution.py:201
  240.5 196.7 %copy-start.2 = (f32[128,1024]{1,0:T(8,128)S(1)}, f32[128,1024]{1,0:T(8,128)}, u32[]{:S(2)}) copy-start(f32[128,1024]{1,0:T(8,128)} %gather_fusion.2) | copy-start | bytes 1572868
  437.2 8.4 %copy-start.7 = (bf16[128,1024]{1,0:T(8,128)(2,1)S(1)}, bf16[128,1024]{1,0:T(8,128)(2,1)}, u32[]{:S(2)}) copy-start(bf16[128,1024]{1,0:T(8,128)(2,1)} %param.19) | copy-start | bytes 786436
  451.2 27.7 %all-to-all-start.2 = ((f32[128,2,1024]{2,1,0:T(2,128)}), f32[128,2,1024]{2,1,0:T(2,128)}, u32[]{:S(2)}, u32[]{:S(2)}) async-start(f32[128,2,1024]{2,1,0:T(2,128)} %reshape.284), calls=%async_computation.4 | async-start | bytes 2097152 | tf_op jit(solution)/shard_map/all_to_all | solution.py:218
  480.8 6.7 %copy-start.1 = (f32[2048]{0:T(1024)S(1)}, f32[2048]{0:T(1024)}, u32[]{:S(2)}) copy-start(f32[2048]{0:T(1024)} %param.13) | copy-start | bytes 24580
Sparse Core Ops, SparseCore 0:
  82.1 52.7 all-gather.4
  137.9 54.9 all-gather.2
  232.5 99.2 reduce-scatter.2
  336.0 101.1 reduce-scatter.4
where the time goes:
time: 502 us; the launch traced here: 501 us
  waiting for transfers between devices  337 us (67%)
  matrix products  44.9 us (9%)
  local copies, waits for them, and re-layouts  38.4 us (8%)
  other arithmetic  29.3 us (6%)
  blocking collectives  20.8 us (4%)
  between operations  15.3 us (3%)
  starting transfers between devices  15.1 us (3%)
    reduce_scatter x1, waiting for transfers between devices, per_device(): lax.psum_scatter(grad_key_all.reshape(key_total, model_width), 'cp', scat...  105 us
    reduce_scatter x1, waiting for transfers between devices, per_device(): lax.psum_scatter(grad_value_all.reshape(key_total, model_width), 'cp', sc...  89.3 us
    all_gather x1, waiting for transfers between devices, per_device(): lax.all_gather(key_rows, 'cp', axis=0, tiled=True)  57.9 us
    all_gather x1, waiting for transfers between devices, per_device(): lax.all_gather(value_rows, 'cp', axis=0, tiled=True)  49.2 us
    all_to_all x1, blocking collectives, per_device(): lax.all_to_all(requests.reshape(devices, capacity), ('dp', 'cp'), split_a...  20.8 us
    all_to_all x1, waiting for transfers between devices, per_device(): lax.all_to_all(fetched.reshape(devices, capacity, model_width), ('dp', 'c...  18.6 us
    all_to_all x1, waiting for transfers between devices, per_device(): lax.all_to_all(outgoing.reshape(devices, capacity, model_width), ('dp', '...  16.3 us
  transfers between devices with their start and end apart: 6, of which 6 were waited for; matrix products, arithmetic and copies ran while one was open for 3% of the time, Pallas kernels for 0%

commit v1 on v0

v1 whole, which is shorter than its diff:
```python
import jax
import jax.numpy as jnp
from jax import lax
from jax.sharding import PartitionSpec as P

HEADS = 8
EPSILON = 1e-05


def normalize(values):
    center = jnp.mean(values, axis=-1, keepdims=True)
    shifted = values - center
    inv_spread = lax.rsqrt(jnp.mean(shifted * shifted, axis=-1, keepdims=True) + EPSILON)
    return (shifted * inv_spread, inv_spread)


def normalize_back(grad_in, normed, inv_spread):
    return inv_spread * (
        grad_in
        - jnp.mean(grad_in, axis=-1, keepdims=True)
        - normed * jnp.mean(grad_in * normed, axis=-1, keepdims=True)
    )


def split_scale(scale):
    high = lax.reduce_precision(scale, 8, 7)
    rest = scale - high
    middle = lax.reduce_precision(rest, 8, 7)
    return high, middle, rest - middle


def per_device(
    table_rows,
    row_scales,
    owners,
    shard_rows,
    history_lengths,
    input_weight,
    output_weight,
    cotangent,
):
    f32, bf16 = jnp.float32, jnp.bfloat16
    rows = owners.shape[0]
    table_size, width = table_rows.shape
    heads = HEADS
    hdim = width // heads
    devices = lax.axis_size(("dp", "cp"))
    n_cp = lax.axis_size("cp")
    cores = n_cp // heads
    capacity = 2
    slots = devices * capacity
    cycle = rows * n_cp
    half = cycle // 2
    quarter = heads // 2
    groups = [[heads_i * cores + c for heads_i in range(heads)] for c in range(cores)]
    swap = [(i, i ^ 1) for i in range(n_cp)]
    core = lax.axis_index("cp") % cores

    target = owners[:, 0]
    matches = target[:, None] == jnp.arange(devices, dtype=jnp.int32)[None, :]
    counts = matches.astype(jnp.int32)
    ranked = jnp.sum((jnp.cumsum(counts, axis=0) - counts) * counts, axis=1)
    placing = matches[:, :, None] & (ranked[:, None, None] == jnp.arange(capacity, dtype=jnp.int32))
    requests = jnp.sum(jnp.where(placing, shard_rows[:, None, None] + 1, 0), axis=0)
    incoming = lax.all_to_all(
        requests, ("dp", "cp"), split_axis=0, concat_axis=0, tiled=True
    ).reshape(slots)
    place = placing.reshape(rows, slots).astype(bf16)
    chosen = (
        (incoming - 1)[:, None] == jnp.arange(table_size, dtype=jnp.int32)[None, :]
    ).astype(bf16)

    pieces = jnp.stack(split_scale(row_scales), axis=1).astype(bf16)
    pieces = jnp.pad(pieces, ((0, 0), (0, 125)))
    fetched = jnp.concatenate(
        [
            jnp.dot(chosen, table_rows, preferred_element_type=f32).astype(bf16),
            jnp.dot(chosen, pieces, preferred_element_type=f32).astype(bf16),
        ],
        axis=1,
    )
    returned = lax.all_to_all(
        fetched.reshape(devices, capacity, width + 128),
        ("dp", "cp"),
        split_axis=0,
        concat_axis=0,
        tiled=True,
    ).reshape(slots, width + 128)
    gathered = jnp.dot(place, returned, preferred_element_type=f32)
    scale = gathered[:, width] + (gathered[:, width + 1] + gathered[:, width + 2])
    embedded = gathered[:, :width] * scale[:, None]

    def to_heads(values):
        return lax.all_to_all(
            values, "cp", split_axis=0, concat_axis=0, tiled=True, axis_index_groups=groups
        )

    lengths = history_lengths[0]
    ends = jnp.cumsum(lengths)
    begins = ends - lengths
    longest = jnp.sum(jnp.where(lengths == jnp.max(lengths), begins, 0))
    residue = jnp.arange(half, dtype=jnp.int32)
    upper = (residue >= longest) ^ (core == 1)
    position = jnp.where(upper, residue, residue + half)
    inside = (position[:, None] >= begins[None, :]) & (position[:, None] < ends[None, :])
    first = jnp.sum(jnp.where(inside, begins[None, :], 0), axis=1)
    length = jnp.sum(jnp.where(inside, lengths[None, :], 0), axis=1).astype(f32)
    own = (
        jnp.arange(quarter, dtype=jnp.int32)[:, None] * (2 * rows)
        + core * rows
        + jnp.arange(rows, dtype=jnp.int32)[None, :]
    )
    own_upper = ((own >= longest) ^ (core == 1))[:, :, None]

    def split_histories(values):
        keep = jnp.where(own_upper, values[:quarter], values[quarter:])
        send = jnp.where(own_upper, values[quarter:], values[:quarter])
        received = lax.ppermute(send, "cp", swap)
        pair = jnp.where(
            core == 0, jnp.stack([keep, received], 1), jnp.stack([received, keep], 1)
        )
        return pair.reshape(half, values.shape[-1])

    def join_histories(values):
        pair = values.reshape(quarter, 2, rows, values.shape[-1])
        keep = jnp.where(core == 0, pair[:, 0], pair[:, 1])
        send = jnp.where(core == 0, pair[:, 1], pair[:, 0])
        received = lax.ppermute(send, "cp", swap)
        return jnp.concatenate(
            [jnp.where(own_upper, keep, received), jnp.where(own_upper, received, keep)], axis=0
        )

    grad_mixed = jnp.einsum("rk,dk->rd", cotangent, output_weight, preferred_element_type=f32)
    grad_mixed_heads = split_histories(
        to_heads(grad_mixed.astype(bf16).reshape(rows, heads, hdim).transpose(1, 0, 2))
    )

    normed, inv_embed = normalize(embedded)
    projected = jnp.dot(normed.astype(bf16), input_weight, preferred_element_type=f32)
    activated = (projected * jax.nn.sigmoid(projected)).astype(bf16)
    branches = to_heads(
        activated.reshape(rows, 4, heads, hdim).transpose(2, 0, 1, 3).reshape(heads, rows, 4 * hdim)
    )
    branches = split_histories(branches)
    gate, value, query, key = [branches[:, i * hdim : (i + 1) * hdim] for i in range(4)]

    scaling = hdim ** (-0.5)
    scores = jnp.einsum("qe,ke->qk", query, key, preferred_element_type=f32) * scaling
    allowed = (position[None, :] >= first[:, None]) & (position[None, :] <= position[:, None])
    sig = jax.nn.sigmoid(scores)
    weights = jnp.where(allowed, scores * sig / length[:, None], 0.0).astype(bf16)
    slope = jnp.where(
        allowed, sig * (1.0 + scores * (1.0 - sig)) / length[:, None] * scaling, 0.0
    )
    attention = jnp.dot(weights, value, preferred_element_type=f32)

    gated = grad_mixed_heads.astype(f32) * gate.astype(f32)
    center = jnp.mean(attention, axis=1)
    shifted = attention - center[:, None]
    stats = jnp.stack(
        [
            center,
            jnp.sum(shifted * shifted, axis=1),
            jnp.sum(gated, axis=1),
            jnp.sum(gated * shifted, axis=1),
        ]
    )
    stats = to_heads(jnp.broadcast_to(stats[None], (heads,) + stats.shape))
    mean = jnp.mean(stats[:, 0], axis=0)
    offset = stats[:, 0] - mean[None]
    variance = jnp.sum(stats[:, 1] + hdim * offset * offset, axis=0) / width
    inv_attn = lax.rsqrt(variance + EPSILON)
    mean_grad = jnp.sum(stats[:, 2], axis=0) / width
    mean_prod = inv_attn * jnp.sum(stats[:, 3] + offset * stats[:, 2], axis=0) / width
    attn_norm = (attention - mean[:, None]) * inv_attn[:, None]
    grad_attn = (
        inv_attn[:, None] * (gated - mean_grad[:, None] - attn_norm * mean_prod[:, None])
    ).astype(bf16)

    grad_weights = jnp.einsum("qe,ke->qk", grad_attn, value, preferred_element_type=f32)
    grad_scores = (grad_weights * slope).astype(bf16)
    grad_query = jnp.dot(grad_scores, key, preferred_element_type=f32)
    grad_key = jnp.einsum("qk,qe->ke", grad_scores, query, preferred_element_type=f32)
    grad_value = jnp.einsum("qk,qe->ke", weights, grad_attn, preferred_element_type=f32)

    back = jnp.concatenate([attn_norm, grad_value, grad_query, grad_key], axis=1).astype(bf16)
    back = to_heads(join_histories(back))
    back = back.reshape(heads, rows, 4, hdim).transpose(1, 2, 0, 3).reshape(rows, 4, width)
    attn_norm_rows = back[:, 0].astype(f32)
    mixed = attn_norm_rows * activated[:, :width].astype(f32)
    layer_out = (
        embedded + jnp.dot(mixed.astype(bf16), output_weight, preferred_element_type=f32)
    ).astype(bf16)
    grad_act = jnp.concatenate(
        [grad_mixed * attn_norm_rows, back[:, 1:].reshape(rows, 3 * width).astype(f32)], axis=1
    )
    sig = jax.nn.sigmoid(projected)
    grad_proj = (grad_act * sig * (1.0 + projected * (1.0 - sig))).astype(bf16)
    grad_norm = jnp.einsum("rk,dk->rd", grad_proj, input_weight, preferred_element_type=f32)
    grad_embed = cotangent.astype(f32) + normalize_back(grad_norm, normed, inv_embed)

    outgoing = jnp.einsum(
        "rs,rd->sd", place, grad_embed.astype(bf16), preferred_element_type=f32
    ).astype(bf16)
    arrived = lax.all_to_all(
        outgoing.reshape(devices, capacity, width),
        ("dp", "cp"),
        split_axis=0,
        concat_axis=0,
        tiled=True,
    ).reshape(slots, width)
    table_grad = (
        jnp.einsum("sr,sd->rd", chosen, arrived, preferred_element_type=f32) * row_scales[:, None]
    )
    return (layer_out, table_grad)


def solution(mesh):
    return jax.shard_map(
        per_device,
        mesh=mesh,
        in_specs=(
            P(("dp", "cp"), None),
            P(("dp", "cp")),
            P(("dp", "cp"), None),
            P(("dp", "cp")),
            P("dp", None),
            P(),
            P(),
            P(("dp", "cp"), None),
        ),
        out_specs=(P(("dp", "cp"), None), P(("dp", "cp"), None)),
        check_vma=False,
    )
```

time: 502 us -> 211 us (0.42)
  waiting for transfers between devices: 337 us -> 66.2 us
  starting transfers between devices: 15.1 us -> 39.4 us
  between operations: 15.3 us -> 1.07 us
  local copies, waits for them, and re-layouts: 38.4 us -> 26.9 us
  blocking collectives: 20.8 us -> 9.35 us
  matrix products: 44.9 us -> 37.2 us
    reduce_scatter x2 -> x0, waiting for transfers between devices: 195 us -> none  [the longest x1 105 us: per_device(): lax.psum_scatter(grad_key_all.reshape(key_total, model_width), 'cp', scat...]
    all_gather x2 -> x0, waiting for transfers between devices: 107 us -> none  [the longest x1 57.9 us: per_device(): lax.all_gather(key_rows, 'cp', axis=0, tiled=True)]
    all_to_all x2 -> x6, waiting for transfers between devices: 34.9 us -> 64.6 us  [the longest x3 31.6 us: to_heads(): lax.all_to_all(values, 'cp', split_axis=0, concat_axis=0, tiled=True, axi...]
    all_to_all x2 -> x6, starting transfers between devices: 14.7 us -> 33.7 us  [the longest x3 12.5 us: to_heads(): lax.all_to_all(values, 'cp', split_axis=0, concat_axis=0, tiled=True, axi...]
    reshape x6 -> x5, local copies, waits for them, and re-layouts: 21 us -> 7.3 us  [the longest x1 2.75 us: per_device(): activated.reshape(rows, 4, heads, hdim).transpose(2, 0, 1, 3)]
    all_to_all x1, blocking collectives: 20.8 us -> 9.35 us  [to_heads(): lax.all_to_all(values, 'cp', split_axis=0, concat_axis=0, tiled=True, axi...]
    gather x3 -> x0, local copies, waits for them, and re-layouts: 8.59 us -> none  [the longest x1 5.08 us: per_device(): table_rows[lookup].astype(jnp.float32) * row_scales[lookup][:, None]]
    mul x2 -> x1, other arithmetic: 9.39 us -> 1.81 us  [per_device(): grad_mixed * attn_norm_rows]
  transfers between devices with their start and end apart: 6 -> 9, of which waited for: 6 -> 7; matrix products, arithmetic and copies ran while one was open for 3% -> 7% of each run, Pallas kernels for 0% -> 0%
where the time goes in v1:
time: 211 us; the launch traced here: 210 us
  waiting for transfers between devices  66.2 us (31%)
  starting transfers between devices  39.4 us (19%)
  matrix products  37.2 us (18%)
  other arithmetic  29.8 us (14%)
  local copies, waits for them, and re-layouts  26.9 us (13%)
  blocking collectives  9.35 us (4%)
    all_to_all x3, waiting for transfers between devices, to_heads(): lax.all_to_all(values, 'cp', split_axis=0, concat_axis=0, tiled=True, axi...  31.6 us
    all_to_all x1, waiting for transfers between devices, per_device(): lax.all_to_all(fetched.reshape(devices, capacity, width + 128), ('dp', 'c...  13 us
    all_to_all x3, starting transfers between devices, to_heads(): lax.all_to_all(values, 'cp', split_axis=0, concat_axis=0, tiled=True, axi...  12.5 us
    all_to_all x1, starting transfers between devices, per_device(): lax.all_to_all(requests, ('dp', 'cp'), split_axis=0, concat_axis=0, tiled...  11.5 us
    all_to_all x1, waiting for transfers between devices, per_device(): lax.all_to_all(outgoing.reshape(devices, capacity, width), ('dp', 'cp'),...  11.4 us
    all_to_all x1, blocking collectives, to_heads(): lax.all_to_all(values, 'cp', split_axis=0, concat_axis=0, tiled=True, axi...  9.35 us
    all_to_all x1, waiting for transfers between devices, per_device(): lax.all_to_all(requests, ('dp', 'cp'), split_axis=0, concat_axis=0, tiled...  8.66 us
    dot_general x1, matrix products, per_device(): jnp.einsum('rk,dk->rd', grad_proj, input_weight, preferred_element_type=f32)  7.49 us
  transfers between devices with their start and end apart: 9, of which 7 were waited for; matrix products, arithmetic and copies ran while one was open for 7% of the time, Pallas kernels for 0%

profile of v1, /device:TPU:1, one launch (start us, length us, event | category | flops | bytes accessed | tf_op | source)
XLA Modules:
  0.0 209.9 jit_solution(4274937481610784518)
XLA Ops:
  3.3 2.9 %select_reduce_fusion = (s32[128,2]{1,0:T(8,128)}, pred[128,128,2]{0,2,1:T(4,128)(4,1)S(1)}) fusion(s32[128]{0:T(128)S(1)} %broadcast_add_fusion, pred[128,2]{0,1:T(4,128)(4,1)S(1)} %iota_compare_fusion.11, pred[128,128]{0,1:T(8,128)(4,1)S(1)} %copy.68), kind=kLoop, calls=%fused_computation.87 | loop fusion | flops 98048 | bytes 50944 | tf_op jit(solution)/shard_map/reduce_sum | solution.py:64
  6.2 11.5 %all-to-all-start = ((s32[128,1,2]{2,1,0:T(1,128)}), s32[128,1,2]{2,1,0:T(1,128)S(1)}, u32[]{:S(2)}, u32[]{:S(2)}) async-start(s32[128,1,2]{2,1,0:T(1,128)} %bitcast.1), calls=%async_computation | async-start | bytes 131072 | tf_op jit(solution)/shard_map/all_to_all | solution.py:65
  18.5 8.7 %all-to-all-done = s32[128,1,2]{2,1,0:T(1,128)S(1)} async-done(((s32[128,1,2]{2,1,0:T(1,128)}), s32[128,1,2]{2,1,0:T(1,128)S(1)}, u32[]{:S(2)}, u32[]{:S(2)}) %all-to-all-start) | async-done | bytes 1056 | tf_op jit(solution)/shard_map/all_to_all | solution.py:65
  27.4 3.5 %fusion.4 = bf16[256,1024]{1,0:T(8,128)(2,1)S(1)} fusion(bf16[2048,1024]{1,0:T(8,128)(2,1)} %param.8, s32[256]{0:T(256)S(1)} %sub.83), kind=kOutput, calls=%fused_computation.14 | convolution fusion | flops 1074528256 | bytes 4719616 | tf_op jit(solution)/shard_map/dot_general | solution.py:77
  32.5 4.5 %all-to-all-start.1 = ((bf16[128,2,1152]{2,1,0:T(2,128)(2,1)}), bf16[128,2,1152]{2,1,0:T(2,128)(2,1)S(1)}, u32[]{:S(2)}, u32[]{:S(2)}) async-start(bf16[128,2,1152]{2,1,0:T(2,128)(2,1)} %reshape.236), calls=%async_computation.1 | async-start | bytes 1179648 | tf_op jit(solution)/shard_map/all_to_all | solution.py:82
  38.4 13.0 %all-to-all-done.1 = bf16[128,2,1152]{2,1,0:T(2,128)(2,1)S(1)} async-done(((bf16[128,2,1152]{2,1,0:T(2,128)(2,1)}), bf16[128,2,1152]{2,1,0:T(2,128)(2,1)S(1)}, u32[]{:S(2)}, u32[]{:S(2)}) %all-to-all-start.1) | async-done | bytes 589856 | tf_op jit(solution)/shard_map/all_to_all | solution.py:82
  52.4 6.1 %multiply_convert_fusion.1 = (bf16[128,4096]{1,0:T(8,128)(2,1)S(1)}, f32[128,4096]{1,0:T(8,128)}) fusion(bf16[1024,4096]{1,0:T(8,128)(2,1)} %param.13, f32[128]{0:T(128)S(1)} %add_rsqrt_fusion.1, f32[128]{0:T(128)S(1)} %broadcast_multiply_fusion.5, f32[128]{0:T(128)S(1)} %fusion.51, f32[128,1152]{1,0:T(8,128)S(1)} %convolution_bitcast_fusion), kind=kOutput, calls=%fused_computation.9 | convolution fusion | flops 1076887552 | bytes 12060160 | tf_op jit(solution)/shard_map/dot_general | solution.py:139
  60.7 2.8 %copy.72 = bf16[128,4,8,128]{0,3,1,2:T(8,128)(2,1)} copy(bf16[128,4,8,128]{3,2,1,0:T(8,128)(2,1)} %bitcast.109) | data formatting | bytes 2097152 | tf_op jit(solution)/shard_map/reshape | solution.py:142
  63.4 4.2 %all-to-all-start.2 = ((bf16[8,128,512]{1,2,0:T(8,128)(2,1)}), bf16[8,128,512]{1,2,0:T(8,128)(2,1)}, u32[]{:S(2)}, u32[]{:S(2)}) async-start(bf16[8,128,512]{1,2,0:T(8,128)(2,1)} %bitcast.108), calls=%async_computation.2 | async-start | bytes 2097152 | tf_op jit(solution)/shard_map/all_to_all | solution.py:94
  71.4 12.0 %all-to-all-done.2 = bf16[8,128,512]{1,2,0:T(8,128)(2,1)} async-done(((bf16[8,128,512]{1,2,0:T(8,128)(2,1)}), bf16[8,128,512]{1,2,0:T(8,128)(2,1)}, u32[]{:S(2)}, u32[]{:S(2)}) %all-to-all-start.2) | async-done | bytes 1048608 | tf_op jit(solution)/shard_map/all_to_all | solution.py:94
  83.3 3.8 %all-to-all-start.3 = ((bf16[8,128,128]{2,1,0:T(8,128)(2,1)}), bf16[8,128,128]{2,1,0:T(8,128)(2,1)S(1)}, u32[]{:S(2)}, u32[]{:S(2)}) async-start(bf16[8,128,128]{2,1,0:T(8,128)(2,1)} %bitcast_bitcast_fusion), calls=%async_computation.3 | async-start | bytes 524288 | tf_op jit(solution)/shard_map/all_to_all | solution.py:94
  87.2 2.3 %select_bitcast_fusion.1 = (bf16[4,1,128,512]{2,3,0,1:T(8,128)(2,1)}, bf16[4,128,512]{1,2,0:T(8,128)(2,1)}) fusion(pred[4,128]{1,0:T(4,128)(4,1)S(1)} %fusion.61, bf16[8,128,512]{1,2,0:T(8,128)(2,1)} %all-to-all-done.2), kind=kLoop, calls=%fused_computation.57 | loop fusion | flops 524288 | bytes 2097664 | tf_op jit(solution)/shard_map/stack | solution.py:120
  90.9 3.5 %all-to-all-done.3 = bf16[8,128,128]{2,1,0:T(8,128)(2,1)S(1)} async-done(((bf16[8,128,128]{2,1,0:T(8,128)(2,1)}), bf16[8,128,128]{2,1,0:T(8,128)(2,1)S(1)}, u32[]{:S(2)}, u32[]{:S(2)}) %all-to-all-start.3) | async-done | bytes 262176 | tf_op jit(solution)/shard_map/all_to_all | solution.py:94
  95.3 2.6 %collective-permute-start.1 = (bf16[4,128,128]{2,1,0:T(8,128)(2,1)}, bf16[4,128,128]{2,1,0:T(8,128)(2,1)S(1)}, u32[]{:S(2)}, u32[]{:S(2)}) collective-permute-start(bf16[4,128,128]{2,1,0:T(8,128)(2,1)} %get-tuple-element.22), channel_id=1, source_target_pairs={{0,1},{1,0},{2,3},{3,2},{4,5},{5,4},{6,7},{7,6},{8,9},{9,8},{10,11... | collective-permute-start | bytes 393224 | tf_op jit(solution)/shard_map/ppermute | solution.py:118
  102.3 2.7 %maximum_select_fusion = bf16[4,2,128,512]{2,3,0,1:T(8,128)(2,1)} fusion(bf16[4,1,128,512]{2,3,0,1:T(8,128)(2,1)} %bitcast.11, bf16[4,1,128,512]{2,3,0,1:T(8,128)(2,1)} %get-tuple-element.17, pred[]{:T(512)S(6)} %eq.78), kind=kLoop, calls=%fused_computation.27 | loop fusion | flops 1572864 | bytes 2097153 | tf_op jit(solution)/shard_map/jit(_where)/select_n | solution.py:119
  105.0 2.3 %copy.73 = bf16[4,2,128,512]{3,2,1,0:T(8,128)(2,1)} copy(bf16[4,2,128,512]{2,3,0,1:T(8,128)(2,1)} %maximum_select_fusion) | data formatting | bytes 2097152 | tf_op jit(solution)/shard_map/jit(_where)/select_n | solution.py:119
  107.3 3.1 %select_convert_fusion = (bf16[1024,1024]{1,0:T(8,128)(2,1)S(1)}, f32[1024,1024]{1,0:T(8,128)S(1)}) fusion(f32[1024]{0:T(1024)} %convert_element_type.88, s32[1024]{0:T(1024)S(1)} %add_select_fusion, s32[1024]{0:T(1024)} %get-tuple-element.11, bf16[1024,512]{1,0:T(8,128)(2,1)} %bitcast.110), kind=kOutput, calls=%fused_computation.2 | convolution fusion | flops 279969792 | bytes 6832128 | tf_op jit(solution)/shard_map/qe,ke->qk/dot_general | solution.py:148
  111.9 9.3 %all_to_all.39 = f32[8,4,1024]{2,1,0:T(4,128)S(1)} all-to-all(f32[8,4,1024]{2,1,0:T(4,128)S(1)} %broadcast_in_dim.113), channel_id=1, replica_groups={{0,2,4,6,8,10,12,14},{1,3,5,7,9,11,13,15},{16,18,20,22,24,26,28,30},{17..., dimensions={0} | all-to-all | bytes 262144 | tf_op jit(solution)/shard_map/all_to_all | solution.py:94
  123.8 3.3 %multiply_convert_fusion = bf16[1024,1024]{1,0:T(8,128)(2,1)S(1)} fusion(f32[1024,1024]{1,0:T(8,128)S(1)} %get-tuple-element.39, bf16[1024,128]{1,0:T(8,128)(2,1)S(1)} %get-tuple-element.20, f32[1024]{0:T(1024)S(1)} %copy-done.11, s32[1024]{0:T(1024)S(1)} %add_select_fusion, s32[1024]{0:T(1024)S(1)} %copy-done.10, bf16[1024,512]{1,0:T(8,128)(2,1)S(1)} %bitcast.114), kind=kOutput, calls=%fused_computation.1 | convolution fusion | flops 285212672 | bytes 6832128 | tf_op jit(solution)/shard_map/qe,ke->qk/dot_general | solution.py:180
  141.3 4.5 %all-to-all-start.5 = ((bf16[8,128,512]{1,2,0:T(8,128)(2,1)}), bf16[8,128,512]{1,2,0:T(8,128)(2,1)}, u32[]{:S(2)}, u32[]{:S(2)}) async-start(bf16[8,128,512]{1,2,0:T(8,128)(2,1)} %pad_maximum_fusion.1), calls=%async_computation.5 | async-start | bytes 2097152 | tf_op jit(solution)/shard_map/all_to_all | solution.py:94
  145.8 16.1 %all-to-all-done.5 = bf16[8,128,512]{1,2,0:T(8,128)(2,1)} async-done(((bf16[8,128,512]{1,2,0:T(8,128)(2,1)}), bf16[8,128,512]{1,2,0:T(8,128)(2,1)}, u32[]{:S(2)}, u32[]{:S(2)}) %all-to-all-start.5) | async-done | bytes 1048608 | tf_op jit(solution)/shard_map/all_to_all | solution.py:94
  161.9 2.4 %copy.82 = bf16[128,4,8,128]{3,2,0,1:T(8,128)(2,1)} copy(bf16[128,4,8,128]{0,3,1,2:T(8,128)(2,1)} %bitcast.31) | data formatting | bytes 2097152 | tf_op jit(solution)/shard_map/transpose | solution.py:188
  164.3 2.3 %reshape.244 = bf16[128,4,1024]{2,0,1:T(8,128)(2,1)} reshape(bf16[128,4,8,128]{3,2,0,1:T(8,128)(2,1)} %copy.82) | data formatting | bytes 2097152 | tf_op jit(solution)/shard_map/reshape | solution.py:188
  166.6 2.5 %slice_convert_fusion = f32[128,3,1024]{2,0,1:T(8,128)} fusion(bf16[128,4,1024]{2,0,1:T(8,128)(2,1)} %reshape.244), kind=kLoop, calls=%fused_computation.34 | loop fusion | flops 393216 | bytes 2359296 | tf_op jit(solution)/shard_map/convert_element_type | solution.py:195
  169.1 1.8 convert_multiply_fusion
  170.9 3.0 %copy.83 = f32[128,3,1024]{0,2,1:T(8,128)} copy(f32[128,3,1024]{2,0,1:T(8,128)} %slice_convert_fusion) | data formatting | bytes 3145728 | tf_op jit(solution)/shard_map/convert_element_type | solution.py:195
  173.9 3.1 %copy.84 = f32[128,3072]{1,0:T(8,128)} copy(f32[128,3072]{0,1:T(8,128)} %bitcast.107) | data formatting | bytes 3145728 | tf_op jit(solution)/shard_map/convert_element_type | solution.py:195
  177.0 7.5 %fusion.70 = (f32[128]{0:T(128)S(1)}, f32[128]{0:T(128)S(1)}, f32[128,1024]{1,0:T(8,128)S(1)}) fusion(f32[128]{0:T(128)S(1)} %copy-done.15, f32[128]{0:T(128)S(1)} %copy-done.13, f32[128]{0:T(128)S(1)} %fusion.51, f32[128,1152]{1,0:T(8,128)S(1)} %convolution_bitcast_fusion, bf16[1024,4096]{1,0:T(8,128)(2,1)} %param.13, f32[128,3072]{1,0:T(8,128)} %copy.84, ...), kind=kOutput, calls=%fused_computation.146 | convolution fusion | flops 1079770880 | bytes 13634048 | tf_op jit(solution)/shard_map/rk,dk->rd/dot_general | solution.py:199
  186.0 5.2 %all-to-all-start.6 = ((bf16[128,2,1024]{2,1,0:T(2,128)(2,1)}), bf16[128,2,1024]{2,1,0:T(2,128)(2,1)S(1)}, u32[]{:S(2)}, u32[]{:S(2)}) async-start(bf16[128,2,1024]{2,1,0:T(2,128)(2,1)} %reshape.245), calls=%async_computation.6 | async-start | bytes 1048576 | tf_op jit(solution)/shard_map/all_to_all | solution.py:205
  191.2 2.2 %fusion.5 = bf16[128,1024]{1,0:T(8,128)(2,1)} fusion(bf16[1024,1024]{1,0:T(8,128)(2,1)S(1)} %copy-done, bf16[128,4096]{1,0:T(8,128)(2,1)} %copy-done.2, bf16[128,4,1024]{2,0,1:T(8,128)(2,1)} %reshape.244, f32[128]{0:T(128)S(1)} %fusion.51, f32[128,1152]{1,0:T(8,128)S(1)} %convolution_bitcast_fusion), kind=kOutput, calls=%fused_computation.20 | convolution fusion | flops 269352960 | bytes 3408384 | tf_op jit(solution)/shard_map/dot_general | solution.py:192
  193.4 11.4 %all-to-all-done.6 = bf16[128,2,1024]{2,1,0:T(2,128)(2,1)S(1)} async-done(((bf16[128,2,1024]{2,1,0:T(2,128)(2,1)}), bf16[128,2,1024]{2,1,0:T(2,128)(2,1)S(1)}, u32[]{:S(2)}, u32[]{:S(2)}) %all-to-all-start.6) | async-done | bytes 524320 | tf_op jit(solution)/shard_map/all_to_all | solution.py:205
  205.0 4.9 %convolution_multiply_fusion = f32[2048,1024]{1,0:T(8,128)} fusion(bf16[256,1024]{1,0:T(8,128)(2,1)S(1)} %reshape.246, f32[2048]{0:T(1024)S(1)} %copy-done.7, s32[256]{0:T(256)S(1)} %sub.83), kind=kOutput, calls=%fused_computation | convolution fusion | flops 1076363264 | bytes 8922112 | tf_op jit(solution)/shard_map/sr,sd->rd/dot_general | solution.py:213
  (98 shorter events, 40.0 us)
Async XLA Ops:
  0.6 69.2 %copy-start = (bf16[1024,1024]{1,0:T(8,128)(2,1)S(1)}, bf16[1024,1024]{1,0:T(8,128)(2,1)}, u32[]{:S(2)}) copy-start(bf16[1024,1024]{1,0:T(8,128)(2,1)} %param.14) | copy-start | bytes 6291460
  6.2 20.9 %all-to-all-start = ((s32[128,1,2]{2,1,0:T(1,128)}), s32[128,1,2]{2,1,0:T(1,128)S(1)}, u32[]{:S(2)}, u32[]{:S(2)}) async-start(s32[128,1,2]{2,1,0:T(1,128)} %bitcast.1), calls=%async_computation | async-start | bytes 131072 | tf_op jit(solution)/shard_map/all_to_all | solution.py:65
  31.4 5.6 %copy-start.8 = (s32[1,3]{1,0:T(1,128)S(1)}, s32[1,3]{1,0:T(1,128)}, u32[]{:S(2)}) copy-start(s32[1,3]{1,0:T(1,128)} %param.12) | copy-start | bytes 40
  32.5 18.9 %all-to-all-start.1 = ((bf16[128,2,1152]{2,1,0:T(2,128)(2,1)}), bf16[128,2,1152]{2,1,0:T(2,128)(2,1)S(1)}, u32[]{:S(2)}, u32[]{:S(2)}) async-start(bf16[128,2,1152]{2,1,0:T(2,128)(2,1)} %reshape.236), calls=%async_computation.1 | async-start | bytes 1179648 | tf_op jit(solution)/shard_map/all_to_all | solution.py:82
  37.3 30.4 %copy-start.9 = (s32[3,1]{0,1:T(1,128)}, s32[3,1]{0,1:T(1,128)S(1)}, u32[]{:S(2)}) copy-start(s32[3,1]{0,1:T(1,128)S(1)} %reduce-window.4) | copy-start | bytes 40
  52.1 6.3 %copy-start.12 = (f32[128]{0:T(128)}, f32[128]{0:T(128)S(1)}, u32[]{:S(2)}) copy-start(f32[128]{0:T(128)S(1)} %broadcast_multiply_fusion.5) | copy-start | bytes 1540
  52.4 6.1 %copy-start.14 = (f32[128]{0:T(128)}, f32[128]{0:T(128)S(1)}, u32[]{:S(2)}) copy-start(f32[128]{0:T(128)S(1)} %add_rsqrt_fusion.1) | copy-start | bytes 1540
  58.5 1.0 copy-start.2
  60.7 9.1 %copy-start.3 = (bf16[128,1024]{1,0:T(8,128)(2,1)S(1)}, bf16[128,1024]{1,0:T(8,128)(2,1)}, u32[]{:S(2)}) copy-start(bf16[128,1024]{1,0:T(8,128)(2,1)} %param.15) | copy-start | bytes 786436
  63.4 19.9 %all-to-all-start.2 = ((bf16[8,128,512]{1,2,0:T(8,128)(2,1)}), bf16[8,128,512]{1,2,0:T(8,128)(2,1)}, u32[]{:S(2)}, u32[]{:S(2)}) async-start(bf16[8,128,512]{1,2,0:T(8,128)(2,1)} %bitcast.108), calls=%async_computation.2 | async-start | bytes 2097152 | tf_op jit(solution)/shard_map/all_to_all | solution.py:94
  83.3 11.1 %all-to-all-start.3 = ((bf16[8,128,128]{2,1,0:T(8,128)(2,1)}), bf16[8,128,128]{2,1,0:T(8,128)(2,1)S(1)}, u32[]{:S(2)}, u32[]{:S(2)}) async-start(bf16[8,128,128]{2,1,0:T(8,128)(2,1)} %bitcast_bitcast_fusion), calls=%async_computation.3 | async-start | bytes 524288 | tf_op jit(solution)/shard_map/all_to_all | solution.py:94
  89.5 12.8 %collective-permute-start = (bf16[4,128,512]{1,2,0:T(8,128)(2,1)}, bf16[4,128,512]{1,2,0:T(8,128)(2,1)}, u32[]{:S(2)}, u32[]{:S(2)}) collective-permute-start(bf16[4,128,512]{1,2,0:T(8,128)(2,1)} %get-tuple-element.18), channel_id=1, source_target_pairs={{0,1},{1,0},{2,3},{3,2},{4,5},{5,4},{6,7},{7,6},{8,9},{9,8},{10,11... | collective-permute-start | bytes 1572872 | tf_op jit(solution)/shard_map/ppermute | solution.py:118
  95.3 5.2 %collective-permute-start.1 = (bf16[4,128,128]{2,1,0:T(8,128)(2,1)}, bf16[4,128,128]{2,1,0:T(8,128)(2,1)S(1)}, u32[]{:S(2)}, u32[]{:S(2)}) collective-permute-start(bf16[4,128,128]{2,1,0:T(8,128)(2,1)} %get-tuple-element.22), channel_id=1, source_target_pairs={{0,1},{1,0},{2,3},{3,2},{4,5},{5,4},{6,7},{7,6},{8,9},{9,8},{10,11... | collective-permute-start | bytes 393224 | tf_op jit(solution)/shard_map/ppermute | solution.py:118
  100.5 0.6 copy-start.6
  107.3 3.1 %copy-start.1 = (bf16[4,2,128,512]{3,2,1,0:T(8,128)(2,1)S(1)}, bf16[4,2,128,512]{3,2,1,0:T(8,128)(2,1)}, u32[]{:S(2)}) copy-start(bf16[4,2,128,512]{3,2,1,0:T(8,128)(2,1)} %copy.73) | copy-start | bytes 3145732
  123.0 0.8 copy-start.10
  123.0 0.8 copy-start.11
  136.8 3.2 %collective-permute-start.2 = (bf16[4,128,512]{1,2,0:T(8,128)(2,1)S(1)}, bf16[4,128,512]{1,2,0:T(8,128)(2,1)S(1)}, u32[]{:S(2)}, u32[]{:S(2)}) collective-permute-start(bf16[4,128,512]{1,2,0:T(8,128)(2,1)S(1)} %select_bitcast_fusion), channel_id=1, source_target_pairs={{0,1},{1,0},{2,3},{3,2},{4,5},{5,4},{6,7},{7,6},{8,9},{9,8},{10,11... | collective-permute-start | bytes 1572872 | tf_op jit(solution)/shard_map/ppermute | solution.py:128
  141.3 20.6 %all-to-all-start.5 = ((bf16[8,128,512]{1,2,0:T(8,128)(2,1)}), bf16[8,128,512]{1,2,0:T(8,128)(2,1)}, u32[]{:S(2)}, u32[]{:S(2)}) async-start(bf16[8,128,512]{1,2,0:T(8,128)(2,1)} %pad_maximum_fusion.1), calls=%async_computation.5 | async-start | bytes 2097152 | tf_op jit(solution)/shard_map/all_to_all | solution.py:94
  173.9 3.1 %copy-start.5 = (f32[128,1024]{1,0:T(8,128)S(1)}, f32[128,1024]{1,0:T(8,128)}, u32[]{:S(2)}) copy-start(f32[128,1024]{1,0:T(8,128)} %convert_multiply_fusion) | copy-start | bytes 1572868
  173.9 3.1 %copy-start.13 = (f32[128]{0:T(128)S(1)}, f32[128]{0:T(128)}, u32[]{:S(2)}) copy-start(f32[128]{0:T(128)} %copy-done.12) | copy-start | bytes 1540
  173.9 3.1 %copy-start.15 = (f32[128]{0:T(128)S(1)}, f32[128]{0:T(128)}, u32[]{:S(2)}) copy-start(f32[128]{0:T(128)} %copy-done.14) | copy-start | bytes 1540
  177.0 7.5 %copy-start.4 = (bf16[128,1024]{1,0:T(8,128)(2,1)S(1)}, bf16[128,1024]{1,0:T(8,128)(2,1)}, u32[]{:S(2)}) copy-start(bf16[128,1024]{1,0:T(8,128)(2,1)} %param.15) | copy-start | bytes 786436
  186.0 18.7 %all-to-all-start.6 = ((bf16[128,2,1024]{2,1,0:T(2,128)(2,1)}), bf16[128,2,1024]{2,1,0:T(2,128)(2,1)S(1)}, u32[]{:S(2)}, u32[]{:S(2)}) async-start(bf16[128,2,1024]{2,1,0:T(2,128)(2,1)} %reshape.245), calls=%async_computation.6 | async-start | bytes 1048576 | tf_op jit(solution)/shard_map/all_to_all | solution.py:205
  191.2 13.8 %copy-start.7 = (f32[2048]{0:T(1024)S(1)}, f32[2048]{0:T(1024)}, u32[]{:S(2)}) copy-start(f32[2048]{0:T(1024)} %param.9) | copy-start | bytes 24580

commit v2 on v1

v2 whole, which is shorter than its diff:
```python
import jax
import jax.numpy as jnp
from jax import lax
from jax.experimental import pallas as pl
from jax.experimental.pallas import tpu as pltpu
from jax.sharding import PartitionSpec as P

HEADS = 8
EPSILON = 1e-05
CAPACITY = 2
TILE = 256
F32, BF16, I32 = jnp.float32, jnp.bfloat16, jnp.int32


def nt_dot(left, right):
    return lax.dot_general(left, right, (((1,), (1,)), ((), ())), preferred_element_type=F32)


def tn_dot(left, right):
    return lax.dot_general(left, right, (((0,), (0,)), ((), ())), preferred_element_type=F32)


def nn_dot(left, right):
    return jnp.dot(left, right, preferred_element_type=F32)


def iota(shape, axis):
    return lax.broadcasted_iota(I32, shape, axis)


def normalize(values):
    center = jnp.mean(values, axis=-1, keepdims=True)
    shifted = values - center
    inv_spread = lax.rsqrt(jnp.mean(shifted * shifted, axis=-1, keepdims=True) + EPSILON)
    return (shifted * inv_spread, inv_spread)


def normalize_back(grad_in, normed, inv_spread):
    return inv_spread * (
        grad_in
        - jnp.mean(grad_in, axis=-1, keepdims=True)
        - normed * jnp.mean(grad_in * normed, axis=-1, keepdims=True)
    )


def full(shape):
    return pl.BlockSpec(shape, lambda *_: (0,) * len(shape))


def params(steps=0):
    if steps:
        return pltpu.CompilerParams(dimension_semantics=("arbitrary",))
    return pltpu.CompilerParams()


def request_kernel(core_ref, lengths_ref, owner_ref, row_ref, request_ref, slot_ref, facts_ref):
    shape = request_ref.shape
    match = owner_ref[...] == iota(shape, 0)
    earlier = jnp.where(iota(shape, 0) < iota(shape, 1), 1.0, 0.0).astype(BF16)
    before = nn_dot(jnp.where(match, 1.0, 0.0).astype(BF16), earlier)
    rank = jnp.sum(jnp.where(match, before, 0.0), axis=0, keepdims=True).astype(I32)
    slot_ref[...] = owner_ref[...] * CAPACITY + rank
    wanted = row_ref[...].astype(F32) + 1.0
    lists = [
        jnp.sum(jnp.where(match & (before == c), wanted, 0.0), axis=1, keepdims=True)
        for c in range(CAPACITY)
    ]
    lane = iota(shape, 1)
    request_ref[...] = jnp.where(
        lane == 0, lists[0], jnp.where(lane == 1, lists[1], 0.0)
    ).astype(I32)
    core = core_ref[0]
    one, two, three = lengths_ref[0, 0], lengths_ref[0, 1], lengths_ref[0, 2]
    half = (one + two + three) // 2
    most = jnp.maximum(one, jnp.maximum(two, three))
    longest = jnp.where(one == most, 0, jnp.where(two == most, one, one + two))
    inner = jnp.where(one == most, two, one)
    facts_ref[0] = core
    facts_ref[1] = jnp.where(core == 0, longest & (half - 1), 0)
    facts_ref[2] = jnp.where(core == 0, 0, inner)
    facts_ref[3] = longest


def split_scale(scale):
    high = scale.astype(BF16).astype(F32)
    rest = scale - high
    middle = rest.astype(BF16).astype(F32)
    return high, middle, rest - middle


def fetch_kernel(incoming_ref, table_ref, scale_ref, out_ref, chosen_ref):
    step = pl.program_id(0)
    slots, size = chosen_ref.shape
    chunk = table_ref.shape[1]
    width = chunk * pl.num_programs(0)

    @pl.when(step == 0)
    def _():
        devices = slots // CAPACITY
        device_of = iota((slots, devices), 0) >> 1 == iota((slots, devices), 1)
        spread = jnp.where(device_of, 1.0, 0.0).astype(BF16)
        wanted = incoming_ref[...]
        high = nn_dot(spread, (wanted >> 4).astype(F32).astype(BF16))
        low = nn_dot(spread, (wanted & 15).astype(F32).astype(BF16))
        mine = iota((slots, 128), 1) == (iota((slots, 128), 0) & 1)
        row = jnp.sum(jnp.where(mine, high * 16.0 + low, 0.0), axis=1, keepdims=True)
        chosen = row.astype(I32) - 1 == iota((slots, size), 1)
        chosen_ref[...] = jnp.where(chosen, 1.0, 0.0).astype(BF16)
        scale = jnp.sum(jnp.where(chosen, scale_ref[...], 0.0), axis=1, keepdims=True)
        high, middle, low = split_scale(scale)
        lane = iota((slots, 128), 1)
        pieces = jnp.where(
            lane == 0, high, jnp.where(lane == 1, middle, jnp.where(lane == 2, low, 0.0))
        )
        out_ref[:, 1024:1152] = pieces.astype(BF16)

    base = pl.multiple_of(step * chunk, chunk)
    out_ref[:, pl.ds(base, chunk)] = nn_dot(chosen_ref[...], table_ref[...]).astype(BF16)


def project_kernel(gathered_ref, mixed_ref, wu, wv, wq, wk, packed_ref, proj_ref, embed_ref, norm):
    width = embed_ref.shape[1]

    @pl.when(pl.program_id(0) == 0)
    def _():
        total = gathered_ref[...]
        scale = total[:, width : width + 1] + (
            total[:, width + 1 : width + 2] + total[:, width + 2 : width + 3]
        )
        embedded = total[:, :width] * scale
        embed_ref[...] = embedded
        norm[...] = normalize(embedded)[0].astype(BF16)

    for t, w in enumerate((wu, wv, wq, wk)):
        projected = nn_dot(norm[...], w[...])
        proj_ref[t] = projected
        active = (projected * jax.nn.sigmoid(projected)).astype(BF16)
        for i in range(2):
            packed_ref[i, :, t * 128 : (t + 1) * 128] = active[:, i * 128 : (i + 1) * 128]
    for i in range(2):
        packed_ref[i, :, 512:640] = mixed_ref[:, i * 128 : (i + 1) * 128].astype(BF16)


def upper_rows(facts, s, shape):
    rows = shape[0]
    residue = s * 2 * rows + facts[0] * rows + iota(shape, 0)
    return (jnp.where(residue >= facts[3], 1, 0) ^ facts[0]) == 1


def choose(mask, yes, no):
    return jnp.where(mask, yes.astype(F32), no.astype(F32)).astype(BF16)


def split_kernel(facts, x_ref, send_ref):
    quarter = send_ref.shape[0]
    for s in range(quarter):
        upper = upper_rows(facts, s, send_ref.shape[1:])
        send_ref[s] = choose(upper, x_ref[s + quarter], x_ref[s])


def join_kernel(facts, mine_ref, received_ref, out_ref):
    quarter = mine_ref.shape[0]
    for s in range(quarter):
        upper = upper_rows(facts, s, mine_ref.shape[1:])
        out_ref[s] = choose(upper, mine_ref[s], received_ref[s])
        out_ref[s + quarter] = choose(upper, received_ref[s], mine_ref[s])


def needed_keys(block, count):
    return list(range(count)) if block == 0 else list(range(block + 1))


def block_base(block, shift, count):
    return pl.multiple_of(((shift // TILE + block) & (count - 1)) * TILE, TILE)


def order_of(base, shape, axis, shift, half):
    return (base + iota(shape, axis) - shift) & (half - 1)


def query_terms(place, bound, half):
    later = place >= bound
    length = jnp.where(later, half - bound, bound).astype(F32)
    return jnp.where(later, bound, 0), 1.0 / length


def attend_kernel(facts, x_ref, received_ref, y_ref, att_ref, stats_ref):
    core, shift, bound = facts[0], facts[1], facts[2]
    half = y_ref.shape[0]
    quarter, rows, lanes = received_ref.shape
    heads = stats_ref.shape[0]
    for s in range(quarter):
        keep = choose(upper_rows(facts, s, (rows, lanes)), x_ref[s], x_ref[s + quarter])
        near = pl.multiple_of((2 * s + core) * rows, rows)
        far = pl.multiple_of((2 * s + 1 - core) * rows, rows)
        y_ref[pl.ds(near, rows), :] = keep
        y_ref[pl.ds(far, rows), :] = received_ref[s]

    hdim = 128
    scaling = hdim ** (-0.5)
    count = half // TILE
    for qi in range(count):
        base = block_base(qi, shift, count)
        span = pl.ds(base, TILE)
        place = order_of(base, (TILE, 1), 0, shift, half)
        first, inv_length = query_terms(place, bound, half)
        query = y_ref[span, 256:384]
        attention = 0.0
        for ki in needed_keys(qi, count):
            key_base = block_base(ki, shift, count)
            keys = pl.ds(key_base, TILE)
            scores = nt_dot(query, y_ref[keys, 384:512]) * scaling
            at = order_of(key_base, (1, TILE), 1, shift, half)
            allowed = (at <= place) & (at >= first)
            weights = jnp.where(
                allowed, scores * jax.nn.sigmoid(scores) * inv_length, 0.0
            ).astype(BF16)
            attention += nn_dot(weights, y_ref[keys, 128:256])

        att_ref[span, :] = attention
        gated = y_ref[span, 512:640].astype(F32) * y_ref[span, 0:128].astype(F32)
        center = jnp.mean(attention, axis=1, keepdims=True)
        shifted = attention - center
        columns = [
            center,
            jnp.sum(shifted * shifted, axis=1, keepdims=True),
            jnp.sum(gated, axis=1, keepdims=True),
            jnp.sum(gated * shifted, axis=1, keepdims=True),
        ]
        lane = iota((TILE, 128), 1)
        table = jnp.zeros((TILE, 128), F32)
        for i, column in enumerate(columns):
            table = jnp.where(lane == i, column, table)
        turned = table.T[0:4]
        for h in range(heads):
            stats_ref[h, :, span] = turned


def backward_kernel(facts, y_ref, att_ref, stats_ref, mine_ref, send_ref, attn, grad, dq, dk, dv):
    core, shift, bound = facts[0], facts[1], facts[2]
    half = y_ref.shape[0]
    heads = stats_ref.shape[0]
    quarter, rows = mine_ref.shape[0], mine_ref.shape[1]
    hdim = 128
    width = heads * hdim
    scaling = hdim ** (-0.5)
    count = half // TILE
    stat = [[stats_ref[h, i : i + 1, :] for i in range(4)] for h in range(heads)]
    mean = sum(s[0] for s in stat) / heads
    variance, mean_grad, mean_prod = 0.0, 0.0, 0.0
    for center, spread, grad_sum, prod_sum in stat:
        offset = center - mean
        variance += spread + hdim * offset * offset
        mean_grad += grad_sum
        mean_prod += prod_sum + offset * grad_sum
    inv_attn = lax.rsqrt(variance / width + EPSILON)
    line = iota((128, half), 0)
    table = jnp.where(
        line == 0,
        mean,
        jnp.where(
            line == 1,
            inv_attn,
            jnp.where(line == 2, mean_grad / width, inv_attn * mean_prod / width),
        ),
    )
    columns = table.T
    for qi in range(count):
        span = slice(qi * TILE, (qi + 1) * TILE)
        inv = columns[span, 1:2]
        attn_norm = (att_ref[span, :] - columns[span, 0:1]) * inv
        gated = y_ref[span, 512:640].astype(F32) * y_ref[span, 0:128].astype(F32)
        attn[span, :] = attn_norm.astype(BF16)
        grad[span, :] = (
            inv * (gated - columns[span, 2:3] - attn_norm * columns[span, 3:4])
        ).astype(BF16)
    dq[...] = jnp.zeros_like(dq)
    for ki in range(count):
        key_base = block_base(ki, shift, count)
        keys = pl.ds(key_base, TILE)
        at = order_of(key_base, (TILE, 1), 0, shift, half)
        key, value = y_ref[keys, 384:512], y_ref[keys, 128:256]
        grad_key, grad_value = 0.0, 0.0
        for qi in range(count):
            if ki not in needed_keys(qi, count):
                continue
            base = block_base(qi, shift, count)
            span = pl.ds(base, TILE)
            place = order_of(base, (1, TILE), 1, shift, half)
            first, inv_length = query_terms(place, bound, half)
            query, grad_out = y_ref[span, 256:384], grad[span, :]
            scores = nt_dot(key, query) * scaling
            allowed = (at <= place) & (at >= first)
            sig = jax.nn.sigmoid(scores)
            product = scores * sig
            weights = jnp.where(allowed, product * inv_length, 0.0).astype(BF16)
            slope = (sig + product * (1.0 - sig)) * (inv_length * scaling)
            grad_weights = nt_dot(value, grad_out)
            grad_scores = jnp.where(allowed, grad_weights * slope, 0.0).astype(BF16)
            grad_value += nn_dot(weights, grad_out)
            grad_key += nn_dot(grad_scores, query)
            dq[span, :] += tn_dot(grad_scores, key)
        dk[keys, :] = grad_key.astype(BF16)
        dv[keys, :] = grad_value.astype(BF16)

    for s in range(quarter):
        near = pl.ds(pl.multiple_of((2 * s + core) * rows, rows), rows)
        far = pl.ds(pl.multiple_of((2 * s + 1 - core) * rows, rows), rows)
        for i, ref in enumerate((attn, dv, dq, dk)):
            columns = slice(i * hdim, (i + 1) * hdim)
            mine_ref[s, :, columns] = ref[near, :].astype(BF16)
            send_ref[s, :, columns] = ref[far, :].astype(BF16)


def finish_kernel(
    back_ref, proj_ref, mixed_ref, slot_ref, embed_ref, cot_ref, wu, wv, wq, wk, out_ref, gated_ref, acc
):
    step = pl.program_id(0)

    def part(i):
        columns = slice(i * 128, (i + 1) * 128)
        return jnp.concatenate([back_ref[0, :, columns], back_ref[1, :, columns]], axis=1).astype(F32)

    attn_norm = part(0)
    total = 0.0
    for t, w in enumerate((wu, wv, wq, wk)):
        projected = proj_ref[t]
        sig = jax.nn.sigmoid(projected)
        slope = sig * (1.0 + projected * (1.0 - sig))
        if t == 0:
            grad_act = mixed_ref[...] * attn_norm
            gate = (projected * sig).astype(BF16).astype(F32)
            gated_ref[...] = (attn_norm * gate).astype(BF16)
        else:
            grad_act = part(t)
        total += nt_dot((grad_act * slope).astype(BF16), w[...])

    @pl.when(step == 0)
    def _():
        acc[...] = total

    @pl.when(step > 0)
    def _():
        acc[...] += total

    @pl.when(step == pl.num_programs(0) - 1)
    def _():
        normed, inv_embed = normalize(embed_ref[...])
        grad_embed = cot_ref[...].astype(F32) + normalize_back(acc[...], normed, inv_embed)
        slots, rows = out_ref.shape[0], slot_ref.shape[1]
        place = jnp.where(slot_ref[...] == iota((slots, rows), 0), 1.0, 0.0).astype(BF16)
        out_ref[...] = nn_dot(place, grad_embed.astype(BF16)).astype(BF16)


def table_kernel(incoming_ref, arrived_ref, scale_ref, out_ref):
    block, slots = out_ref.shape[0], arrived_ref.shape[0]
    base = pl.program_id(0) * block
    chosen = incoming_ref[...] - 1 - base == iota((block, slots), 0)
    total = nn_dot(jnp.where(chosen, 1.0, 0.0).astype(BF16), arrived_ref[...])
    scale = jnp.broadcast_to(scale_ref[...], (128, block)).T
    out_ref[...] = total * scale[:, 0:1]


def per_device(
    table_rows,
    row_scales,
    owners,
    shard_rows,
    history_lengths,
    input_weight,
    output_weight,
    cotangent,
):
    rows = owners.shape[0]
    table_size, width = table_rows.shape
    heads = HEADS
    hdim = width // heads
    devices = lax.axis_size(("dp", "cp"))
    n_cp = lax.axis_size("cp")
    cores = n_cp // heads
    half = rows * n_cp // 2
    quarter = heads // 2
    slots = devices * CAPACITY
    groups = [[i * cores + c for i in range(heads)] for c in range(cores)]
    swap = [(i, i ^ 1) for i in range(n_cp)]
    core = (lax.axis_index("cp") % cores).reshape(1)
    everyone = ("dp", "cp")
    shape = jax.ShapeDtypeStruct
    smem = pl.BlockSpec(memory_space=pltpu.SMEM)

    def exchange(values, axes, **options):
        return lax.all_to_all(values, axes, split_axis=0, concat_axis=0, tiled=True, **options)

    def to_heads(values):
        return exchange(values, "cp", axis_index_groups=groups)

    def to_all(values):
        lanes = values.shape[1]
        return exchange(values.reshape(devices, CAPACITY, lanes), everyone).reshape(slots, lanes)

    scale_line = row_scales.reshape(1, table_size)
    requests, slot_line, facts = pl.pallas_call(
        request_kernel,
        in_specs=[smem, smem, full((1, rows)), full((1, rows))],
        out_specs=(full((devices, 128)), full((1, rows)), smem),
        out_shape=(shape((devices, 128), I32), shape((1, rows), I32), shape((4,), I32)),
        grid=(1,),
        compiler_params=params(1),
        name="request",
    )(core, history_lengths, owners.reshape(1, rows), shard_rows.reshape(1, rows))
    incoming = exchange(requests.reshape(devices, 1, 128), everyone).reshape(devices, 128)

    wide = width + 128
    chunk = width // 4
    fetched = pl.pallas_call(
        fetch_kernel,
        grid=(width // chunk,),
        in_specs=[
            full((devices, 128)),
            pl.BlockSpec((table_size, chunk), lambda i: (0, i)),
            full((1, table_size)),
        ],
        out_specs=full((slots, wide)),
        out_shape=shape((slots, wide), BF16),
        scratch_shapes=[pltpu.VMEM((slots, table_size), BF16)],
        compiler_params=params(1),
        name="fetch",
    )(incoming, table_rows, scale_line)
    returned = to_all(fetched)
    place = (slot_line == jnp.arange(slots, dtype=I32)[:, None]).astype(BF16)
    gathered = jnp.einsum("sr,sd->rd", place, returned, preferred_element_type=F32)

    grad_mixed = jnp.einsum("rk,dk->rd", cotangent, output_weight, preferred_element_type=F32)

    pair = 2 * hdim
    weight_specs = [
        pl.BlockSpec((width, pair), lambda i, t=t: (0, t * (heads // 2) + i)) for t in range(4)
    ]
    packed, projected, embedded = pl.pallas_call(
        project_kernel,
        grid=(heads // 2,),
        in_specs=[full((rows, wide)), pl.BlockSpec((rows, pair), lambda i: (0, i))] + weight_specs,
        out_specs=(
            pl.BlockSpec((2, rows, 5 * hdim), lambda i: (i, 0, 0)),
            pl.BlockSpec((4, rows, pair), lambda i: (0, 0, i)),
            full((rows, width)),
        ),
        out_shape=(
            shape((heads, rows, 5 * hdim), BF16),
            shape((4, rows, width), F32),
            shape((rows, width), F32),
        ),
        scratch_shapes=[pltpu.VMEM((rows, width), BF16)],
        compiler_params=params(1),
        name="project",
    )(gathered, grad_mixed, *([input_weight] * 4))

    branches = to_heads(packed)
    send = pl.pallas_call(
        split_kernel,
        in_specs=[smem, full(branches.shape)],
        out_specs=full((quarter, rows, 5 * hdim)),
        out_shape=shape((quarter, rows, 5 * hdim), BF16),
        grid=(1,),
        compiler_params=params(1),
        name="split",
    )(facts, branches)
    received = lax.ppermute(send, "cp", swap)
    ordered, attention, stats = pl.pallas_call(
        attend_kernel,
        in_specs=[smem, full(branches.shape), full(received.shape)],
        out_specs=(full((half, 5 * hdim)), full((half, hdim)), full((heads, 4, half))),
        out_shape=(
            shape((half, 5 * hdim), BF16),
            shape((half, hdim), F32),
            shape((heads, 4, half), F32),
        ),
        grid=(1,),
        compiler_params=params(1),
        name="attend",
    )(facts, branches, received)
    stats = to_heads(stats)

    backed = shape((quarter, rows, 4 * hdim), BF16)
    mine, send = pl.pallas_call(
        backward_kernel,
        in_specs=[smem, full(ordered.shape), full(attention.shape), full(stats.shape)],
        out_specs=(full(backed.shape), full(backed.shape)),
        out_shape=(backed, backed),
        scratch_shapes=[
            pltpu.VMEM((half, hdim), BF16),
            pltpu.VMEM((half, hdim), BF16),
            pltpu.VMEM((half, hdim), F32),
            pltpu.VMEM((half, hdim), BF16),
            pltpu.VMEM((half, hdim), BF16),
        ],
        grid=(1,),
        compiler_params=params(1),
        name="backward",
    )(facts, ordered, attention, stats)
    received = lax.ppermute(send, "cp", swap)
    joined = pl.pallas_call(
        join_kernel,
        in_specs=[smem, full(backed.shape), full(backed.shape)],
        out_specs=full((heads, rows, 4 * hdim)),
        out_shape=shape((heads, rows, 4 * hdim), BF16),
        grid=(1,),
        compiler_params=params(1),
        name="join",
    )(facts, mine, received)
    back = to_heads(joined)

    outgoing, mixed = pl.pallas_call(
        finish_kernel,
        grid=(heads // 2,),
        in_specs=[
            pl.BlockSpec((2, rows, 4 * hdim), lambda i: (i, 0, 0)),
            pl.BlockSpec((4, rows, pair), lambda i: (0, 0, i)),
            pl.BlockSpec((rows, pair), lambda i: (0, i)),
            full((1, rows)),
            full((rows, width)),
            full((rows, width)),
        ]
        + weight_specs,
        out_specs=(full((slots, width)), pl.BlockSpec((rows, pair), lambda i: (0, i))),
        out_shape=(shape((slots, width), BF16), shape((rows, width), BF16)),
        scratch_shapes=[pltpu.VMEM((rows, width), F32)],
        compiler_params=params(1),
        name="finish",
    )(back, projected, grad_mixed, slot_line, embedded, cotangent, *([input_weight] * 4))
    arrived = to_all(outgoing)
    layer_out = (
        embedded + jnp.dot(mixed, output_weight, preferred_element_type=F32)
    ).astype(BF16)

    block = 256
    table_grad = pl.pallas_call(
        table_kernel,
        grid=(table_size // block,),
        in_specs=[
            full((1, slots)),
            full((slots, width)),
            pl.BlockSpec((1, block), lambda i: (0, i)),
        ],
        out_specs=pl.BlockSpec((block, width), lambda i: (i, 0)),
        out_shape=shape((table_size, width), F32),
        compiler_params=params(1),
        name="table",
    )(incoming[:, :CAPACITY].reshape(1, slots), arrived, scale_line)
    return (layer_out, table_grad)


def solution(mesh):
    return jax.shard_map(
        per_device,
        mesh=mesh,
        in_specs=(
            P(("dp", "cp"), None),
            P(("dp", "cp")),
            P(("dp", "cp"), None),
            P(("dp", "cp")),
            P("dp", None),
            P(),
            P(),
            P(("dp", "cp"), None),
        ),
        out_specs=(P(("dp", "cp"), None), P(("dp", "cp"), None)),
        check_vma=False,
    )
```

time: 211 us -> 179 us (0.85)
  blocking collectives: 9.35 us -> 75.1 us
  Pallas kernels: 0 us -> 47.8 us
  waiting for transfers between devices: 66.2 us -> 28.2 us
  matrix products: 37.2 us -> 3.89 us
  other arithmetic: 29.8 us -> 0 us
  starting transfers between devices: 39.4 us -> 13.5 us
  local copies, waits for them, and re-layouts: 26.9 us -> 8.4 us
    all_to_all x1 -> x4, blocking collectives: 9.35 us -> 75.1 us  [exchange(): lax.all_to_all(values, axes, split_axis=0, concat_axis=0, tiled=True, **o...]
    pallas_call x0 -> x9, Pallas kernels: none -> 47.8 us  [the longest x1 8.76 us: per_device(): pl.pallas_call(finish_kernel, grid=(heads // 2,), in_specs=[pl.BlockSpec(...]
    all_to_all x6 -> x2, waiting for transfers between devices: 64.6 us -> 24.5 us  [exchange(): lax.all_to_all(values, axes, split_axis=0, concat_axis=0, tiled=True, **o...]
    dot_general x14 -> x2, matrix products: 36.3 us -> 2.28 us  [the longest x1 1.15 us: per_device(): jnp.dot(mixed, output_weight, preferred_element_type=F32)]
    all_to_all x6 -> x2, starting transfers between devices: 33.7 us -> 9.42 us  [exchange(): lax.all_to_all(values, axes, split_axis=0, concat_axis=0, tiled=True, **o...]
    reduce_sum x9 -> x0, other arithmetic: 7.62 us -> none  [the longest x1 2.87 us: per_device(): jnp.sum(jnp.where(placing, shard_rows[:, None, None] + 1, 0), axis=0)]
    convert_element_type x2 -> x0, local copies, waits for them, and re-layouts: 6.11 us -> none  [per_device(): back[:, 1:].reshape(rows, 3 * width).astype(f32)]
    another operation x7 -> x0, other arithmetic: 5.73 us -> none  [the longest x2 3.13 us: split_histories(): jnp.stack([keep, received], 1)]
  transfers between devices with their start and end apart: 9 -> 4, of which waited for: 7 -> 4; matrix products, arithmetic and copies ran while one was open for 7% -> 2% of each run, Pallas kernels for 0% -> 0%
where the time goes in v2:
time: 179 us; the launch traced here: 178 us
  blocking collectives  75.1 us (42%)
  Pallas kernels  47.8 us (27%)
  waiting for transfers between devices  28.2 us (16%)
  starting transfers between devices  13.5 us (8%)
  local copies, waits for them, and re-layouts  8.4 us (5%)
  matrix products  3.89 us (2%)
    all_to_all x4, blocking collectives, exchange(): lax.all_to_all(values, axes, split_axis=0, concat_axis=0, tiled=True, **o...  75.1 us
    all_to_all x2, waiting for transfers between devices, exchange(): lax.all_to_all(values, axes, split_axis=0, concat_axis=0, tiled=True, **o...  24.5 us
    all_to_all x2, starting transfers between devices, exchange(): lax.all_to_all(values, axes, split_axis=0, concat_axis=0, tiled=True, **o...  9.42 us
    pallas_call x1, Pallas kernels, per_device(): pl.pallas_call(finish_kernel, grid=(heads // 2,), in_specs=[pl.BlockSpec(...  8.76 us
    pallas_call x1, Pallas kernels, per_device(): pl.pallas_call(backward_kernel, in_specs=[smem, full(ordered.shape), full...  7.94 us
    pallas_call x1, Pallas kernels, per_device(): pl.pallas_call(project_kernel, grid=(heads // 2,), in_specs=[full((rows,...  7.4 us
    pallas_call x1, Pallas kernels, per_device(): pl.pallas_call(table_kernel, grid=(table_size // block,), in_specs=[full(...  6.89 us
    pallas_call x1, Pallas kernels, per_device(): pl.pallas_call(fetch_kernel, grid=(width // chunk,), in_specs=[full((devi...  5.54 us
  transfers between devices with their start and end apart: 4, of which 4 were waited for; matrix products, arithmetic and copies ran while one was open for 2% of the time, Pallas kernels for 0%

profile of v2, /device:TPU:1, one launch (start us, length us, event | category | flops | bytes accessed | tf_op | source)
XLA Modules:
  0.0 177.7 jit_solution(13774670567479840001)
XLA Ops:
  0.6 0.0 copy-start
  0.7 1.7 request.1
  2.4 21.3 %all_to_all.30 = s32[128,1,128]{2,1,0:T(1,128)} all-to-all(s32[128,1,128]{2,1,0:T(1,128)} %bitcast.17), channel_id=1, replica_groups=mesh['dp'=8,'cp'=16] {'dp','cp'}, dimensions={0} | all-to-all | bytes 131072 | tf_op jit(solution)/shard_map/all_to_all | solution.py:392
  23.7 5.5 %fetch.1 = bf16[256,1152]{1,0:T(8,128)(2,1)} custom-call(s32[128,128]{1,0:T(8,128)} %bitcast.15, bf16[2048,1024]{1,0:T(8,128)(2,1)} %table_ref.1, f32[1,2048]{1,0:T(1,128)} %bitcast.18), custom_call_target="tpu_custom_call" | custom-call | tf_op jit(solution)/shard_map/fetch/pallas_call | solution.py:415
  29.2 2.6 %reshape.43 = bf16[128,2,1152]{2,1,0:T(2,128)(2,1)} reshape(bf16[256,1152]{1,0:T(8,128)(2,1)} %fetch.1) | data formatting | bytes 1179648 | tf_op jit(solution)/shard_map/reshape | solution.py:399
  31.9 4.5 %all-to-all-start.1 = ((bf16[128,2,1152]{2,1,0:T(2,128)(2,1)}), bf16[128,2,1152]{2,1,0:T(2,128)(2,1)S(1)}, u32[]{:S(2)}, u32[]{:S(2)}) async-start(bf16[128,2,1152]{2,1,0:T(2,128)(2,1)} %reshape.43), calls=%async_computation.1 | async-start | bytes 1179648 | tf_op jit(solution)/shard_map/all_to_all | solution.py:392
  36.4 1.6 fusion.3.mixed_ref
  38.0 12.7 %all-to-all-done.1 = bf16[128,2,1152]{2,1,0:T(2,128)(2,1)S(1)} async-done(((bf16[128,2,1152]{2,1,0:T(2,128)(2,1)}), bf16[128,2,1152]{2,1,0:T(2,128)(2,1)S(1)}, u32[]{:S(2)}, u32[]{:S(2)}) %all-to-all-start.1) | async-done | bytes 589856 | tf_op jit(solution)/shard_map/all_to_all | solution.py:392
  50.8 0.2 reshape.44
  51.0 1.1 fusion.1.gathered_ref
  52.1 7.4 %project.1 = (bf16[8,128,640]{2,1,0:T(8,128)(2,1)}, f32[4,128,1024]{2,1,0:T(8,128)}, f32[128,1024]{1,0:T(8,128)}) custom-call(f32[128,1152]{1,0:T(8,128)} %fusion.1.gathered_ref, f32[128,1024]{1,0:T(8,128)} %fusion.3.mixed_ref, bf16[1024,4096]{1,0:T(8,128)(2,1)} %wk.3, bf16[1024,4096]{1,0:T(8,128)(2,1)} %wk.3, bf16[1024,4096]{1,0:T(8,128)(2,1)} %wk.3, ...), custom_call_target="tpu_custom_call" | custom-call | tf_op jit(solution)/shard_map/project/pallas_call | solution.py:439
  59.5 22.4 %all_to_all.31.x_ref = bf16[8,128,640]{2,1,0:T(8,128)(2,1)} all-to-all(bf16[8,128,640]{2,1,0:T(8,128)(2,1)} %get-tuple-element.19), channel_id=1, replica_groups={{0,2,4,6,8,10,12,14},{1,3,5,7,9,11,13,15},{16,18,20,22,24,26,28,30},{17..., dimensions={0} | all-to-all | bytes 2621440 | tf_op jit(solution)/shard_map/all_to_all | solution.py:392
  82.0 2.4 %split.1 = bf16[4,128,640]{2,1,0:T(8,128)(2,1)} custom-call(s32[4]{0:T(128)} %get-tuple-element.18.facts, bf16[8,128,640]{2,1,0:T(8,128)(2,1)} %all_to_all.31.x_ref), custom_call_target="tpu_custom_call" | custom-call | tf_op jit(solution)/shard_map/split/pallas_call | solution.py:459
  84.3 2.4 %collective-permute-start = (bf16[4,128,640]{2,1,0:T(8,128)(2,1)}, bf16[4,128,640]{2,1,0:T(8,128)(2,1)S(1)}, u32[]{:S(2)}, u32[]{:S(2)}) collective-permute-start(bf16[4,128,640]{2,1,0:T(8,128)(2,1)} %split.1), channel_id=1, source_target_pairs={{0,1},{1,0},{2,3},{3,2},{4,5},{5,4},{6,7},{7,6},{8,9},{9,8},{10,11... | collective-permute-start | bytes 1966088 | tf_op jit(solution)/shard_map/ppermute | solution.py:468
  86.8 1.9 %collective-permute-done.received_ref = bf16[4,128,640]{2,1,0:T(8,128)(2,1)S(1)} collective-permute-done((bf16[4,128,640]{2,1,0:T(8,128)(2,1)}, bf16[4,128,640]{2,1,0:T(8,128)(2,1)S(1)}, u32[]{:S(2)}, u32[]{:S(2)}) %collective-permute-start) | collective-permute-done | bytes 655392 | tf_op jit(solution)/shard_map/ppermute | solution.py:468
  88.7 0.8 copy-done.3
  89.6 4.7 %attend.1 = (bf16[1024,640]{1,0:T(8,128)(2,1)}, f32[1024,128]{1,0:T(8,128)}, f32[8,4,1024]{2,1,0:T(4,128)}) custom-call(s32[4]{0:T(128)} %get-tuple-element.18.facts, bf16[8,128,640]{2,1,0:T(8,128)(2,1)} %all_to_all.31.x_ref, bf16[4,128,640]{2,1,0:T(8,128)(2,1)} %copy-done.3), custom_call_target="tpu_custom_call" | custom-call | tf_op jit(solution)/shard_map/attend/pallas_call | solution.py:469
  94.3 10.8 %all_to_all.32.stats_ref = f32[8,4,1024]{2,1,0:T(4,128)} all-to-all(f32[8,4,1024]{2,1,0:T(4,128)} %get-tuple-element.22), channel_id=1, replica_groups={{0,2,4,6,8,10,12,14},{1,3,5,7,9,11,13,15},{16,18,20,22,24,26,28,30},{17..., dimensions={0} | all-to-all | bytes 262144 | tf_op jit(solution)/shard_map/all_to_all | solution.py:392
  105.0 7.9 %backward.1 = (bf16[4,128,512]{2,1,0:T(8,128)(2,1)}, bf16[4,128,512]{2,1,0:T(8,128)(2,1)}) custom-call(s32[4]{0:T(128)} %get-tuple-element.18.facts, bf16[1024,640]{1,0:T(8,128)(2,1)} %get-tuple-element.20.y_ref, f32[1024,128]{1,0:T(8,128)} %get-tuple-element.21.att_ref, f32[8,4,1024]{2,1,0:T(4,128)} %all_to_all.32.stats_ref), custom_call_target="tpu_custom_call" | custom-call | tf_op jit(solution)/shard_map/backward/pallas_call | solution.py:485
  113.0 1.7 collective-permute-start.1
  114.7 1.7 collective-permute-done.1.received_ref
  116.4 0.8 copy-done.5
  117.2 2.5 %join.1 = bf16[8,128,512]{2,1,0:T(8,128)(2,1)} custom-call(s32[4]{0:T(128)} %get-tuple-element.18.facts, bf16[4,128,512]{2,1,0:T(8,128)(2,1)} %get-tuple-element.23.mine_ref, bf16[4,128,512]{2,1,0:T(8,128)(2,1)} %copy-done.5), custom_call_target="tpu_custom_call" | custom-call | tf_op jit(solution)/shard_map/join/pallas_call | solution.py:502
  119.7 20.6 %all_to_all.33.back_ref = bf16[8,128,512]{2,1,0:T(8,128)(2,1)} all-to-all(bf16[8,128,512]{2,1,0:T(8,128)(2,1)} %join.1), channel_id=1, replica_groups={{0,2,4,6,8,10,12,14},{1,3,5,7,9,11,13,15},{16,18,20,22,24,26,28,30},{17..., dimensions={0} | all-to-all | bytes 2097152 | tf_op jit(solution)/shard_map/all_to_all | solution.py:392
  140.4 8.8 %finish.1 = (bf16[256,1024]{1,0:T(8,128)(2,1)}, bf16[128,1024]{1,0:T(8,128)(2,1)}) custom-call(bf16[8,128,512]{2,1,0:T(8,128)(2,1)} %all_to_all.33.back_ref, f32[4,128,1024]{2,1,0:T(8,128)} %get-tuple-element.25.proj_ref, f32[128,1024]{1,0:T(8,128)} %fusion.3.mixed_ref, s32[1,128]{1,0:T(1,128)} %get-tuple-element.15.slot_ref, ...), custom_call_target="tpu_custom_call" | custom-call | tf_op jit(solution)/shard_map/finish/pallas_call | solution.py:513
  149.1 2.1 %reshape.46 = bf16[128,2,1024]{2,1,0:T(2,128)(2,1)} reshape(bf16[256,1024]{1,0:T(8,128)(2,1)} %get-tuple-element.27) | data formatting | bytes 1048576 | tf_op jit(solution)/shard_map/reshape | solution.py:399
  151.3 4.9 %all-to-all-start.5 = ((bf16[128,2,1024]{2,1,0:T(2,128)(2,1)}), bf16[128,2,1024]{2,1,0:T(2,128)(2,1)S(1)}, u32[]{:S(2)}, u32[]{:S(2)}) async-start(bf16[128,2,1024]{2,1,0:T(2,128)(2,1)} %reshape.46), calls=%async_computation.5 | async-start | bytes 1048576 | tf_op jit(solution)/shard_map/all_to_all | solution.py:392
  156.2 0.7 reshape.45.incoming_ref
  156.9 1.2 fusion
  158.1 11.7 %all-to-all-done.5 = bf16[128,2,1024]{2,1,0:T(2,128)(2,1)S(1)} async-done(((bf16[128,2,1024]{2,1,0:T(2,128)(2,1)}), bf16[128,2,1024]{2,1,0:T(2,128)(2,1)S(1)}, u32[]{:S(2)}, u32[]{:S(2)}) %all-to-all-start.5) | async-done | bytes 524320 | tf_op jit(solution)/shard_map/all_to_all | solution.py:392
  169.8 1.0 reshape.47.arrived_ref
  170.8 6.9 %table.1 = f32[2048,1024]{1,0:T(8,128)} custom-call(s32[1,256]{1,0:T(1,128)} %reshape.45.incoming_ref, bf16[256,1024]{1,0:T(8,128)(2,1)} %reshape.47.arrived_ref, f32[1,2048]{1,0:T(1,128)} %bitcast.19), custom_call_target="tpu_custom_call" | custom-call | tf_op jit(solution)/shard_map/table/pallas_call | solution.py:537
  (13 shorter events, 0.0 us)
Async XLA Ops:
  0.6 35.7 %copy-start = (bf16[1024,1024]{1,0:T(8,128)(2,1)S(1)}, bf16[1024,1024]{1,0:T(8,128)(2,1)}, u32[]{:S(2)}) copy-start(bf16[1024,1024]{1,0:T(8,128)(2,1)} %param.14) | copy-start | bytes 6291460
  29.2 7.2 %copy-start.2 = (bf16[128,1024]{1,0:T(8,128)(2,1)S(1)}, bf16[128,1024]{1,0:T(8,128)(2,1)}, u32[]{:S(2)}) copy-start(bf16[128,1024]{1,0:T(8,128)(2,1)} %cot_ref.1) | copy-start | bytes 786436
  31.9 18.9 %all-to-all-start.1 = ((bf16[128,2,1152]{2,1,0:T(2,128)(2,1)}), bf16[128,2,1152]{2,1,0:T(2,128)(2,1)S(1)}, u32[]{:S(2)}, u32[]{:S(2)}) async-start(bf16[128,2,1152]{2,1,0:T(2,128)(2,1)} %reshape.43), calls=%async_computation.1 | async-start | bytes 1179648 | tf_op jit(solution)/shard_map/all_to_all | solution.py:392
  36.4 14.6 %copy-start.7 = (s32[1,128]{1,0:T(1,128)S(1)}, s32[1,128]{1,0:T(1,128)}, u32[]{:S(2)}) copy-start(s32[1,128]{1,0:T(1,128)} %get-tuple-element.15.slot_ref) | copy-start | bytes 1540
  84.3 4.4 %collective-permute-start = (bf16[4,128,640]{2,1,0:T(8,128)(2,1)}, bf16[4,128,640]{2,1,0:T(8,128)(2,1)S(1)}, u32[]{:S(2)}, u32[]{:S(2)}) collective-permute-start(bf16[4,128,640]{2,1,0:T(8,128)(2,1)} %split.1), channel_id=1, source_target_pairs={{0,1},{1,0},{2,3},{3,2},{4,5},{5,4},{6,7},{7,6},{8,9},{9,8},{10,11... | collective-permute-start | bytes 1966088 | tf_op jit(solution)/shard_map/ppermute | solution.py:468
  88.7 0.8 copy-start.3
  113.0 3.4 %collective-permute-start.1 = (bf16[4,128,512]{2,1,0:T(8,128)(2,1)}, bf16[4,128,512]{2,1,0:T(8,128)(2,1)S(1)}, u32[]{:S(2)}, u32[]{:S(2)}) collective-permute-start(bf16[4,128,512]{2,1,0:T(8,128)(2,1)} %get-tuple-element.24), channel_id=1, source_target_pairs={{0,1},{1,0},{2,3},{3,2},{4,5},{5,4},{6,7},{7,6},{8,9},{9,8},{10,11... | collective-permute-start | bytes 1572872 | tf_op jit(solution)/shard_map/ppermute | solution.py:501
  116.4 0.8 copy-start.5
  149.1 7.1 %copy-start.4 = (s32[128,1,128]{2,1,0:T(1,128)S(1)}, s32[128,1,128]{2,1,0:T(1,128)}, u32[]{:S(2)}) copy-start(s32[128,1,128]{2,1,0:T(1,128)} %all_to_all.30) | copy-start | bytes 196612
  149.1 7.8 %copy-start.1 = (f32[128,1024]{1,0:T(8,128)S(1)}, f32[128,1024]{1,0:T(8,128)}, u32[]{:S(2)}) copy-start(f32[128,1024]{1,0:T(8,128)} %get-tuple-element.17.embed_ref) | copy-start | bytes 1572868
  149.1 7.8 %copy-start.6 = (bf16[128,1024]{1,0:T(8,128)(2,1)S(1)}, bf16[128,1024]{1,0:T(8,128)(2,1)}, u32[]{:S(2)}) copy-start(bf16[128,1024]{1,0:T(8,128)(2,1)} %get-tuple-element.26) | copy-start | bytes 786436
  151.3 18.5 %all-to-all-start.5 = ((bf16[128,2,1024]{2,1,0:T(2,128)(2,1)}), bf16[128,2,1024]{2,1,0:T(2,128)(2,1)S(1)}, u32[]{:S(2)}, u32[]{:S(2)}) async-start(bf16[128,2,1024]{2,1,0:T(2,128)(2,1)} %reshape.46), calls=%async_computation.5 | async-start | bytes 1048576 | tf_op jit(solution)/shard_map/all_to_all | solution.py:392

commit v3 on v2

v3 whole, which is shorter than its diff:
```python
import jax
import jax.numpy as jnp
from jax import lax
from jax.experimental import pallas as pl
from jax.experimental.pallas import tpu as pltpu
from jax.sharding import PartitionSpec as P

HEADS = 8
EPSILON = 1e-05
CAPACITY = 2
TILE = 256
F32, BF16, I32 = jnp.float32, jnp.bfloat16, jnp.int32


def nt_dot(left, right):
    return lax.dot_general(left, right, (((1,), (1,)), ((), ())), preferred_element_type=F32)


def tn_dot(left, right):
    return lax.dot_general(left, right, (((0,), (0,)), ((), ())), preferred_element_type=F32)


def nn_dot(left, right):
    return jnp.dot(left, right, preferred_element_type=F32)


def copies(source, target, sems, spans):
    started = [
        pltpu.make_async_copy(source.at[span], target.at[span], sems.at[n])
        for n, span in enumerate(spans)
    ]
    for copy in started:
        copy.start()
    return started


def column_spans(total, step):
    return [(slice(None), slice(base, base + step)) for base in range(0, total, step)]


def iota(shape, axis):
    return lax.broadcasted_iota(I32, shape, axis)


def normalize(values):
    center = jnp.mean(values, axis=-1, keepdims=True)
    shifted = values - center
    inv_spread = lax.rsqrt(jnp.mean(shifted * shifted, axis=-1, keepdims=True) + EPSILON)
    return (shifted * inv_spread, inv_spread)


def normalize_back(grad_in, normed, inv_spread):
    return inv_spread * (
        grad_in
        - jnp.mean(grad_in, axis=-1, keepdims=True)
        - normed * jnp.mean(grad_in * normed, axis=-1, keepdims=True)
    )


def request_kernel(core_ref, lengths_ref, owner_ref, row_ref, request_ref, slot_ref, facts_ref):
    shape = request_ref.shape
    match = owner_ref[...] == iota(shape, 0)
    earlier = jnp.where(iota(shape, 0) < iota(shape, 1), 1.0, 0.0).astype(BF16)
    before = nn_dot(jnp.where(match, 1.0, 0.0).astype(BF16), earlier)
    rank = jnp.sum(jnp.where(match, before, 0.0), axis=0, keepdims=True).astype(I32)
    slot_ref[...] = owner_ref[...] * CAPACITY + rank
    wanted = row_ref[...].astype(F32) + 1.0
    lists = [
        jnp.sum(jnp.where(match & (before == c), wanted, 0.0), axis=1, keepdims=True)
        for c in range(CAPACITY)
    ]
    lane = iota(shape, 1)
    request_ref[...] = jnp.where(
        lane == 0, lists[0], jnp.where(lane == 1, lists[1], 0.0)
    ).astype(I32)
    core = core_ref[0]
    one, two, three = lengths_ref[0, 0], lengths_ref[0, 1], lengths_ref[0, 2]
    half = (one + two + three) // 2
    most = jnp.maximum(one, jnp.maximum(two, three))
    longest = jnp.where(one == most, 0, jnp.where(two == most, one, one + two))
    inner = jnp.where(one == most, two, one)
    facts_ref[0] = core
    facts_ref[1] = jnp.where(core == 0, longest & (half - 1), 0)
    facts_ref[2] = jnp.where(core == 0, 0, inner)
    facts_ref[3] = longest


def split_scale(scale):
    high = scale.astype(BF16).astype(F32)
    rest = scale - high
    middle = rest.astype(BF16).astype(F32)
    return high, middle, rest - middle


def fetch_kernel(incoming_ref, table_hbm, scale_ref, out_ref, table_ref, sems):
    loads = copies(table_hbm, table_ref, sems, column_spans(table_ref.shape[1], 512))
    slots, size, width = out_ref.shape[0], table_ref.shape[0], table_ref.shape[1]
    devices = slots // CAPACITY
    device_of = iota((slots, devices), 0) >> 1 == iota((slots, devices), 1)
    spread = jnp.where(device_of, 1.0, 0.0).astype(BF16)
    wanted = incoming_ref[...]
    high = nn_dot(spread, (wanted >> 4).astype(F32).astype(BF16))
    low = nn_dot(spread, (wanted & 15).astype(F32).astype(BF16))
    mine = iota((slots, 128), 1) == (iota((slots, 128), 0) & 1)
    row = jnp.sum(jnp.where(mine, high * 16.0 + low, 0.0), axis=1, keepdims=True)
    chosen = row.astype(I32) - 1 == iota((slots, size), 1)
    hot = jnp.where(chosen, 1.0, 0.0).astype(BF16)
    scale = jnp.sum(jnp.where(chosen, scale_ref[...], 0.0), axis=1, keepdims=True)
    high, middle, low = split_scale(scale)
    lane = iota((slots, 128), 1)
    pieces = jnp.where(
        lane == 0, high, jnp.where(lane == 1, middle, jnp.where(lane == 2, low, 0.0))
    )
    out_ref[:, width : width + 128] = pieces.astype(BF16)
    for n, base in enumerate(range(0, width, 512)):
        loads[n].wait()
        out_ref[:, base : base + 512] = nn_dot(hot, table_ref[:, base : base + 512]).astype(BF16)


def project_kernel(
    returned_ref, slot_ref, mixed_ref, weight_hbm, packed_ref, proj_ref, embed_ref, gate_ref, weight_ref, sems
):
    width = embed_ref.shape[1]
    loads = copies(weight_hbm, weight_ref, sems, column_spans(4 * width, width))
    heads = packed_ref.shape[0]
    slots, rows = returned_ref.shape[0], slot_ref.shape[1]
    place = jnp.where(slot_ref[...] == iota((slots, rows), 0), 1.0, 0.0).astype(BF16)
    total = tn_dot(place, returned_ref[...])
    scale = total[:, width : width + 1] + (
        total[:, width + 1 : width + 2] + total[:, width + 2 : width + 3]
    )
    embedded = total[:, :width] * scale
    embed_ref[...] = embedded
    normed = normalize(embedded)[0].astype(BF16)
    for t in range(4):
        loads[t].wait()
        for pair in range(heads // 2):
            columns = slice(pair * 256, (pair + 1) * 256)
            base = t * width + pair * 256
            projected = nn_dot(normed, weight_ref[:, base : base + 256])
            proj_ref[:, base : base + 256] = projected
            active = (projected * jax.nn.sigmoid(projected)).astype(BF16)
            if t == 0:
                gate_ref[:, columns] = active
                active = (active.astype(F32) * mixed_ref[:, columns]).astype(BF16)
            for i in range(2):
                packed_ref[2 * pair + i, :, t * 128 : (t + 1) * 128] = active[
                    :, i * 128 : (i + 1) * 128
                ]


def upper_rows(facts, core, s, shape):
    rows = shape[0]
    residue = s * 2 * rows + core * rows + iota(shape, 0)
    return (jnp.where(residue >= facts[3], 1, 0) ^ facts[0]) == 1


def choose(mask, yes, no):
    return jnp.where(mask, yes.astype(F32), no.astype(F32)).astype(BF16)


def join_kernel(facts, mine_ref, received_ref, out_ref):
    quarter = mine_ref.shape[0]
    for s in range(quarter):
        upper = upper_rows(facts, facts[0], s, mine_ref.shape[1:])
        out_ref[s] = choose(upper, mine_ref[s], received_ref[s])
        out_ref[s + quarter] = choose(upper, received_ref[s], mine_ref[s])


def needed_keys(block, count):
    return list(range(count)) if block == 0 else list(range(block + 1))


def block_base(block, shift, count):
    return pl.multiple_of(((shift // TILE + block) & (count - 1)) * TILE, TILE)


def order_of(base, shape, axis, shift, half):
    return (base + iota(shape, axis) - shift) & (half - 1)


def query_terms(place, bound, half):
    later = place >= bound
    length = jnp.where(later, half - bound, bound).astype(F32)
    return jnp.where(later, bound, 0), 1.0 / length


def attend_kernel(facts, x_ref, received_ref, y_hbm, att_hbm, stats_ref, y_ref, att_ref, y_sem, att_sems):
    core, shift, bound = facts[0], facts[1], facts[2]
    half = y_ref.shape[0]
    heads, rows, lanes = received_ref.shape
    quarter = heads // 2
    for s in range(quarter):
        for ref, side in ((x_ref, core), (received_ref, 1 - core)):
            upper = upper_rows(facts, side, s, (rows, lanes))
            at = pl.multiple_of((2 * s + side) * rows, rows)
            y_ref[pl.ds(at, rows), :] = choose(upper, ref[s], ref[s + quarter])

    stores = [pltpu.make_async_copy(y_ref, y_hbm, y_sem)]
    stores[0].start()
    hdim = 128
    scaling = hdim ** (-0.5)
    count = half // TILE
    for qi in range(count):
        base = block_base(qi, shift, count)
        span = pl.ds(base, TILE)
        place = order_of(base, (TILE, 1), 0, shift, half)
        first, inv_length = query_terms(place, bound, half)
        query = y_ref[span, 256:384]
        attention = 0.0
        for ki in needed_keys(qi, count):
            key_base = block_base(ki, shift, count)
            keys = pl.ds(key_base, TILE)
            scores = nt_dot(query, y_ref[keys, 384:512]) * scaling
            at = order_of(key_base, (1, TILE), 1, shift, half)
            allowed = (at <= place) & (at >= first)
            weights = jnp.where(
                allowed, scores * jax.nn.sigmoid(scores) * inv_length, 0.0
            ).astype(BF16)
            attention += nn_dot(weights, y_ref[keys, 128:256])

        att_ref[span, :] = attention
        stores.append(
            pltpu.make_async_copy(att_ref.at[span], att_hbm.at[span], att_sems.at[qi])
        )
        stores[-1].start()
        gated = y_ref[span, 0:128].astype(F32)
        center = jnp.mean(attention, axis=1, keepdims=True)
        shifted = attention - center
        columns = [
            center,
            jnp.sum(shifted * shifted, axis=1, keepdims=True),
            jnp.sum(gated, axis=1, keepdims=True),
            jnp.sum(gated * shifted, axis=1, keepdims=True),
        ]
        lane = iota((TILE, 128), 1)
        table = jnp.zeros((TILE, 128), F32)
        for i, column in enumerate(columns):
            table = jnp.where(lane == i, column, table)
        turned = table.T[0:4]
        for h in range(heads):
            stats_ref[h, :, span] = turned
    for store in stores:
        store.wait()


def backward_kernel(
    facts, y_hbm, att_hbm, stats_ref, mine_ref, send_ref, y_ref, att_ref, attn, grad, dq, dk, dv, sems
):
    core, shift, bound = facts[0], facts[1], facts[2]
    rows_in = [
        pltpu.make_async_copy(att_hbm, att_ref, sems.at[0]),
        pltpu.make_async_copy(y_hbm, y_ref, sems.at[1]),
    ]
    for load in rows_in:
        load.start()
    half = y_ref.shape[0]
    heads = stats_ref.shape[0]
    quarter, rows = mine_ref.shape[0], mine_ref.shape[1]
    hdim = 128
    width = heads * hdim
    count = half // TILE
    stat = [[stats_ref[h, i : i + 1, :] for i in range(4)] for h in range(heads)]
    mean = sum(s[0] for s in stat) / heads
    variance, mean_grad, mean_prod = 0.0, 0.0, 0.0
    for center, spread, grad_sum, prod_sum in stat:
        offset = center - mean
        variance += spread + hdim * offset * offset
        mean_grad += grad_sum
        mean_prod += prod_sum + offset * grad_sum
    inv_attn = lax.rsqrt(variance / width + EPSILON)
    line = iota((128, half), 0)
    table = jnp.where(
        line == 0,
        mean,
        jnp.where(
            line == 1,
            inv_attn,
            jnp.where(line == 2, mean_grad / width, inv_attn * mean_prod / width),
        ),
    )
    columns = table.T
    for load in rows_in:
        load.wait()
    for qi in range(count):
        span = slice(qi * TILE, (qi + 1) * TILE)
        inv = columns[span, 1:2]
        attn_norm = (att_ref[span, :] - columns[span, 0:1]) * inv
        gated = y_ref[span, 0:128].astype(F32)
        attn[span, :] = attn_norm.astype(BF16)
        grad[span, :] = (
            inv * (gated - columns[span, 2:3] - attn_norm * columns[span, 3:4])
        ).astype(BF16)
    dq[...] = jnp.zeros_like(dq)
    scaling = hdim ** (-0.5)
    for ki in range(count):
        key_base = block_base(ki, shift, count)
        keys = pl.ds(key_base, TILE)
        at = order_of(key_base, (TILE, 1), 0, shift, half)
        key, value = y_ref[keys, 384:512], y_ref[keys, 128:256]
        grad_key, grad_value = 0.0, 0.0
        for qi in range(count):
            if ki not in needed_keys(qi, count):
                continue
            base = block_base(qi, shift, count)
            span = pl.ds(base, TILE)
            place = order_of(base, (1, TILE), 1, shift, half)
            first, inv_length = query_terms(place, bound, half)
            query, grad_out = y_ref[span, 256:384], grad[span, :]
            scores = nt_dot(key, query) * scaling
            allowed = (at <= place) & (at >= first)
            sig = jax.nn.sigmoid(scores)
            product = scores * sig
            weights = jnp.where(allowed, product * inv_length, 0.0).astype(BF16)
            slope = (sig + product * (1.0 - sig)) * (inv_length * scaling)
            grad_weights = nt_dot(value, grad_out)
            grad_scores = jnp.where(allowed, grad_weights * slope, 0.0).astype(BF16)
            grad_value += nn_dot(weights, grad_out)
            grad_key += nn_dot(grad_scores, query)
            dq[span, :] += tn_dot(grad_scores, key)
        dk[keys, :] = grad_key.astype(BF16)
        dv[keys, :] = grad_value.astype(BF16)

    for s in range(quarter):
        near = pl.ds(pl.multiple_of((2 * s + core) * rows, rows), rows)
        far = pl.ds(pl.multiple_of((2 * s + 1 - core) * rows, rows), rows)
        for i, ref in enumerate((attn, dv, dq, dk)):
            columns = slice(i * hdim, (i + 1) * hdim)
            mine_ref[s, :, columns] = ref[near, :].astype(BF16)
            send_ref[s, :, columns] = ref[far, :].astype(BF16)


def finish_kernel(
    back_ref, proj_ref, mixed_ref, gate_ref, slot_ref, embed_ref, cot_ref, weight_hbm, out_ref, gated_ref, weight_ref, sems
):
    heads = back_ref.shape[0]
    width = embed_ref.shape[1]
    loads = copies(weight_hbm, weight_ref, sems, column_spans(4 * width, width))
    total = 0.0
    for t in range(4):
        loads[t].wait()
        for pair in range(heads // 2):
            columns = slice(pair * 256, (pair + 1) * 256)
            lanes = slice(t * 128, (t + 1) * 128)
            base = t * width + pair * 256
            grad_act = jnp.concatenate(
                [back_ref[2 * pair, :, lanes], back_ref[2 * pair + 1, :, lanes]], axis=1
            ).astype(F32)
            if t == 0:
                gated_ref[:, columns] = (grad_act * gate_ref[:, columns].astype(F32)).astype(BF16)
                grad_act = grad_act * mixed_ref[:, columns]
            projected = proj_ref[:, base : base + 256]
            sig = jax.nn.sigmoid(projected)
            slope = sig * (1.0 + projected * (1.0 - sig))
            total += nt_dot((grad_act * slope).astype(BF16), weight_ref[:, base : base + 256])
    normed, inv_embed = normalize(embed_ref[...])
    grad_embed = cot_ref[...].astype(F32) + normalize_back(total, normed, inv_embed)
    slots, rows = out_ref.shape[0], slot_ref.shape[1]
    place = jnp.where(slot_ref[...] == iota((slots, rows), 0), 1.0, 0.0).astype(BF16)
    out_ref[...] = nn_dot(place, grad_embed.astype(BF16)).astype(BF16)


def table_kernel(incoming_ref, arrived_ref, scale_ref, out_ref, buffer, sems):
    slots = arrived_ref.shape[0]
    steps = sems.shape[0]
    block = buffer.shape[0] // steps
    copies = []
    for n in range(steps):
        span = pl.ds(n * block, block)
        chosen = incoming_ref[...] - 1 - n * block == iota((block, slots), 0)
        total = nn_dot(jnp.where(chosen, 1.0, 0.0).astype(BF16), arrived_ref[...])
        scale = jnp.broadcast_to(scale_ref[:, span], (128, block)).T
        buffer[span, :] = total * scale[:, 0:1]
        copies.append(pltpu.make_async_copy(buffer.at[span], out_ref.at[span], sems.at[n]))
        copies[-1].start()
    for copy in copies:
        copy.wait()


def per_device(
    table_rows,
    row_scales,
    owners,
    shard_rows,
    history_lengths,
    input_weight,
    output_weight,
    cotangent,
):
    rows = owners.shape[0]
    table_size, width = table_rows.shape
    heads = HEADS
    hdim = width // heads
    devices = lax.axis_size(("dp", "cp"))
    n_cp = lax.axis_size("cp")
    cores = n_cp // heads
    half = rows * n_cp // 2
    quarter = heads // 2
    slots = devices * CAPACITY
    groups = [[i * cores + c for i in range(heads)] for c in range(cores)]
    swap = [(i, i ^ 1) for i in range(n_cp)]
    core = (lax.axis_index("cp") % cores).reshape(1)
    everyone = ("dp", "cp")
    shape = jax.ShapeDtypeStruct
    smem = pl.BlockSpec(memory_space=pltpu.SMEM)
    vmem = pl.BlockSpec(memory_space=pltpu.VMEM)
    hbm = pl.BlockSpec(memory_space=pltpu.HBM)

    def kernel(body, name, ins, outs, out_shape, mib, scratch=()):
        return pl.pallas_call(
            body,
            in_specs=ins,
            out_specs=outs,
            out_shape=out_shape,
            scratch_shapes=list(scratch),
            compiler_params=pltpu.CompilerParams(vmem_limit_bytes=mib << 20 if mib else None),
            name=name,
        )

    def exchange(values, axes, **options):
        return lax.all_to_all(values, axes, split_axis=0, concat_axis=0, tiled=True, **options)

    def to_heads(values):
        return exchange(values, "cp", axis_index_groups=groups)

    def to_all(values):
        lanes = values.shape[1]
        return exchange(values.reshape(devices, CAPACITY, lanes), everyone).reshape(slots, lanes)

    dma = pltpu.SemaphoreType.DMA

    def far(values):
        return pltpu.with_memory_space_constraint(values, pltpu.HBM)

    weight_far = far(input_weight)
    scale_line = row_scales.reshape(1, table_size)
    requests, slot_line, facts = kernel(
        request_kernel,
        "request",
        [smem, smem, vmem, vmem],
        (vmem, vmem, smem),
        (shape((devices, 128), I32), shape((1, rows), I32), shape((4,), I32)),
        0,
    )(core, history_lengths, owners.reshape(1, rows), shard_rows.reshape(1, rows))
    incoming = exchange(requests.reshape(devices, 1, 128), everyone).reshape(devices, 128)

    wide = width + 128
    fetched = kernel(
        fetch_kernel,
        "fetch",
        [vmem, hbm, vmem],
        vmem,
        shape((slots, wide), BF16),
        16,
        (pltpu.VMEM((table_size, width), BF16), dma((width // 512,))),
    )(incoming, far(table_rows), scale_line)
    returned = to_all(fetched)

    grad_mixed = jnp.einsum("rk,dk->rd", cotangent, output_weight, preferred_element_type=F32)

    near_weight = (pltpu.VMEM((width, 4 * width), BF16), dma((4,)))
    packed, projected, embedded, gate = kernel(
        project_kernel,
        "project",
        [vmem] * 3 + [hbm],
        (vmem, vmem, vmem, vmem),
        (
            shape((heads, rows, 4 * hdim), BF16),
            shape((rows, 4 * width), F32),
            shape((rows, width), F32),
            shape((rows, width), BF16),
        ),
        24,
        near_weight,
    )(returned, slot_line, grad_mixed, weight_far)

    branches = to_heads(packed)
    received = lax.ppermute(branches, "cp", swap)
    ordered, attention, stats = kernel(
        attend_kernel,
        "attend",
        [smem, vmem, vmem],
        (hbm, hbm, vmem),
        (
            pltpu.HBM((half, 4 * hdim), BF16),
            pltpu.HBM((half, hdim), F32),
            shape((heads, 4, half), F32),
        ),
        16,
        (
            pltpu.VMEM((half, 4 * hdim), BF16),
            pltpu.VMEM((half, hdim), F32),
            dma(()),
            dma((half // TILE,)),
        ),
    )(facts, branches, received)
    stats = to_heads(stats)

    backed = shape((quarter, rows, 4 * hdim), BF16)
    near = pltpu.VMEM((half, hdim), BF16)
    mine, send = kernel(
        backward_kernel,
        "backward",
        [smem, hbm, hbm, vmem],
        (vmem, vmem),
        (backed, backed),
        24,
        (pltpu.VMEM((half, 4 * hdim), BF16), pltpu.VMEM((half, hdim), F32))
        + (near, near, pltpu.VMEM((half, hdim), F32), near, near, dma((2,))),
    )(facts, far(ordered), far(attention), stats)
    received = lax.ppermute(send, "cp", swap)
    joined = kernel(
        join_kernel,
        "join",
        [smem, vmem, vmem],
        vmem,
        shape((heads, rows, 4 * hdim), BF16),
        8,
    )(facts, mine, received)
    back = to_heads(joined)

    outgoing, mixed = kernel(
        finish_kernel,
        "finish",
        [vmem] * 7 + [hbm],
        (vmem, vmem),
        (shape((slots, width), BF16), shape((rows, width), BF16)),
        24,
        near_weight,
    )(back, projected, grad_mixed, gate, slot_line, embedded, cotangent, weight_far)
    arrived = to_all(outgoing)
    layer_out = (
        embedded + jnp.dot(mixed, output_weight, preferred_element_type=F32)
    ).astype(BF16)

    table_grad = kernel(
        table_kernel,
        "table",
        [vmem] * 3,
        hbm,
        shape((table_size, width), F32),
        24,
        (pltpu.VMEM((table_size, width), F32), pltpu.SemaphoreType.DMA((16,))),
    )(incoming[:, :CAPACITY].reshape(1, slots), arrived, scale_line)
    return (layer_out, table_grad)


def solution(mesh):
    return jax.shard_map(
        per_device,
        mesh=mesh,
        in_specs=(
            P(("dp", "cp"), None),
            P(("dp", "cp")),
            P(("dp", "cp"), None),
            P(("dp", "cp")),
            P("dp", None),
            P(),
            P(),
            P(("dp", "cp"), None),
        ),
        out_specs=(P(("dp", "cp"), None), P(("dp", "cp"), None)),
        check_vma=False,
    )
```

time: 179 us -> 150 us (0.84)
  Pallas kernels: 47.8 us -> 29.8 us
  blocking collectives: 75.1 us -> 66.6 us
  local copies, waits for them, and re-layouts: 8.4 us -> 5.77 us
  matrix products: 3.89 us -> 1.98 us
  starting transfers between devices: 13.5 us -> 15.3 us
    pallas_call x9 -> x8, Pallas kernels: 47.8 us -> 29.8 us  [the longest x1 7.31 us: per_device(): kernel(backward_kernel, 'backward', [smem, hbm, hbm, vmem], (vmem, vmem),...]
    all_to_all x4, blocking collectives: 75.1 us -> 66.6 us  [exchange(): lax.all_to_all(values, axes, split_axis=0, concat_axis=0, tiled=True, **o...]
    reshape x2, local copies, waits for them, and re-layouts: 4.75 us -> 2.03 us  [to_all(): values.reshape(devices, CAPACITY, lanes)]
    ppermute x0 -> x1, starting transfers between devices: none -> 2.41 us  [per_device(): received = lax.ppermute(branches, 'cp', swap)]
    ppermute x2 -> x1, starting transfers between devices: 4.12 us -> 1.72 us  [per_device(): received = lax.ppermute(send, 'cp', swap)]
    ppermute x0 -> x1, waiting for transfers between devices: none -> 2.29 us  [per_device(): received = lax.ppermute(branches, 'cp', swap)]
    ppermute x2 -> x1, waiting for transfers between devices: 3.68 us -> 1.54 us  [per_device(): received = lax.ppermute(send, 'cp', swap)]
  transfers between devices with their start and end apart: 4 -> 4, of which waited for: 4 -> 4; matrix products, arithmetic and copies ran while one was open for 2% -> 1% of each run, Pallas kernels for 0% -> 0%
where the time goes in v3:
time: 150 us
  blocking collectives  66.6 us (44%)
  Pallas kernels  29.8 us (20%)
  waiting for transfers between devices  29.4 us (20%)
  starting transfers between devices  15.3 us (10%)
  local copies, waits for them, and re-layouts  5.77 us (4%)
  matrix products  1.98 us (1%)
    all_to_all x4, blocking collectives, exchange(): lax.all_to_all(values, axes, split_axis=0, concat_axis=0, tiled=True, **o...  66.6 us
    all_to_all x2, waiting for transfers between devices, exchange(): lax.all_to_all(values, axes, split_axis=0, concat_axis=0, tiled=True, **o...  25.6 us
    all_to_all x2, starting transfers between devices, exchange(): lax.all_to_all(values, axes, split_axis=0, concat_axis=0, tiled=True, **o...  11.1 us
    pallas_call x1, Pallas kernels, per_device(): kernel(backward_kernel, 'backward', [smem, hbm, hbm, vmem], (vmem, vmem),...  7.31 us
    pallas_call x1, Pallas kernels, per_device(): kernel(finish_kernel, 'finish', [vmem] * 7 + [hbm], (vmem, vmem), (shape(...  5.1 us
    pallas_call x1, Pallas kernels, per_device(): kernel(project_kernel, 'project', [vmem] * 3 + [hbm], (vmem, vmem, vmem,...  4.53 us
    pallas_call x1, Pallas kernels, per_device(): kernel(table_kernel, 'table', [vmem] * 3, hbm, shape((table_size, width),...  3.67 us
    pallas_call x1, Pallas kernels, per_device(): kernel(attend_kernel, 'attend', [smem, vmem, vmem], (hbm, hbm, vmem), (pl...  3.61 us
  transfers between devices with their start and end apart: 4, of which 4 were waited for; matrix products, arithmetic and copies ran while one was open for 1% of the time, Pallas kernels for 0%

profile of v3, /device:TPU:1, one launch (start us, length us, event | category | flops | bytes accessed | tf_op | source)
XLA Modules:
  0.0 149.8 jit_solution(5626166378346109636)
XLA Ops:
  0.6 0.0 copy-start
  0.7 1.7 %request.1 = (s32[128,128]{1,0:T(8,128)}, s32[1,128]{1,0:T(1,128)}, s32[4]{0:T(128)}) custom-call(s32[1]{0:T(128)} %bitcast.core_ref, s32[1,3]{1,0:T(1,128)} %lengths_ref.1, s32[1,128]{1,0:T(1,128)} %bitcast.18, s32[1,128]{1,0:T(1,128)} %bitcast.19), custom_call_target="tpu_custom_call" | custom-call | tf_op jit(solution)/shard_map/request/pallas_call | solution.py:437
  2.4 20.9 %all_to_all.30 = s32[128,1,128]{2,1,0:T(1,128)S(1)} all-to-all(s32[128,1,128]{2,1,0:T(1,128)} %bitcast.17), channel_id=1, replica_groups=mesh['dp'=8,'cp'=16] {'dp','cp'}, dimensions={0} | all-to-all | bytes 131072 | tf_op jit(solution)/shard_map/all_to_all | solution.py:421
  23.3 0.7 copy-done.6
  24.0 3.0 %fetch.1 = bf16[256,1152]{1,0:T(8,128)(2,1)S(1)} custom-call(s32[128,128]{1,0:T(8,128)S(1)} %bitcast.13, bf16[2048,1024]{1,0:T(8,128)(2,1)} %table_hbm.1, f32[1,2048]{1,0:T(1,128)S(1)} %bitcast.15), custom_call_target="tpu_custom_call" | custom-call | tf_op jit(solution)/shard_map/fetch/pallas_call | solution.py:448
  27.0 0.0 copy-start.3
  27.0 1.0 reshape.43
  28.1 5.5 %all-to-all-start.1 = ((bf16[128,2,1152]{2,1,0:T(2,128)(2,1)}), bf16[128,2,1152]{2,1,0:T(2,128)(2,1)}, u32[]{:S(2)}, u32[]{:S(2)}) async-start(bf16[128,2,1152]{2,1,0:T(2,128)(2,1)} %reshape.43), calls=%async_computation.1 | async-start | bytes 1179648 | tf_op jit(solution)/shard_map/all_to_all | solution.py:421
  33.6 0.8 fusion.1.mixed_ref
  34.4 13.2 %all-to-all-done.1 = bf16[128,2,1152]{2,1,0:T(2,128)(2,1)} async-done(((bf16[128,2,1152]{2,1,0:T(2,128)(2,1)}), bf16[128,2,1152]{2,1,0:T(2,128)(2,1)}, u32[]{:S(2)}, u32[]{:S(2)}) %all-to-all-start.1) | async-done | bytes 589856 | tf_op jit(solution)/shard_map/all_to_all | solution.py:421
  47.7 2.0 %reshape.44.returned_ref = bf16[256,1152]{1,0:T(8,128)(2,1)S(1)} reshape(bf16[128,2,1152]{2,1,0:T(2,128)(2,1)} %all-to-all-done.1) | data formatting | bytes 1179648 | tf_op jit(solution)/shard_map/reshape | solution.py:428
  49.7 4.5 %project.1 = (bf16[8,128,512]{2,1,0:T(8,128)(2,1)S(1)}, f32[128,4096]{1,0:T(8,128)S(1)}, f32[128,1024]{1,0:T(8,128)S(1)}, bf16[128,1024]{1,0:T(8,128)(2,1)S(1)}) custom-call(bf16[256,1152]{1,0:T(8,128)(2,1)S(1)} %reshape.44.returned_ref, s32[1,128]{1,0:T(1,128)S(1)} %copy-done.9, f32[128,1024]{1,0:T(8,128)S(1)} %fusion.1.mixed_ref, bf16[1024,4096]{1,0:T(8,128)(2,1)} %weight_hbm.3), custom_call_target="tpu_custom_call" | custom-call | tf_op jit(solution)/shard_map/project/pallas_call | solution.py:462
  54.2 18.1 %all_to_all.31.x_ref = bf16[8,128,512]{2,1,0:T(8,128)(2,1)S(1)} all-to-all(bf16[8,128,512]{2,1,0:T(8,128)(2,1)S(1)} %get-tuple-element.20), channel_id=1, replica_groups={{0,2,4,6,8,10,12,14},{1,3,5,7,9,11,13,15},{16,18,20,22,24,26,28,30},{17..., dimensions={0} | all-to-all | bytes 2097152 | tf_op jit(solution)/shard_map/all_to_all | solution.py:421
  72.3 2.4 %collective-permute-start = (bf16[8,128,512]{2,1,0:T(8,128)(2,1)S(1)}, bf16[8,128,512]{2,1,0:T(8,128)(2,1)S(1)}, u32[]{:S(2)}, u32[]{:S(2)}) collective-permute-start(bf16[8,128,512]{2,1,0:T(8,128)(2,1)S(1)} %all_to_all.31.x_ref), channel_id=1, source_target_pairs={{0,1},{1,0},{2,3},{3,2},{4,5},{5,4},{6,7},{7,6},{8,9},{9,8},{10,11... | collective-permute-start | bytes 3145736 | tf_op jit(solution)/shard_map/ppermute | solution.py:478
  74.7 2.3 %collective-permute-done.received_ref = bf16[8,128,512]{2,1,0:T(8,128)(2,1)S(1)} collective-permute-done((bf16[8,128,512]{2,1,0:T(8,128)(2,1)S(1)}, bf16[8,128,512]{2,1,0:T(8,128)(2,1)S(1)}, u32[]{:S(2)}, u32[]{:S(2)}) %collective-permute-start) | collective-permute-done | bytes 1048608 | tf_op jit(solution)/shard_map/ppermute | solution.py:478
  77.0 3.6 %attend.1 = (bf16[1024,512]{1,0:T(8,128)(2,1)}, f32[1024,128]{1,0:T(8,128)}, f32[8,4,1024]{2,1,0:T(4,128)S(1)}) custom-call(s32[4]{0:T(128)S(1)} %copy-done.8, bf16[8,128,512]{2,1,0:T(8,128)(2,1)S(1)} %all_to_all.31.x_ref, bf16[8,128,512]{2,1,0:T(8,128)(2,1)S(1)} %collective-permute-done.received_ref), custom_call_target="tpu_custom_call" | custom-call | tf_op jit(solution)/shard_map/attend/pallas_call | solution.py:479
  80.6 9.6 %all_to_all.32.stats_ref = f32[8,4,1024]{2,1,0:T(4,128)S(1)} all-to-all(f32[8,4,1024]{2,1,0:T(4,128)S(1)} %get-tuple-element.23), channel_id=1, replica_groups={{0,2,4,6,8,10,12,14},{1,3,5,7,9,11,13,15},{16,18,20,22,24,26,28,30},{17..., dimensions={0} | all-to-all | bytes 262144 | tf_op jit(solution)/shard_map/all_to_all | solution.py:421
  90.2 7.3 %backward.1 = (bf16[4,128,512]{2,1,0:T(8,128)(2,1)S(1)}, bf16[4,128,512]{2,1,0:T(8,128)(2,1)S(1)}) custom-call(s32[4]{0:T(128)S(1)} %copy-done.8, bf16[1024,512]{1,0:T(8,128)(2,1)} %get-tuple-element.21.y_hbm, f32[1024,128]{1,0:T(8,128)} %get-tuple-element.22.att_hbm, f32[8,4,1024]{2,1,0:T(4,128)S(1)} %all_to_all.32.stats_ref), custom_call_target="tpu_custom_call" | custom-call | tf_op jit(solution)/shard_map/backward/pallas_call | solution.py:501
  97.5 1.7 %collective-permute-start.1 = (bf16[4,128,512]{2,1,0:T(8,128)(2,1)S(1)}, bf16[4,128,512]{2,1,0:T(8,128)(2,1)S(1)}, u32[]{:S(2)}, u32[]{:S(2)}) collective-permute-start(bf16[4,128,512]{2,1,0:T(8,128)(2,1)S(1)} %get-tuple-element.25), channel_id=1, source_target_pairs={{0,1},{1,0},{2,3},{3,2},{4,5},{5,4},{6,7},{7,6},{8,9},{9,8},{10,11... | collective-permute-start | bytes 1572872 | tf_op jit(solution)/shard_map/ppermute | solution.py:511
  99.3 1.5 %collective-permute-done.1.received_ref = bf16[4,128,512]{2,1,0:T(8,128)(2,1)S(1)} collective-permute-done((bf16[4,128,512]{2,1,0:T(8,128)(2,1)S(1)}, bf16[4,128,512]{2,1,0:T(8,128)(2,1)S(1)}, u32[]{:S(2)}, u32[]{:S(2)}) %collective-permute-start.1) | collective-permute-done | bytes 524320 | tf_op jit(solution)/shard_map/ppermute | solution.py:511
  100.8 0.8 join.1
  101.6 18.0 %all_to_all.33.back_ref = bf16[8,128,512]{2,1,0:T(8,128)(2,1)S(1)} all-to-all(bf16[8,128,512]{2,1,0:T(8,128)(2,1)S(1)} %join.1), channel_id=1, replica_groups={{0,2,4,6,8,10,12,14},{1,3,5,7,9,11,13,15},{16,18,20,22,24,26,28,30},{17..., dimensions={0} | all-to-all | bytes 2097152 | tf_op jit(solution)/shard_map/all_to_all | solution.py:421
  119.7 5.1 %finish.1 = (bf16[256,1024]{1,0:T(8,128)(2,1)S(1)}, bf16[128,1024]{1,0:T(8,128)(2,1)S(1)}) custom-call(bf16[8,128,512]{2,1,0:T(8,128)(2,1)S(1)} %all_to_all.33.back_ref, f32[128,4096]{1,0:T(8,128)S(1)} %get-tuple-element.26.proj_ref, f32[128,1024]{1,0:T(8,128)S(1)} %fusion.1.mixed_ref, bf16[128,1024]{1,0:T(8,128)(2,1)S(1)} %get-tuple-element.27.gate_ref, ...), custom_call_target="tpu_custom_call" | custom-call | tf_op jit(solution)/shard_map/finish/pallas_call | solution.py:522
  124.8 0.0 copy-start.4
  124.8 0.7 copy-done.4
  125.5 1.0 reshape.46
  126.5 5.6 %all-to-all-start.5 = ((bf16[128,2,1024]{2,1,0:T(2,128)(2,1)}), bf16[128,2,1024]{2,1,0:T(2,128)(2,1)S(1)}, u32[]{:S(2)}, u32[]{:S(2)}) async-start(bf16[128,2,1024]{2,1,0:T(2,128)(2,1)} %reshape.46), calls=%async_computation.5 | async-start | bytes 1048576 | tf_op jit(solution)/shard_map/all_to_all | solution.py:421
  132.1 0.1 reshape.45.incoming_ref
  132.3 1.2 fusion
  133.4 12.4 %all-to-all-done.5 = bf16[128,2,1024]{2,1,0:T(2,128)(2,1)S(1)} async-done(((bf16[128,2,1024]{2,1,0:T(2,128)(2,1)}), bf16[128,2,1024]{2,1,0:T(2,128)(2,1)S(1)}, u32[]{:S(2)}, u32[]{:S(2)}) %all-to-all-start.5) | async-done | bytes 524320 | tf_op jit(solution)/shard_map/all_to_all | solution.py:421
  145.8 0.2 reshape.47.arrived_ref
  146.0 3.7 %table.1 = f32[2048,1024]{1,0:T(8,128)} custom-call(s32[1,256]{1,0:T(1,128)S(1)} %reshape.45.incoming_ref, bf16[256,1024]{1,0:T(8,128)(2,1)S(1)} %reshape.47.arrived_ref, f32[1,2048]{1,0:T(1,128)S(1)} %bitcast.16), custom_call_target="tpu_custom_call" | custom-call | tf_op jit(solution)/shard_map/table/pallas_call | solution.py:536
  (15 shorter events, 0.0 us)
Async XLA Ops:
  0.6 33.0 %copy-start = (bf16[1024,1024]{1,0:T(8,128)(2,1)S(1)}, bf16[1024,1024]{1,0:T(8,128)(2,1)}, u32[]{:S(2)}) copy-start(bf16[1024,1024]{1,0:T(8,128)(2,1)} %param.14) | copy-start | bytes 6291460
  23.3 0.7 copy-start.6
  27.0 6.6 %copy-start.3 = (bf16[128,1024]{1,0:T(8,128)(2,1)S(1)}, bf16[128,1024]{1,0:T(8,128)(2,1)}, u32[]{:S(2)}) copy-start(bf16[128,1024]{1,0:T(8,128)(2,1)} %cot_ref.1) | copy-start | bytes 786436
  28.1 19.6 %all-to-all-start.1 = ((bf16[128,2,1152]{2,1,0:T(2,128)(2,1)}), bf16[128,2,1152]{2,1,0:T(2,128)(2,1)}, u32[]{:S(2)}, u32[]{:S(2)}) async-start(bf16[128,2,1152]{2,1,0:T(2,128)(2,1)} %reshape.43), calls=%async_computation.1 | async-start | bytes 1179648 | tf_op jit(solution)/shard_map/all_to_all | solution.py:421
  33.6 16.1 %copy-start.9 = (s32[1,128]{1,0:T(1,128)S(1)}, s32[1,128]{1,0:T(1,128)}, u32[]{:S(2)}) copy-start(s32[1,128]{1,0:T(1,128)} %get-tuple-element.17.slot_ref) | copy-start | bytes 1540
  54.2 65.5 %copy-start.1 = (f32[128,1024]{1,0:T(8,128)}, f32[128,1024]{1,0:T(8,128)S(1)}, u32[]{:S(2)}) copy-start(f32[128,1024]{1,0:T(8,128)S(1)} %get-tuple-element.18.embed_ref) | copy-start | bytes 1572868
  54.2 22.8 %copy-start.8 = (s32[4]{0:T(128)S(1)}, s32[4]{0:T(128)}, u32[]{:S(2)}) copy-start(s32[4]{0:T(128)} %get-tuple-element.19.facts) | copy-start | bytes 52
  72.3 4.7 %collective-permute-start = (bf16[8,128,512]{2,1,0:T(8,128)(2,1)S(1)}, bf16[8,128,512]{2,1,0:T(8,128)(2,1)S(1)}, u32[]{:S(2)}, u32[]{:S(2)}) collective-permute-start(bf16[8,128,512]{2,1,0:T(8,128)(2,1)S(1)} %all_to_all.31.x_ref), channel_id=1, source_target_pairs={{0,1},{1,0},{2,3},{3,2},{4,5},{5,4},{6,7},{7,6},{8,9},{9,8},{10,11... | collective-permute-start | bytes 3145736 | tf_op jit(solution)/shard_map/ppermute | solution.py:478
  97.5 3.3 %collective-permute-start.1 = (bf16[4,128,512]{2,1,0:T(8,128)(2,1)S(1)}, bf16[4,128,512]{2,1,0:T(8,128)(2,1)S(1)}, u32[]{:S(2)}, u32[]{:S(2)}) collective-permute-start(bf16[4,128,512]{2,1,0:T(8,128)(2,1)S(1)} %get-tuple-element.25), channel_id=1, source_target_pairs={{0,1},{1,0},{2,3},{3,2},{4,5},{5,4},{6,7},{7,6},{8,9},{9,8},{10,11... | collective-permute-start | bytes 1572872 | tf_op jit(solution)/shard_map/ppermute | solution.py:511
  124.8 0.7 copy-start.4
  125.5 6.8 %copy-start.2 = (f32[128,1024]{1,0:T(8,128)S(1)}, f32[128,1024]{1,0:T(8,128)}, u32[]{:S(2)}) copy-start(f32[128,1024]{1,0:T(8,128)} %copy-done.1) | copy-start | bytes 1572868
  125.5 6.8 %copy-start.5 = (bf16[128,1024]{1,0:T(8,128)(2,1)S(1)}, bf16[128,1024]{1,0:T(8,128)(2,1)}, u32[]{:S(2)}) copy-start(bf16[128,1024]{1,0:T(8,128)(2,1)} %copy-done.4) | copy-start | bytes 786436
  126.5 19.3 %all-to-all-start.5 = ((bf16[128,2,1024]{2,1,0:T(2,128)(2,1)}), bf16[128,2,1024]{2,1,0:T(2,128)(2,1)S(1)}, u32[]{:S(2)}, u32[]{:S(2)}) async-start(bf16[128,2,1024]{2,1,0:T(2,128)(2,1)} %reshape.46), calls=%async_computation.5 | async-start | bytes 1048576 | tf_op jit(solution)/shard_map/all_to_all | solution.py:421
  132.3 13.7 %copy-start.7 = (f32[2048]{0:T(1024)S(1)}, f32[2048]{0:T(1024)}, u32[]{:S(2)}) copy-start(f32[2048]{0:T(1024)} %param.9) | copy-start | bytes 24580

commit v4 on v3

--- a/solution.py
+++ b/solution.py
@@ -40,6 +40,11 @@
 
 def iota(shape, axis):
     return lax.broadcasted_iota(I32, shape, axis)
+
+
+def silu_parts(half_value):
+    twice = 1.0 + jnp.tanh(half_value)
+    return twice, half_value * twice
 
 
 def normalize(values):
@@ -92,7 +97,9 @@
     return high, middle, rest - middle
 
 
-def fetch_kernel(incoming_ref, table_hbm, scale_ref, out_ref, table_ref, sems):
+def fetch_kernel(incoming_ref, table_hbm, scale_hbm, out_ref, table_ref, scale_ref, sems, scale_sem):
+    scale_load = pltpu.make_async_copy(scale_hbm, scale_ref, scale_sem)
+    scale_load.start()
     loads = copies(table_hbm, table_ref, sems, column_spans(table_ref.shape[1], 512))
     slots, size, width = out_ref.shape[0], table_ref.shape[0], table_ref.shape[1]
     devices = slots // CAPACITY
@@ -105,6 +112,7 @@
     row = jnp.sum(jnp.where(mine, high * 16.0 + low, 0.0), axis=1, keepdims=True)
     chosen = row.astype(I32) - 1 == iota((slots, size), 1)
     hot = jnp.where(chosen, 1.0, 0.0).astype(BF16)
+    scale_load.wait()
     scale = jnp.sum(jnp.where(chosen, scale_ref[...], 0.0), axis=1, keepdims=True)
     high, middle, low = split_scale(scale)
     lane = iota((slots, 128), 1)
@@ -115,6 +123,14 @@
     for n, base in enumerate(range(0, width, 512)):
         loads[n].wait()
         out_ref[:, base : base + 512] = nn_dot(hot, table_ref[:, base : base + 512]).astype(BF16)
+
+
+def mix_kernel(cot_ref, weight_ref, out_ref):
+    out_ref[...] = nt_dot(cot_ref[...], weight_ref[...])
+
+
+def output_kernel(embed_ref, mixed_ref, weight_ref, out_ref):
+    out_ref[...] = (embed_ref[...] + nn_dot(mixed_ref[...], weight_ref[...])).astype(BF16)
 
 
 def project_kernel(
@@ -139,7 +155,7 @@
             base = t * width + pair * 256
             projected = nn_dot(normed, weight_ref[:, base : base + 256])
             proj_ref[:, base : base + 256] = projected
-            active = (projected * jax.nn.sigmoid(projected)).astype(BF16)
+            active = silu_parts(0.5 * projected)[1].astype(BF16)
             if t == 0:
                 gate_ref[:, columns] = active
                 active = (active.astype(F32) * mixed_ref[:, columns]).astype(BF16)
@@ -167,99 +183,74 @@
         out_ref[s + quarter] = choose(upper, received_ref[s], mine_ref[s])
 
 
-def needed_keys(block, count):
-    return list(range(count)) if block == 0 else list(range(block + 1))
-
-
-def block_base(block, shift, count):
-    return pl.multiple_of(((shift // TILE + block) & (count - 1)) * TILE, TILE)
-
-
-def order_of(base, shape, axis, shift, half):
-    return (base + iota(shape, axis) - shift) & (half - 1)
-
-
-def query_terms(place, bound, half):
+def rows_of(facts, s, side, rows, half):
+    start = ((s - facts[1] // TILE) & (half // TILE - 1)) * TILE + side * rows
+    return pl.ds(pl.multiple_of(start, rows), rows)
+
+
+def share_of(facts, query_base, keys, half):
+    seam, bound = facts[1] & (TILE - 1), facts[2]
+    place = (query_base + iota((1, TILE), 1) - seam) & (half - 1)
     later = place >= bound
-    length = jnp.where(later, half - bound, bound).astype(F32)
-    return jnp.where(later, bound, 0), 1.0 / length
-
-
-def attend_kernel(facts, x_ref, received_ref, y_hbm, att_hbm, stats_ref, y_ref, att_ref, y_sem, att_sems):
-    core, shift, bound = facts[0], facts[1], facts[2]
-    half = y_ref.shape[0]
-    heads, rows, lanes = received_ref.shape
+    first = jnp.where(later, bound, 0)
+    inv_length = 1.0 / jnp.where(later, half - bound, bound).astype(F32)
+    at = (iota((keys, 1), 0) - seam) & (half - 1)
+    return jnp.where((at <= place) & (at >= first), inv_length, 0.0)
+
+
+def blocks_of(half):
+    for base in range(0, half, TILE):
+        yield base, (half if base == 0 else base + TILE)
+
+
+def attend_kernel(
+    facts, x_ref, received_ref, y_ref, att_ref, grad_ref, stats_ref, turned
+):
+    core = facts[0]
+    half, lanes = y_ref.shape
+    heads, rows = received_ref.shape[0], received_ref.shape[1]
     quarter = heads // 2
+    hdim = att_ref.shape[0]
     for s in range(quarter):
         for ref, side in ((x_ref, core), (received_ref, 1 - core)):
             upper = upper_rows(facts, side, s, (rows, lanes))
-            at = pl.multiple_of((2 * s + side) * rows, rows)
-            y_ref[pl.ds(at, rows), :] = choose(upper, ref[s], ref[s + quarter])
-
-    stores = [pltpu.make_async_copy(y_ref, y_hbm, y_sem)]
-    stores[0].start()
-    hdim = 128
-    scaling = hdim ** (-0.5)
-    count = half // TILE
-    for qi in range(count):
-        base = block_base(qi, shift, count)
-        span = pl.ds(base, TILE)
-        place = order_of(base, (TILE, 1), 0, shift, half)
-        first, inv_length = query_terms(place, bound, half)
-        query = y_ref[span, 256:384]
-        attention = 0.0
-        for ki in needed_keys(qi, count):
-            key_base = block_base(ki, shift, count)
-            keys = pl.ds(key_base, TILE)
-            scores = nt_dot(query, y_ref[keys, 384:512]) * scaling
-            at = order_of(key_base, (1, TILE), 1, shift, half)
-            allowed = (at <= place) & (at >= first)
-            weights = jnp.where(
-                allowed, scores * jax.nn.sigmoid(scores) * inv_length, 0.0
-            ).astype(BF16)
-            attention += nn_dot(weights, y_ref[keys, 128:256])
-
-        att_ref[span, :] = attention
-        stores.append(
-            pltpu.make_async_copy(att_ref.at[span], att_hbm.at[span], att_sems.at[qi])
-        )
-        stores[-1].start()
-        gated = y_ref[span, 0:128].astype(F32)
-        center = jnp.mean(attention, axis=1, keepdims=True)
+            y_ref[rows_of(facts, s, side, rows, half), :] = choose(upper, ref[s], ref[s + quarter])
+    for base in range(0, half, TILE):
+        span = slice(base, base + TILE)
+        grad_ref[:, span] = y_ref[span, 0:128].astype(F32).T.astype(BF16)
+        turned[:, span] = y_ref[span, 128:256].astype(F32).T.astype(BF16)
+    for base, keys in blocks_of(half):
+        span = slice(base, base + TILE)
+        half_scores = nt_dot(y_ref[0:keys, 384:512], y_ref[span, 256:384]) * (0.5 * hdim**-0.5)
+        weights = (silu_parts(half_scores)[1] * share_of(facts, base, keys, half)).astype(BF16)
+        attention = nn_dot(turned[:, 0:keys], weights)
+        att_ref[:, span] = attention
+        gated = grad_ref[:, span].astype(F32)
+        center = jnp.mean(attention, axis=0, keepdims=True)
         shifted = attention - center
-        columns = [
+        lines = [
             center,
-            jnp.sum(shifted * shifted, axis=1, keepdims=True),
-            jnp.sum(gated, axis=1, keepdims=True),
-            jnp.sum(gated * shifted, axis=1, keepdims=True),
+            jnp.sum(shifted * shifted, axis=0, keepdims=True),
+            jnp.sum(gated, axis=0, keepdims=True),
+            jnp.sum(gated * shifted, axis=0, keepdims=True),
         ]
-        lane = iota((TILE, 128), 1)
-        table = jnp.zeros((TILE, 128), F32)
-        for i, column in enumerate(columns):
-            table = jnp.where(lane == i, column, table)
-        turned = table.T[0:4]
+        line = iota((8, TILE), 0)
+        table = jnp.zeros((8, TILE), F32)
+        for i, values in enumerate(lines):
+            table = jnp.where(line == i, values, table)
         for h in range(heads):
-            stats_ref[h, :, span] = turned
-    for store in stores:
-        store.wait()
+            stats_ref[h, :, span] = table[0:4]
 
 
 def backward_kernel(
-    facts, y_hbm, att_hbm, stats_ref, mine_ref, send_ref, y_ref, att_ref, attn, grad, dq, dk, dv, sems
+    facts, y_ref, att_ref, gated_ref, stats_ref, mine_ref, send_ref, attn, grad, dq, dk, dv
 ):
-    core, shift, bound = facts[0], facts[1], facts[2]
-    rows_in = [
-        pltpu.make_async_copy(att_hbm, att_ref, sems.at[0]),
-        pltpu.make_async_copy(y_hbm, y_ref, sems.at[1]),
-    ]
-    for load in rows_in:
-        load.start()
+    core = facts[0]
     half = y_ref.shape[0]
     heads = stats_ref.shape[0]
     quarter, rows = mine_ref.shape[0], mine_ref.shape[1]
-    hdim = 128
+    hdim = att_ref.shape[0]
     width = heads * hdim
-    count = half // TILE
     stat = [[stats_ref[h, i : i + 1, :] for i in range(4)] for h in range(heads)]
     mean = sum(s[0] for s in stat) / heads
     variance, mean_grad, mean_prod = 0.0, 0.0, 0.0
@@ -269,69 +260,45 @@
         mean_grad += grad_sum
         mean_prod += prod_sum + offset * grad_sum
     inv_attn = lax.rsqrt(variance / width + EPSILON)
-    line = iota((128, half), 0)
-    table = jnp.where(
-        line == 0,
-        mean,
-        jnp.where(
-            line == 1,
-            inv_attn,
-            jnp.where(line == 2, mean_grad / width, inv_attn * mean_prod / width),
-        ),
-    )
-    columns = table.T
-    for load in rows_in:
-        load.wait()
-    for qi in range(count):
-        span = slice(qi * TILE, (qi + 1) * TILE)
-        inv = columns[span, 1:2]
-        attn_norm = (att_ref[span, :] - columns[span, 0:1]) * inv
-        gated = y_ref[span, 0:128].astype(F32)
-        attn[span, :] = attn_norm.astype(BF16)
-        grad[span, :] = (
-            inv * (gated - columns[span, 2:3] - attn_norm * columns[span, 3:4])
+    mean_grad = mean_grad / width
+    mean_prod = inv_attn * mean_prod / width
+    for base in range(0, half, TILE):
+        span = slice(base, base + TILE)
+        inv = inv_attn[:, span]
+        attn_norm = (att_ref[:, span] - mean[:, span]) * inv
+        attn[span, :] = attn_norm.T.astype(BF16)
+        gated = gated_ref[:, span].astype(F32)
+        grad[:, span] = (
+            inv * (gated - mean_grad[:, span] - attn_norm * mean_prod[:, span])
         ).astype(BF16)
-    dq[...] = jnp.zeros_like(dq)
-    scaling = hdim ** (-0.5)
-    for ki in range(count):
-        key_base = block_base(ki, shift, count)
-        keys = pl.ds(key_base, TILE)
-        at = order_of(key_base, (TILE, 1), 0, shift, half)
-        key, value = y_ref[keys, 384:512], y_ref[keys, 128:256]
-        grad_key, grad_value = 0.0, 0.0
-        for qi in range(count):
-            if ki not in needed_keys(qi, count):
-                continue
-            base = block_base(qi, shift, count)
-            span = pl.ds(base, TILE)
-            place = order_of(base, (1, TILE), 1, shift, half)
-            first, inv_length = query_terms(place, bound, half)
-            query, grad_out = y_ref[span, 256:384], grad[span, :]
-            scores = nt_dot(key, query) * scaling
-            allowed = (at <= place) & (at >= first)
-            sig = jax.nn.sigmoid(scores)
-            product = scores * sig
-            weights = jnp.where(allowed, product * inv_length, 0.0).astype(BF16)
-            slope = (sig + product * (1.0 - sig)) * (inv_length * scaling)
-            grad_weights = nt_dot(value, grad_out)
-            grad_scores = jnp.where(allowed, grad_weights * slope, 0.0).astype(BF16)
-            grad_value += nn_dot(weights, grad_out)
-            grad_key += nn_dot(grad_scores, query)
-            dq[span, :] += tn_dot(grad_scores, key)
-        dk[keys, :] = grad_key.astype(BF16)
-        dv[keys, :] = grad_value.astype(BF16)
-
+    scaling = 0.5 * hdim**-0.5
+    for base, keys in blocks_of(half):
+        span = slice(base, base + TILE)
+        key, query, grad_out = y_ref[0:keys, 384:512], y_ref[span, 256:384], grad[:, span]
+        share = share_of(facts, base, keys, half)
+        twice, product = silu_parts(nt_dot(key, query) * scaling)
+        weights = (product * share).astype(BF16)
+        slope = (twice + product * (2.0 - twice)) * share
+        grad_scores = (nn_dot(y_ref[0:keys, 128:256], grad_out) * slope).astype(BF16)
+        grad_value = nt_dot(weights, grad_out)
+        grad_key = nn_dot(grad_scores, query)
+        dq[span, :] = (tn_dot(grad_scores, key) * scaling).astype(BF16)
+        if base == 0:
+            dv[...] = grad_value
+            dk[...] = grad_key
+        else:
+            dv[0:keys, :] += grad_value
+            dk[0:keys, :] += grad_key
     for s in range(quarter):
-        near = pl.ds(pl.multiple_of((2 * s + core) * rows, rows), rows)
-        far = pl.ds(pl.multiple_of((2 * s + 1 - core) * rows, rows), rows)
-        for i, ref in enumerate((attn, dv, dq, dk)):
-            columns = slice(i * hdim, (i + 1) * hdim)
-            mine_ref[s, :, columns] = ref[near, :].astype(BF16)
-            send_ref[s, :, columns] = ref[far, :].astype(BF16)
+        for out_ref, side in ((mine_ref, core), (send_ref, 1 - core)):
+            at = rows_of(facts, s, side, rows, half)
+            parts = (attn[at, :], dv[at, :], dq[at, :], dk[at, :] * scaling)
+            for i, part in enumerate(parts):
+                out_ref[s, :, i * hdim : (i + 1) * hdim] = part.astype(BF16)
 
 
 def finish_kernel(
-    back_ref, proj_ref, mixed_ref, gate_ref, slot_ref, embed_ref, cot_ref, weight_hbm, out_ref, gated_ref, weight_ref, sems
+    back_ref, proj_ref, mixed_ref, gate_ref, slot_ref, embed_ref, cot_ref, weight_hbm, out_ref, gated_hbm, weight_ref, gated_ref, sems, sem
 ):
     heads = back_ref.shape[0]
     width = embed_ref.shape[1]
@@ -350,14 +317,17 @@
                 gated_ref[:, columns] = (grad_act * gate_ref[:, columns].astype(F32)).astype(BF16)
                 grad_act = grad_act * mixed_ref[:, columns]
             projected = proj_ref[:, base : base + 256]
-            sig = jax.nn.sigmoid(projected)
-            slope = sig * (1.0 + projected * (1.0 - sig))
+            twice, active = silu_parts(0.5 * projected)
+            slope = 0.5 * (twice + active * (2.0 - twice))
             total += nt_dot((grad_act * slope).astype(BF16), weight_ref[:, base : base + 256])
+    store = pltpu.make_async_copy(gated_ref, gated_hbm, sem)
+    store.start()
     normed, inv_embed = normalize(embed_ref[...])
     grad_embed = cot_ref[...].astype(F32) + normalize_back(total, normed, inv_embed)
     slots, rows = out_ref.shape[0], slot_ref.shape[1]
     place = jnp.where(slot_ref[...] == iota((slots, rows), 0), 1.0, 0.0).astype(BF16)
     out_ref[...] = nn_dot(place, grad_embed.astype(BF16)).astype(BF16)
+    store.wait()
 
 
 def table_kernel(incoming_ref, arrived_ref, scale_ref, out_ref, buffer, sems):
@@ -448,15 +418,23 @@
     fetched = kernel(
         fetch_kernel,
         "fetch",
-        [vmem, hbm, vmem],
+        [vmem, hbm, hbm],
         vmem,
         shape((slots, wide), BF16),
         16,
-        (pltpu.VMEM((table_size, width), BF16), dma((width // 512,))),
-    )(incoming, far(table_rows), scale_line)
+        (
+            pltpu.VMEM((table_size, width), BF16),
+            pltpu.VMEM((1, table_size), F32),
+            dma((width // 512,)),
+            dma(()),
+        ),
+    )(incoming, far(table_rows), far(scale_line))
     returned = to_all(fetched)
 
-    grad_mixed = jnp.einsum("rk,dk->rd", cotangent, output_weight, preferred_element_type=F32)
+    output_far = far(output_weight)
+    grad_mixed = kernel(
+        mix_kernel, "mix", [vmem] * 2, vmem, shape((rows, width), F32), 8
+    )(cotangent, output_far)
 
     near_weight = (pltpu.VMEM((width, 4 * width), BF16), dma((4,)))
     packed, projected, embedded, gate = kernel(
@@ -476,38 +454,38 @@
 
     branches = to_heads(packed)
     received = lax.ppermute(branches, "cp", swap)
-    ordered, attention, stats = kernel(
+    ordered, attention, gated, stats = kernel(
         attend_kernel,
         "attend",
         [smem, vmem, vmem],
-        (hbm, hbm, vmem),
+        (vmem, vmem, vmem, vmem),
         (
-            pltpu.HBM((half, 4 * hdim), BF16),
-            pltpu.HBM((half, hdim), F32),
+            shape((half, 4 * hdim), BF16),
+            shape((hdim, half), F32),
+            shape((hdim, half), BF16),
             shape((heads, 4, half), F32),
         ),
         16,
-        (
-            pltpu.VMEM((half, 4 * hdim), BF16),
-            pltpu.VMEM((half, hdim), F32),
-            dma(()),
-            dma((half // TILE,)),
-        ),
+        (pltpu.VMEM((hdim, half), BF16),),
     )(facts, branches, received)
     stats = to_heads(stats)
 
     backed = shape((quarter, rows, 4 * hdim), BF16)
-    near = pltpu.VMEM((half, hdim), BF16)
     mine, send = kernel(
         backward_kernel,
         "backward",
-        [smem, hbm, hbm, vmem],
+        [smem, vmem, vmem, vmem, vmem],
         (vmem, vmem),
         (backed, backed),
         24,
-        (pltpu.VMEM((half, 4 * hdim), BF16), pltpu.VMEM((half, hdim), F32))
-        + (near, near, pltpu.VMEM((half, hdim), F32), near, near, dma((2,))),
-    )(facts, far(ordered), far(attention), stats)
+        (
+            pltpu.VMEM((half, hdim), BF16),
+            pltpu.VMEM((hdim, half), BF16),
+            pltpu.VMEM((half, hdim), BF16),
+            pltpu.VMEM((half, hdim), F32),
+            pltpu.VMEM((half, hdim), F32),
+        ),
+    )(facts, ordered, attention, gated, stats)
     received = lax.ppermute(send, "cp", swap)
     joined = kernel(
         join_kernel,
@@ -523,15 +501,15 @@
         finish_kernel,
         "finish",
         [vmem] * 7 + [hbm],
-        (vmem, vmem),
-        (shape((slots, width), BF16), shape((rows, width), BF16)),
+        (vmem, hbm),
+        (shape((slots, width), BF16), pltpu.HBM((rows, width), BF16)),
         24,
-        near_weight,
+        (near_weight[0], pltpu.VMEM((rows, width), BF16), near_weight[1], dma(())),
     )(back, projected, grad_mixed, gate, slot_line, embedded, cotangent, weight_far)
     arrived = to_all(outgoing)
-    layer_out = (
-        embedded + jnp.dot(mixed, output_weight, preferred_element_type=F32)
-    ).astype(BF16)
+    layer_out = kernel(
+        output_kernel, "output", [vmem] * 3, vmem, shape((rows, width), BF16), 8
+    )(embedded, mixed, output_far)
 
     table_grad = kernel(
         table_kernel,

time: 150 us -> 143 us (0.953)
  waiting for transfers between devices: 29.4 us -> 25.5 us
  local copies, waits for them, and re-layouts: 5.77 us -> 3.55 us
  matrix products: 1.98 us -> 0 us
  Pallas kernels: 29.8 us -> 31.5 us
    all_to_all x2, waiting for transfers between devices: 25.6 us -> 21.7 us  [exchange(): lax.all_to_all(values, axes, split_axis=0, concat_axis=0, tiled=True, **o...]
    dot_general x2 -> x0, matrix products: 1.98 us -> none  [the longest x1 1.15 us: per_device(): jnp.dot(mixed, output_weight, preferred_element_type=F32)]
    reshape x2, local copies, waits for them, and re-layouts: 2.17 us -> 0.42 us  [to_all(): exchange(values.reshape(devices, CAPACITY, lanes), everyone)]
    pallas_call x4 -> x6, Pallas kernels: 19.1 us -> 20.8 us  [the longest x1 5.17 us: per_device(): kernel(finish_kernel, 'finish', [vmem] * 7 + [hbm], (vmem, hbm), (shape((...]
  transfers between devices with their start and end apart: 4 -> 4, of which waited for: 4 -> 4; matrix products, arithmetic and copies ran while one was open for 1% -> 0% of each run, Pallas kernels for 0% -> 4%
where the time goes in v4:
time: 143 us; the launch traced here: 142 us
  blocking collectives  66.4 us (46%)
  Pallas kernels  31.5 us (22%)
  waiting for transfers between devices  25.5 us (18%)
  starting transfers between devices  14.4 us (10%)
  local copies, waits for them, and re-layouts  3.55 us (2%)
    all_to_all x4, blocking collectives, exchange(): lax.all_to_all(values, axes, split_axis=0, concat_axis=0, tiled=True, **o...  66.4 us
    all_to_all x2, waiting for transfers between devices, exchange(): lax.all_to_all(values, axes, split_axis=0, concat_axis=0, tiled=True, **o...  21.7 us
    all_to_all x2, starting transfers between devices, exchange(): lax.all_to_all(values, axes, split_axis=0, concat_axis=0, tiled=True, **o...  10.2 us
    pallas_call x1, Pallas kernels, per_device(): kernel(finish_kernel, 'finish', [vmem] * 7 + [hbm], (vmem, hbm), (shape((...  5.17 us
    pallas_call x1, Pallas kernels, per_device(): kernel(project_kernel, 'project', [vmem] * 3 + [hbm], (vmem, vmem, vmem,...  4.53 us
    pallas_call x1, Pallas kernels, per_device(): kernel(backward_kernel, 'backward', [smem, vmem, vmem, vmem, vmem], (vmem...  4.21 us
    pallas_call x1, Pallas kernels, per_device(): kernel(table_kernel, 'table', [vmem] * 3, hbm, shape((table_size, width),...  3.67 us
    pallas_call x1, Pallas kernels, per_device(): kernel(fetch_kernel, 'fetch', [vmem, hbm, hbm], vmem, shape((slots, wide)...  3.24 us
  transfers between devices with their start and end apart: 4, of which 4 were waited for; matrix products, arithmetic and copies ran while one was open for 0% of the time, Pallas kernels for 4%

profile of v4, /device:TPU:1, one launch (start us, length us, event | category | flops | bytes accessed | tf_op | source)
XLA Modules:
  0.0 142.3 jit_solution(2422420781853845102)
XLA Ops:
  0.6 0.0 copy-start
  0.7 1.7 %request.1 = (s32[128,128]{1,0:T(8,128)}, s32[1,128]{1,0:T(1,128)}, s32[4]{0:T(128)}) custom-call(s32[1]{0:T(128)} %bitcast.core_ref, s32[1,3]{1,0:T(1,128)} %lengths_ref.1, s32[1,128]{1,0:T(1,128)} %bitcast.14, s32[1,128]{1,0:T(1,128)} %bitcast.15), custom_call_target="tpu_custom_call" | custom-call | tf_op jit(solution)/shard_map/request/pallas_call | solution.py:407
  2.3 20.9 %all_to_all.30 = s32[128,1,128]{2,1,0:T(1,128)S(1)} all-to-all(s32[128,1,128]{2,1,0:T(1,128)} %bitcast.13), channel_id=1, replica_groups=mesh['dp'=8,'cp'=16] {'dp','cp'}, dimensions={0} | all-to-all | bytes 131072 | tf_op jit(solution)/shard_map/all_to_all | solution.py:391
  23.3 3.2 %fetch.1 = bf16[256,1152]{1,0:T(8,128)(2,1)S(1)} custom-call(s32[128,128]{1,0:T(8,128)S(1)} %bitcast.9, bf16[2048,1024]{1,0:T(8,128)(2,1)} %table_hbm.1, f32[1,2048]{1,0:T(1,128)} %bitcast.11), custom_call_target="tpu_custom_call" | custom-call | tf_op jit(solution)/shard_map/fetch/pallas_call | solution.py:418
  26.5 1.0 reshape.43
  27.5 4.5 %all-to-all-start.1 = ((bf16[128,2,1152]{2,1,0:T(2,128)(2,1)}), bf16[128,2,1152]{2,1,0:T(2,128)(2,1)S(1)}, u32[]{:S(2)}, u32[]{:S(2)}) async-start(bf16[128,2,1152]{2,1,0:T(2,128)(2,1)} %reshape.43), calls=%async_computation.1 | async-start | bytes 1179648 | tf_op jit(solution)/shard_map/all_to_all | solution.py:391
  32.1 2.4 %mix.1.mixed_ref = f32[128,1024]{1,0:T(8,128)S(1)} custom-call(bf16[128,1024]{1,0:T(8,128)(2,1)S(1)} %copy-done, bf16[1024,1024]{1,0:T(8,128)(2,1)} %weight_ref.3), custom_call_target="tpu_custom_call" | custom-call | tf_op jit(solution)/shard_map/mix/pallas_call | solution.py:435
  34.5 12.0 %all-to-all-done.1 = bf16[128,2,1152]{2,1,0:T(2,128)(2,1)S(1)} async-done(((bf16[128,2,1152]{2,1,0:T(2,128)(2,1)}), bf16[128,2,1152]{2,1,0:T(2,128)(2,1)S(1)}, u32[]{:S(2)}, u32[]{:S(2)}) %all-to-all-start.1) | async-done | bytes 589856 | tf_op jit(solution)/shard_map/all_to_all | solution.py:391
  46.5 0.2 reshape.44.returned_ref
  46.7 4.5 %project.1 = (bf16[8,128,512]{2,1,0:T(8,128)(2,1)S(1)}, f32[128,4096]{1,0:T(8,128)S(1)}, f32[128,1024]{1,0:T(8,128)S(1)}, bf16[128,1024]{1,0:T(8,128)(2,1)S(1)}) custom-call(bf16[256,1152]{1,0:T(8,128)(2,1)S(1)} %reshape.44.returned_ref, s32[1,128]{1,0:T(1,128)S(1)} %copy-done.4, f32[128,1024]{1,0:T(8,128)S(1)} %mix.1.mixed_ref, bf16[1024,4096]{1,0:T(8,128)(2,1)} %weight_hbm.3), custom_call_target="tpu_custom_call" | custom-call | tf_op jit(solution)/shard_map/project/pallas_call | solution.py:440
  51.2 17.9 %all_to_all.31.x_ref = bf16[8,128,512]{2,1,0:T(8,128)(2,1)S(1)} all-to-all(bf16[8,128,512]{2,1,0:T(8,128)(2,1)S(1)} %get-tuple-element.21), channel_id=1, replica_groups={{0,2,4,6,8,10,12,14},{1,3,5,7,9,11,13,15},{16,18,20,22,24,26,28,30},{17..., dimensions={0} | all-to-all | bytes 2097152 | tf_op jit(solution)/shard_map/all_to_all | solution.py:391
  69.1 2.4 %collective-permute-start = (bf16[8,128,512]{2,1,0:T(8,128)(2,1)S(1)}, bf16[8,128,512]{2,1,0:T(8,128)(2,1)S(1)}, u32[]{:S(2)}, u32[]{:S(2)}) collective-permute-start(bf16[8,128,512]{2,1,0:T(8,128)(2,1)S(1)} %all_to_all.31.x_ref), channel_id=1, source_target_pairs={{0,1},{1,0},{2,3},{3,2},{4,5},{5,4},{6,7},{7,6},{8,9},{9,8},{10,11... | collective-permute-start | bytes 3145736 | tf_op jit(solution)/shard_map/ppermute | solution.py:456
  71.6 2.3 %collective-permute-done.received_ref = bf16[8,128,512]{2,1,0:T(8,128)(2,1)S(1)} collective-permute-done((bf16[8,128,512]{2,1,0:T(8,128)(2,1)S(1)}, bf16[8,128,512]{2,1,0:T(8,128)(2,1)S(1)}, u32[]{:S(2)}, u32[]{:S(2)}) %collective-permute-start) | collective-permute-done | bytes 1048608 | tf_op jit(solution)/shard_map/ppermute | solution.py:456
  73.9 3.0 %attend.1 = (bf16[1024,512]{1,0:T(8,128)(2,1)S(1)}, f32[128,1024]{1,0:T(8,128)S(1)}, bf16[128,1024]{1,0:T(8,128)(2,1)S(1)}, f32[8,4,1024]{2,1,0:T(4,128)S(1)}) custom-call(s32[4]{0:T(128)S(1)} %copy-done.3, bf16[8,128,512]{2,1,0:T(8,128)(2,1)S(1)} %all_to_all.31.x_ref, bf16[8,128,512]{2,1,0:T(8,128)(2,1)S(1)} %collective-permute-done.received_ref), custom_call_target="tpu_custom_call" | custom-call | tf_op jit(solution)/shard_map/attend/pallas_call | solution.py:457
  76.8 9.6 %all_to_all.32.stats_ref = f32[8,4,1024]{2,1,0:T(4,128)S(1)} all-to-all(f32[8,4,1024]{2,1,0:T(4,128)S(1)} %get-tuple-element.25), channel_id=1, replica_groups={{0,2,4,6,8,10,12,14},{1,3,5,7,9,11,13,15},{16,18,20,22,24,26,28,30},{17..., dimensions={0} | all-to-all | bytes 262144 | tf_op jit(solution)/shard_map/all_to_all | solution.py:391
  86.5 4.2 %backward.1 = (bf16[4,128,512]{2,1,0:T(8,128)(2,1)S(1)}, bf16[4,128,512]{2,1,0:T(8,128)(2,1)S(1)}) custom-call(s32[4]{0:T(128)S(1)} %copy-done.3, bf16[1024,512]{1,0:T(8,128)(2,1)S(1)} %get-tuple-element.22.y_ref, f32[128,1024]{1,0:T(8,128)S(1)} %get-tuple-element.23.att_ref, bf16[128,1024]{1,0:T(8,128)(2,1)S(1)} %get-tuple-element.24.gated_ref, ...), custom_call_target="tpu_custom_call" | custom-call | tf_op jit(solution)/shard_map/backward/pallas_call | solution.py:474
  90.7 1.7 %collective-permute-start.1 = (bf16[4,128,512]{2,1,0:T(8,128)(2,1)S(1)}, bf16[4,128,512]{2,1,0:T(8,128)(2,1)S(1)}, u32[]{:S(2)}, u32[]{:S(2)}) collective-permute-start(bf16[4,128,512]{2,1,0:T(8,128)(2,1)S(1)} %get-tuple-element.27), channel_id=1, source_target_pairs={{0,1},{1,0},{2,3},{3,2},{4,5},{5,4},{6,7},{7,6},{8,9},{9,8},{10,11... | collective-permute-start | bytes 1572872 | tf_op jit(solution)/shard_map/ppermute | solution.py:489
  92.4 1.5 %collective-permute-done.1.received_ref = bf16[4,128,512]{2,1,0:T(8,128)(2,1)S(1)} collective-permute-done((bf16[4,128,512]{2,1,0:T(8,128)(2,1)S(1)}, bf16[4,128,512]{2,1,0:T(8,128)(2,1)S(1)}, u32[]{:S(2)}, u32[]{:S(2)}) %collective-permute-start.1) | collective-permute-done | bytes 524320 | tf_op jit(solution)/shard_map/ppermute | solution.py:489
  93.9 0.8 join.1
  94.8 18.0 %all_to_all.33.back_ref = bf16[8,128,512]{2,1,0:T(8,128)(2,1)S(1)} all-to-all(bf16[8,128,512]{2,1,0:T(8,128)(2,1)S(1)} %join.1), channel_id=1, replica_groups={{0,2,4,6,8,10,12,14},{1,3,5,7,9,11,13,15},{16,18,20,22,24,26,28,30},{17..., dimensions={0} | all-to-all | bytes 2097152 | tf_op jit(solution)/shard_map/all_to_all | solution.py:391
  112.8 5.2 %finish.1 = (bf16[256,1024]{1,0:T(8,128)(2,1)S(1)}, bf16[128,1024]{1,0:T(8,128)(2,1)}) custom-call(bf16[8,128,512]{2,1,0:T(8,128)(2,1)S(1)} %all_to_all.33.back_ref, f32[128,4096]{1,0:T(8,128)S(1)} %get-tuple-element.28.proj_ref, f32[128,1024]{1,0:T(8,128)S(1)} %mix.1.mixed_ref, bf16[128,1024]{1,0:T(8,128)(2,1)S(1)} %get-tuple-element.29.gate_ref, ...), custom_call_target="tpu_custom_call" | custom-call | tf_op jit(solution)/shard_map/finish/pallas_call | solution.py:500
  118.0 0.0 copy-start.2
  118.0 1.0 reshape.46
  119.0 5.7 %all-to-all-start.5 = ((bf16[128,2,1024]{2,1,0:T(2,128)(2,1)}), bf16[128,2,1024]{2,1,0:T(2,128)(2,1)S(1)}, u32[]{:S(2)}, u32[]{:S(2)}) async-start(bf16[128,2,1024]{2,1,0:T(2,128)(2,1)} %reshape.46), calls=%async_computation.5 | async-start | bytes 1048576 | tf_op jit(solution)/shard_map/all_to_all | solution.py:391
  124.7 0.1 reshape.45.incoming_ref
  124.8 0.0 copy-start.1
  124.8 0.9 copy-done.1
  125.8 2.7 %output.1 = bf16[128,1024]{1,0:T(8,128)(2,1)} custom-call(f32[128,1024]{1,0:T(8,128)S(1)} %get-tuple-element.19.embed_ref, bf16[128,1024]{1,0:T(8,128)(2,1)S(1)} %copy-done.1, bf16[1024,1024]{1,0:T(8,128)(2,1)} %weight_ref.3), custom_call_target="tpu_custom_call" | custom-call | tf_op jit(solution)/shard_map/output/pallas_call | solution.py:510
  128.5 9.8 %all-to-all-done.5 = bf16[128,2,1024]{2,1,0:T(2,128)(2,1)S(1)} async-done(((bf16[128,2,1024]{2,1,0:T(2,128)(2,1)}), bf16[128,2,1024]{2,1,0:T(2,128)(2,1)S(1)}, u32[]{:S(2)}, u32[]{:S(2)}) %all-to-all-start.5) | async-done | bytes 524320 | tf_op jit(solution)/shard_map/all_to_all | solution.py:391
  138.3 0.2 reshape.47.arrived_ref
  138.5 0.0 copy-done.2
  138.5 3.7 %table.1 = f32[2048,1024]{1,0:T(8,128)} custom-call(s32[1,256]{1,0:T(1,128)S(1)} %reshape.45.incoming_ref, bf16[256,1024]{1,0:T(8,128)(2,1)S(1)} %reshape.47.arrived_ref, f32[1,2048]{1,0:T(1,128)S(1)} %bitcast.12), custom_call_target="tpu_custom_call" | custom-call | tf_op jit(solution)/shard_map/table/pallas_call | solution.py:514
  (5 shorter events, 0.0 us)
Async XLA Ops:
  0.6 31.4 %copy-start = (bf16[128,1024]{1,0:T(8,128)(2,1)S(1)}, bf16[128,1024]{1,0:T(8,128)(2,1)}, u32[]{:S(2)}) copy-start(bf16[128,1024]{1,0:T(8,128)(2,1)} %cot_ref.3) | copy-start | bytes 786436
  26.5 20.2 %copy-start.4 = (s32[1,128]{1,0:T(1,128)S(1)}, s32[1,128]{1,0:T(1,128)}, u32[]{:S(2)}) copy-start(s32[1,128]{1,0:T(1,128)} %get-tuple-element.18.slot_ref) | copy-start | bytes 1540
  27.5 18.9 %all-to-all-start.1 = ((bf16[128,2,1152]{2,1,0:T(2,128)(2,1)}), bf16[128,2,1152]{2,1,0:T(2,128)(2,1)S(1)}, u32[]{:S(2)}, u32[]{:S(2)}) async-start(bf16[128,2,1152]{2,1,0:T(2,128)(2,1)} %reshape.43), calls=%async_computation.1 | async-start | bytes 1179648 | tf_op jit(solution)/shard_map/all_to_all | solution.py:391
  46.7 27.2 %copy-start.3 = (s32[4]{0:T(128)S(1)}, s32[4]{0:T(128)}, u32[]{:S(2)}) copy-start(s32[4]{0:T(128)} %get-tuple-element.20.facts) | copy-start | bytes 52
  69.1 4.7 %collective-permute-start = (bf16[8,128,512]{2,1,0:T(8,128)(2,1)S(1)}, bf16[8,128,512]{2,1,0:T(8,128)(2,1)S(1)}, u32[]{:S(2)}, u32[]{:S(2)}) collective-permute-start(bf16[8,128,512]{2,1,0:T(8,128)(2,1)S(1)} %all_to_all.31.x_ref), channel_id=1, source_target_pairs={{0,1},{1,0},{2,3},{3,2},{4,5},{5,4},{6,7},{7,6},{8,9},{9,8},{10,11... | collective-permute-start | bytes 3145736 | tf_op jit(solution)/shard_map/ppermute | solution.py:456
  90.7 3.2 %collective-permute-start.1 = (bf16[4,128,512]{2,1,0:T(8,128)(2,1)S(1)}, bf16[4,128,512]{2,1,0:T(8,128)(2,1)S(1)}, u32[]{:S(2)}, u32[]{:S(2)}) collective-permute-start(bf16[4,128,512]{2,1,0:T(8,128)(2,1)S(1)} %get-tuple-element.27), channel_id=1, source_target_pairs={{0,1},{1,0},{2,3},{3,2},{4,5},{5,4},{6,7},{7,6},{8,9},{9,8},{10,11... | collective-permute-start | bytes 1572872 | tf_op jit(solution)/shard_map/ppermute | solution.py:489
  118.0 20.5 %copy-start.2 = (f32[2048]{0:T(1024)S(1)}, f32[2048]{0:T(1024)}, u32[]{:S(2)}) copy-start(f32[2048]{0:T(1024)} %param.9) | copy-start | bytes 24580
  119.0 19.3 %all-to-all-start.5 = ((bf16[128,2,1024]{2,1,0:T(2,128)(2,1)}), bf16[128,2,1024]{2,1,0:T(2,128)(2,1)S(1)}, u32[]{:S(2)}, u32[]{:S(2)}) async-start(bf16[128,2,1024]{2,1,0:T(2,128)(2,1)} %reshape.46), calls=%async_computation.5 | async-start | bytes 1048576 | tf_op jit(solution)/shard_map/all_to_all | solution.py:391
  124.8 1.0 copy-start.1

commit v5 on v4

--- a/solution.py
+++ b/solution.py
@@ -24,18 +24,17 @@
     return jnp.dot(left, right, preferred_element_type=F32)
 
 
-def copies(source, target, sems, spans):
-    started = [
-        pltpu.make_async_copy(source.at[span], target.at[span], sems.at[n])
-        for n, span in enumerate(spans)
-    ]
-    for copy in started:
-        copy.start()
-    return started
-
-
-def column_spans(total, step):
-    return [(slice(None), slice(base, base + step)) for base in range(0, total, step)]
+def parts_of(source, target, sems, first, axis):
+    loads = []
+    step = target.shape[axis] // sems.shape[0]
+    for n in range(sems.shape[0]):
+        begin, span = [slice(None)] * 2, [slice(None)] * 2
+        begin[axis], span[axis] = pl.ds(first + n * step, step), pl.ds(n * step, step)
+        loads.append(
+            pltpu.make_async_copy(source.at[tuple(begin)], target.at[tuple(span)], sems.at[n])
+        )
+        loads[n].start()
+    return loads
 
 
 def iota(shape, axis):
@@ -97,11 +96,13 @@
     return high, middle, rest - middle
 
 
-def fetch_kernel(incoming_ref, table_hbm, scale_hbm, out_ref, table_ref, scale_ref, sems, scale_sem):
+def fetch_kernel(incoming_ref, upper_ref, table_hbm, scale_hbm, out_ref, lower_ref, scale_ref, sems, scale_sem):
     scale_load = pltpu.make_async_copy(scale_hbm, scale_ref, scale_sem)
     scale_load.start()
-    loads = copies(table_hbm, table_ref, sems, column_spans(table_ref.shape[1], 512))
-    slots, size, width = out_ref.shape[0], table_ref.shape[0], table_ref.shape[1]
+    upper, width = upper_ref.shape
+    loads = parts_of(table_hbm, lower_ref, sems, upper, 0)
+    size = scale_ref.shape[1]
+    slots = out_ref.shape[0] * CAPACITY
     devices = slots // CAPACITY
     device_of = iota((slots, devices), 0) >> 1 == iota((slots, devices), 1)
     spread = jnp.where(device_of, 1.0, 0.0).astype(BF16)
@@ -119,10 +120,14 @@
     pieces = jnp.where(
         lane == 0, high, jnp.where(lane == 1, middle, jnp.where(lane == 2, low, 0.0))
     )
-    out_ref[:, width : width + 128] = pieces.astype(BF16)
-    for n, base in enumerate(range(0, width, 512)):
-        loads[n].wait()
-        out_ref[:, base : base + 512] = nn_dot(hot, table_ref[:, base : base + 512]).astype(BF16)
+    out_ref[:, :, width : width + 128] = pieces.astype(BF16).reshape(devices, CAPACITY, 128)
+    for load in loads:
+        load.wait()
+    for base in range(0, width, 256):
+        columns = slice(base, base + 256)
+        rows = nn_dot(hot[:, :upper], upper_ref[:, columns])
+        rows += nn_dot(hot[:, upper:], lower_ref[:, columns])
+        out_ref[:, :, columns] = rows.astype(BF16).reshape(devices, CAPACITY, 256)
 
 
 def mix_kernel(cot_ref, weight_ref, out_ref):
@@ -137,11 +142,12 @@
     returned_ref, slot_ref, mixed_ref, weight_hbm, packed_ref, proj_ref, embed_ref, gate_ref, weight_ref, sems
 ):
     width = embed_ref.shape[1]
-    loads = copies(weight_hbm, weight_ref, sems, column_spans(4 * width, width))
+    loads = parts_of(weight_hbm, weight_ref, sems, 0, 1)
     heads = packed_ref.shape[0]
-    slots, rows = returned_ref.shape[0], slot_ref.shape[1]
+    devices, capacity, wide = returned_ref.shape
+    slots, rows = devices * capacity, slot_ref.shape[1]
     place = jnp.where(slot_ref[...] == iota((slots, rows), 0), 1.0, 0.0).astype(BF16)
-    total = tn_dot(place, returned_ref[...])
+    total = tn_dot(place, returned_ref[...].reshape(slots, wide))
     scale = total[:, width : width + 1] + (
         total[:, width + 1 : width + 2] + total[:, width + 2 : width + 3]
     )
@@ -302,7 +308,7 @@
 ):
     heads = back_ref.shape[0]
     width = embed_ref.shape[1]
-    loads = copies(weight_hbm, weight_ref, sems, column_spans(4 * width, width))
+    loads = parts_of(weight_hbm, weight_ref, sems, 0, 1)
     total = 0.0
     for t in range(4):
         loads[t].wait()
@@ -324,21 +330,23 @@
     store.start()
     normed, inv_embed = normalize(embed_ref[...])
     grad_embed = cot_ref[...].astype(F32) + normalize_back(total, normed, inv_embed)
-    slots, rows = out_ref.shape[0], slot_ref.shape[1]
+    slots, rows = out_ref.shape[0] * out_ref.shape[1], slot_ref.shape[1]
     place = jnp.where(slot_ref[...] == iota((slots, rows), 0), 1.0, 0.0).astype(BF16)
-    out_ref[...] = nn_dot(place, grad_embed.astype(BF16)).astype(BF16)
+    out_ref[...] = nn_dot(place, grad_embed.astype(BF16)).astype(BF16).reshape(out_ref.shape)
     store.wait()
 
 
 def table_kernel(incoming_ref, arrived_ref, scale_ref, out_ref, buffer, sems):
-    slots = arrived_ref.shape[0]
+    devices, capacity, width = arrived_ref.shape
+    slots = devices * capacity
+    arrived = arrived_ref[...].reshape(slots, width)
     steps = sems.shape[0]
     block = buffer.shape[0] // steps
     copies = []
     for n in range(steps):
         span = pl.ds(n * block, block)
         chosen = incoming_ref[...] - 1 - n * block == iota((block, slots), 0)
-        total = nn_dot(jnp.where(chosen, 1.0, 0.0).astype(BF16), arrived_ref[...])
+        total = nn_dot(jnp.where(chosen, 1.0, 0.0).astype(BF16), arrived)
         scale = jnp.broadcast_to(scale_ref[:, span], (128, block)).T
         buffer[span, :] = total * scale[:, 0:1]
         copies.append(pltpu.make_async_copy(buffer.at[span], out_ref.at[span], sems.at[n]))
@@ -394,13 +402,15 @@
         return exchange(values, "cp", axis_index_groups=groups)
 
     def to_all(values):
-        lanes = values.shape[1]
-        return exchange(values.reshape(devices, CAPACITY, lanes), everyone).reshape(slots, lanes)
+        return exchange(values, everyone)
 
     dma = pltpu.SemaphoreType.DMA
 
     def far(values):
         return pltpu.with_memory_space_constraint(values, pltpu.HBM)
+
+    def near(values):
+        return pltpu.with_memory_space_constraint(values, pltpu.VMEM)
 
     weight_far = far(input_weight)
     scale_line = row_scales.reshape(1, table_size)
@@ -418,17 +428,17 @@
     fetched = kernel(
         fetch_kernel,
         "fetch",
-        [vmem, hbm, hbm],
+        [vmem, vmem, hbm, hbm],
         vmem,
-        shape((slots, wide), BF16),
+        shape((devices, CAPACITY, wide), BF16),
         16,
         (
-            pltpu.VMEM((table_size, width), BF16),
+            pltpu.VMEM((table_size // 2, width), BF16),
             pltpu.VMEM((1, table_size), F32),
-            dma((width // 512,)),
+            dma((2,)),
             dma(()),
         ),
-    )(incoming, far(table_rows), far(scale_line))
+    )(incoming, near(table_rows[: table_size // 2]), far(table_rows), far(scale_line))
     returned = to_all(fetched)
 
     output_far = far(output_weight)
@@ -502,7 +512,7 @@
         "finish",
         [vmem] * 7 + [hbm],
         (vmem, hbm),
-        (shape((slots, width), BF16), pltpu.HBM((rows, width), BF16)),
+        (shape((devices, CAPACITY, width), BF16), pltpu.HBM((rows, width), BF16)),
         24,
         (near_weight[0], pltpu.VMEM((rows, width), BF16), near_weight[1], dma(())),
     )(back, projected, grad_mixed, gate, slot_line, embedded, cotangent, weight_far)

time: 143 us -> 142 us (level)
  blocking collectives: 66.4 us -> 45.5 us
  starting transfers between devices: 14.4 us -> 25.9 us
  waiting for transfers between devices: 25.5 us -> 33.2 us
  Pallas kernels: 31.5 us -> 33.1 us
    all_to_all x4 -> x3, blocking collectives: 66.4 us -> 45.5 us  [exchange(): lax.all_to_all(values, axes, split_axis=0, concat_axis=0, tiled=True, **o...]
    all_to_all x2 -> x3, starting transfers between devices: 10.2 us -> 21.7 us  [exchange(): lax.all_to_all(values, axes, split_axis=0, concat_axis=0, tiled=True, **o...]
    all_to_all x2 -> x3, waiting for transfers between devices: 21.7 us -> 29.4 us  [exchange(): lax.all_to_all(values, axes, split_axis=0, concat_axis=0, tiled=True, **o...]
    reshape x4 -> x0, local copies, waits for them, and re-layouts: 2.45 us -> none  [the longest x2 2.03 us: to_all(): values.reshape(devices, CAPACITY, lanes)]
    slice x0 -> x1, local copies, waits for them, and re-layouts: none -> 1.76 us  [per_device(): table_rows[:table_size // 2]]
  transfers between devices with their start and end apart: 4 -> 5, of which waited for: 4 -> 5; matrix products, arithmetic and copies ran while one was open for 0% -> 1% of each run, Pallas kernels for 4% -> 4%
where the time goes in v5:
time: 142 us; the launch traced here: 141 us
  blocking collectives  45.5 us (32%)
  waiting for transfers between devices  33.2 us (23%)
  Pallas kernels  33.1 us (23%)
  starting transfers between devices  25.9 us (18%)
  local copies, waits for them, and re-layouts  2.87 us (2%)
    all_to_all x3, blocking collectives, exchange(): lax.all_to_all(values, axes, split_axis=0, concat_axis=0, tiled=True, **o...  45.5 us
    all_to_all x3, waiting for transfers between devices, exchange(): lax.all_to_all(values, axes, split_axis=0, concat_axis=0, tiled=True, **o...  29.4 us
    all_to_all x3, starting transfers between devices, exchange(): lax.all_to_all(values, axes, split_axis=0, concat_axis=0, tiled=True, **o...  21.7 us
    pallas_call x1, Pallas kernels, per_device(): kernel(finish_kernel, 'finish', [vmem] * 7 + [hbm], (vmem, hbm), (shape((...  6.37 us
    pallas_call x1, Pallas kernels, per_device(): kernel(project_kernel, 'project', [vmem] * 3 + [hbm], (vmem, vmem, vmem,...  4.54 us
    pallas_call x1, Pallas kernels, per_device(): kernel(backward_kernel, 'backward', [smem, vmem, vmem, vmem, vmem], (vmem...  4.21 us
    pallas_call x1, Pallas kernels, per_device(): kernel(table_kernel, 'table', [vmem] * 3, hbm, shape((table_size, width),...  3.7 us
    pallas_call x1, Pallas kernels, per_device(): kernel(fetch_kernel, 'fetch', [vmem, vmem, hbm, hbm], vmem, shape((device...  3.7 us
  transfers between devices with their start and end apart: 5, of which 5 were waited for; matrix products, arithmetic and copies ran while one was open for 1% of the time, Pallas kernels for 4%

profile of v5, /device:TPU:1, one launch (start us, length us, event | category | flops | bytes accessed | tf_op | source)
XLA Modules:
  0.0 141.5 jit_solution(13784395900770453902)
XLA Ops:
  0.6 1.6 %request.1 = (s32[128,128]{1,0:T(8,128)}, s32[1,128]{1,0:T(1,128)}, s32[4]{0:T(128)}) custom-call(s32[1]{0:T(128)} %bitcast.core_ref, s32[1,3]{1,0:T(1,128)} %lengths_ref.1, s32[1,128]{1,0:T(1,128)} %bitcast.14, s32[1,128]{1,0:T(1,128)} %bitcast.15), custom_call_target="tpu_custom_call" | custom-call | tf_op jit(solution)/shard_map/request/pallas_call | solution.py:417
  2.2 11.5 %all-to-all-start = ((s32[128,1,128]{2,1,0:T(1,128)}), s32[128,1,128]{2,1,0:T(1,128)S(1)}, u32[]{:S(2)}, u32[]{:S(2)}) async-start(s32[128,1,128]{2,1,0:T(1,128)} %bitcast.13), calls=%async_computation | async-start | bytes 131072 | tf_op jit(solution)/shard_map/all_to_all | solution.py:399
  13.7 1.8 %slice.6.upper_ref = bf16[1024,1024]{1,0:T(8,128)(2,1)S(1)} slice(bf16[2048,1024]{1,0:T(8,128)(2,1)} %table_hbm.1), slice={[0:1024], [0:1024]} | slice | bytes 4194304 | tf_op jit(solution)/shard_map/slice | solution.py:441
  15.5 0.0 copy-start
  15.5 7.6 %all-to-all-done = s32[128,1,128]{2,1,0:T(1,128)S(1)} async-done(((s32[128,1,128]{2,1,0:T(1,128)}), s32[128,1,128]{2,1,0:T(1,128)S(1)}, u32[]{:S(2)}, u32[]{:S(2)}) %all-to-all-start) | async-done | bytes 65568 | tf_op jit(solution)/shard_map/all_to_all | solution.py:399
  23.1 3.7 %fetch.1 = bf16[128,2,1152]{2,1,0:T(2,128)(2,1)} custom-call(s32[128,128]{1,0:T(8,128)S(1)} %bitcast.9, bf16[1024,1024]{1,0:T(8,128)(2,1)S(1)} %slice.6.upper_ref, bf16[2048,1024]{1,0:T(8,128)(2,1)} %table_hbm.1, f32[1,2048]{1,0:T(1,128)} %bitcast.11), custom_call_target="tpu_custom_call" | custom-call | tf_op jit(solution)/shard_map/fetch/pallas_call | solution.py:428
  26.8 4.5 %all-to-all-start.1 = ((bf16[128,2,1152]{2,1,0:T(2,128)(2,1)}), bf16[128,2,1152]{2,1,0:T(2,128)(2,1)S(1)}, u32[]{:S(2)}, u32[]{:S(2)}) async-start(bf16[128,2,1152]{2,1,0:T(2,128)(2,1)} %fetch.1), calls=%async_computation.1 | async-start | bytes 1179648 | tf_op jit(solution)/shard_map/all_to_all | solution.py:399
  31.4 0.0 copy-done
  31.4 2.4 %mix.1.mixed_ref = f32[128,1024]{1,0:T(8,128)S(1)} custom-call(bf16[128,1024]{1,0:T(8,128)(2,1)S(1)} %copy-done, bf16[1024,1024]{1,0:T(8,128)(2,1)} %weight_ref.3), custom_call_target="tpu_custom_call" | custom-call | tf_op jit(solution)/shard_map/mix/pallas_call | solution.py:445
  33.8 12.0 %all-to-all-done.1.returned_ref = bf16[128,2,1152]{2,1,0:T(2,128)(2,1)S(1)} async-done(((bf16[128,2,1152]{2,1,0:T(2,128)(2,1)}), bf16[128,2,1152]{2,1,0:T(2,128)(2,1)S(1)}, u32[]{:S(2)}, u32[]{:S(2)}) %all-to-all-start.1) | async-done | bytes 589856 | tf_op jit(solution)/shard_map/all_to_all | solution.py:399
  45.8 0.0 copy-done.4
  45.8 4.5 %project.1 = (bf16[8,128,512]{2,1,0:T(8,128)(2,1)S(1)}, f32[128,4096]{1,0:T(8,128)S(1)}, f32[128,1024]{1,0:T(8,128)S(1)}, bf16[128,1024]{1,0:T(8,128)(2,1)S(1)}) custom-call(bf16[128,2,1152]{2,1,0:T(2,128)(2,1)S(1)} %all-to-all-done.1.returned_ref, s32[1,128]{1,0:T(1,128)S(1)} %copy-done.4, f32[128,1024]{1,0:T(8,128)S(1)} %mix.1.mixed_ref, ...), custom_call_target="tpu_custom_call" | custom-call | tf_op jit(solution)/shard_map/project/pallas_call | solution.py:450
  50.3 17.9 %all_to_all.30.x_ref = bf16[8,128,512]{2,1,0:T(8,128)(2,1)S(1)} all-to-all(bf16[8,128,512]{2,1,0:T(8,128)(2,1)S(1)} %get-tuple-element.21), channel_id=1, replica_groups={{0,2,4,6,8,10,12,14},{1,3,5,7,9,11,13,15},{16,18,20,22,24,26,28,30},{17..., dimensions={0} | all-to-all | bytes 2097152 | tf_op jit(solution)/shard_map/all_to_all | solution.py:399
  68.2 2.4 %collective-permute-start = (bf16[8,128,512]{2,1,0:T(8,128)(2,1)S(1)}, bf16[8,128,512]{2,1,0:T(8,128)(2,1)S(1)}, u32[]{:S(2)}, u32[]{:S(2)}) collective-permute-start(bf16[8,128,512]{2,1,0:T(8,128)(2,1)S(1)} %all_to_all.30.x_ref), channel_id=1, source_target_pairs={{0,1},{1,0},{2,3},{3,2},{4,5},{5,4},{6,7},{7,6},{8,9},{9,8},{10,11... | collective-permute-start | bytes 3145736 | tf_op jit(solution)/shard_map/ppermute | solution.py:466
  70.6 2.3 %collective-permute-done.received_ref = bf16[8,128,512]{2,1,0:T(8,128)(2,1)S(1)} collective-permute-done((bf16[8,128,512]{2,1,0:T(8,128)(2,1)S(1)}, bf16[8,128,512]{2,1,0:T(8,128)(2,1)S(1)}, u32[]{:S(2)}, u32[]{:S(2)}) %collective-permute-start) | collective-permute-done | bytes 1048608 | tf_op jit(solution)/shard_map/ppermute | solution.py:466
  72.9 0.0 copy-done.3
  72.9 3.0 %attend.1 = (bf16[1024,512]{1,0:T(8,128)(2,1)S(1)}, f32[128,1024]{1,0:T(8,128)S(1)}, bf16[128,1024]{1,0:T(8,128)(2,1)S(1)}, f32[8,4,1024]{2,1,0:T(4,128)S(1)}) custom-call(s32[4]{0:T(128)S(1)} %copy-done.3, bf16[8,128,512]{2,1,0:T(8,128)(2,1)S(1)} %all_to_all.30.x_ref, bf16[8,128,512]{2,1,0:T(8,128)(2,1)S(1)} %collective-permute-done.received_ref), custom_call_target="tpu_custom_call" | custom-call | tf_op jit(solution)/shard_map/attend/pallas_call | solution.py:467
  75.9 9.6 %all_to_all.31.stats_ref = f32[8,4,1024]{2,1,0:T(4,128)S(1)} all-to-all(f32[8,4,1024]{2,1,0:T(4,128)S(1)} %get-tuple-element.25), channel_id=1, replica_groups={{0,2,4,6,8,10,12,14},{1,3,5,7,9,11,13,15},{16,18,20,22,24,26,28,30},{17..., dimensions={0} | all-to-all | bytes 262144 | tf_op jit(solution)/shard_map/all_to_all | solution.py:399
  85.5 4.2 %backward.1 = (bf16[4,128,512]{2,1,0:T(8,128)(2,1)S(1)}, bf16[4,128,512]{2,1,0:T(8,128)(2,1)S(1)}) custom-call(s32[4]{0:T(128)S(1)} %copy-done.3, bf16[1024,512]{1,0:T(8,128)(2,1)S(1)} %get-tuple-element.22.y_ref, f32[128,1024]{1,0:T(8,128)S(1)} %get-tuple-element.23.att_ref, bf16[128,1024]{1,0:T(8,128)(2,1)S(1)} %get-tuple-element.24.gated_ref, ...), custom_call_target="tpu_custom_call" | custom-call | tf_op jit(solution)/shard_map/backward/pallas_call | solution.py:484
  89.8 1.7 %collective-permute-start.1 = (bf16[4,128,512]{2,1,0:T(8,128)(2,1)S(1)}, bf16[4,128,512]{2,1,0:T(8,128)(2,1)S(1)}, u32[]{:S(2)}, u32[]{:S(2)}) collective-permute-start(bf16[4,128,512]{2,1,0:T(8,128)(2,1)S(1)} %get-tuple-element.27), channel_id=1, source_target_pairs={{0,1},{1,0},{2,3},{3,2},{4,5},{5,4},{6,7},{7,6},{8,9},{9,8},{10,11... | collective-permute-start | bytes 1572872 | tf_op jit(solution)/shard_map/ppermute | solution.py:499
  91.5 1.5 %collective-permute-done.1.received_ref = bf16[4,128,512]{2,1,0:T(8,128)(2,1)S(1)} collective-permute-done((bf16[4,128,512]{2,1,0:T(8,128)(2,1)S(1)}, bf16[4,128,512]{2,1,0:T(8,128)(2,1)S(1)}, u32[]{:S(2)}, u32[]{:S(2)}) %collective-permute-start.1) | collective-permute-done | bytes 524320 | tf_op jit(solution)/shard_map/ppermute | solution.py:499
  93.0 0.8 join.1
  93.8 18.0 %all_to_all.32.back_ref = bf16[8,128,512]{2,1,0:T(8,128)(2,1)S(1)} all-to-all(bf16[8,128,512]{2,1,0:T(8,128)(2,1)S(1)} %join.1), channel_id=1, replica_groups={{0,2,4,6,8,10,12,14},{1,3,5,7,9,11,13,15},{16,18,20,22,24,26,28,30},{17..., dimensions={0} | all-to-all | bytes 2097152 | tf_op jit(solution)/shard_map/all_to_all | solution.py:399
  111.9 6.4 %finish.1 = (bf16[128,2,1024]{2,1,0:T(2,128)(2,1)}, bf16[128,1024]{1,0:T(8,128)(2,1)}) custom-call(bf16[8,128,512]{2,1,0:T(8,128)(2,1)S(1)} %all_to_all.32.back_ref, f32[128,4096]{1,0:T(8,128)S(1)} %get-tuple-element.28.proj_ref, f32[128,1024]{1,0:T(8,128)S(1)} %mix.1.mixed_ref, bf16[128,1024]{1,0:T(8,128)(2,1)S(1)} %get-tuple-element.29.gate_ref, ...), custom_call_target="tpu_custom_call" | custom-call | tf_op jit(solution)/shard_map/finish/pallas_call | solution.py:510
  118.2 0.0 copy-start.2
  118.2 5.7 %all-to-all-start.5 = ((bf16[128,2,1024]{2,1,0:T(2,128)(2,1)}), bf16[128,2,1024]{2,1,0:T(2,128)(2,1)S(1)}, u32[]{:S(2)}, u32[]{:S(2)}) async-start(bf16[128,2,1024]{2,1,0:T(2,128)(2,1)} %get-tuple-element.31), calls=%async_computation.5 | async-start | bytes 1048576 | tf_op jit(solution)/shard_map/all_to_all | solution.py:399
  124.0 0.1 reshape.31.incoming_ref
  124.1 0.0 copy-start.1
  124.1 0.9 copy-done.1
  125.1 2.7 %output.1 = bf16[128,1024]{1,0:T(8,128)(2,1)} custom-call(f32[128,1024]{1,0:T(8,128)S(1)} %get-tuple-element.19.embed_ref, bf16[128,1024]{1,0:T(8,128)(2,1)S(1)} %copy-done.1, bf16[1024,1024]{1,0:T(8,128)(2,1)} %weight_ref.3), custom_call_target="tpu_custom_call" | custom-call | tf_op jit(solution)/shard_map/output/pallas_call | solution.py:520
  127.8 9.8 %all-to-all-done.5.arrived_ref = bf16[128,2,1024]{2,1,0:T(2,128)(2,1)S(1)} async-done(((bf16[128,2,1024]{2,1,0:T(2,128)(2,1)}), bf16[128,2,1024]{2,1,0:T(2,128)(2,1)S(1)}, u32[]{:S(2)}, u32[]{:S(2)}) %all-to-all-start.5) | async-done | bytes 524320 | tf_op jit(solution)/shard_map/all_to_all | solution.py:399
  137.6 3.7 %table.1 = f32[2048,1024]{1,0:T(8,128)} custom-call(s32[1,256]{1,0:T(1,128)S(1)} %reshape.31.incoming_ref, bf16[128,2,1024]{2,1,0:T(2,128)(2,1)S(1)} %all-to-all-done.5.arrived_ref, f32[1,2048]{1,0:T(1,128)S(1)} %bitcast.12), custom_call_target="tpu_custom_call" | custom-call | tf_op jit(solution)/shard_map/table/pallas_call | solution.py:524
  (3 shorter events, 0.0 us)
Async XLA Ops:
  2.2 20.9 %all-to-all-start = ((s32[128,1,128]{2,1,0:T(1,128)}), s32[128,1,128]{2,1,0:T(1,128)S(1)}, u32[]{:S(2)}, u32[]{:S(2)}) async-start(s32[128,1,128]{2,1,0:T(1,128)} %bitcast.13), calls=%async_computation | async-start | bytes 131072 | tf_op jit(solution)/shard_map/all_to_all | solution.py:399
  15.5 15.9 %copy-start = (bf16[128,1024]{1,0:T(8,128)(2,1)S(1)}, bf16[128,1024]{1,0:T(8,128)(2,1)}, u32[]{:S(2)}) copy-start(bf16[128,1024]{1,0:T(8,128)(2,1)} %cot_ref.3) | copy-start | bytes 786436
  23.1 22.6 %copy-start.4 = (s32[1,128]{1,0:T(1,128)S(1)}, s32[1,128]{1,0:T(1,128)}, u32[]{:S(2)}) copy-start(s32[1,128]{1,0:T(1,128)} %get-tuple-element.18.slot_ref) | copy-start | bytes 1540
  26.8 18.9 %all-to-all-start.1 = ((bf16[128,2,1152]{2,1,0:T(2,128)(2,1)}), bf16[128,2,1152]{2,1,0:T(2,128)(2,1)S(1)}, u32[]{:S(2)}, u32[]{:S(2)}) async-start(bf16[128,2,1152]{2,1,0:T(2,128)(2,1)} %fetch.1), calls=%async_computation.1 | async-start | bytes 1179648 | tf_op jit(solution)/shard_map/all_to_all | solution.py:399
  45.8 27.2 %copy-start.3 = (s32[4]{0:T(128)S(1)}, s32[4]{0:T(128)}, u32[]{:S(2)}) copy-start(s32[4]{0:T(128)} %get-tuple-element.20.facts) | copy-start | bytes 52
  68.2 4.7 %collective-permute-start = (bf16[8,128,512]{2,1,0:T(8,128)(2,1)S(1)}, bf16[8,128,512]{2,1,0:T(8,128)(2,1)S(1)}, u32[]{:S(2)}, u32[]{:S(2)}) collective-permute-start(bf16[8,128,512]{2,1,0:T(8,128)(2,1)S(1)} %all_to_all.30.x_ref), channel_id=1, source_target_pairs={{0,1},{1,0},{2,3},{3,2},{4,5},{5,4},{6,7},{7,6},{8,9},{9,8},{10,11... | collective-permute-start | bytes 3145736 | tf_op jit(solution)/shard_map/ppermute | solution.py:466
  89.8 3.2 %collective-permute-start.1 = (bf16[4,128,512]{2,1,0:T(8,128)(2,1)S(1)}, bf16[4,128,512]{2,1,0:T(8,128)(2,1)S(1)}, u32[]{:S(2)}, u32[]{:S(2)}) collective-permute-start(bf16[4,128,512]{2,1,0:T(8,128)(2,1)S(1)} %get-tuple-element.27), channel_id=1, source_target_pairs={{0,1},{1,0},{2,3},{3,2},{4,5},{5,4},{6,7},{7,6},{8,9},{9,8},{10,11... | collective-permute-start | bytes 1572872 | tf_op jit(solution)/shard_map/ppermute | solution.py:499
  118.2 19.4 %copy-start.2 = (f32[2048]{0:T(1024)S(1)}, f32[2048]{0:T(1024)}, u32[]{:S(2)}) copy-start(f32[2048]{0:T(1024)} %param.9) | copy-start | bytes 24580
  118.2 19.3 %all-to-all-start.5 = ((bf16[128,2,1024]{2,1,0:T(2,128)(2,1)}), bf16[128,2,1024]{2,1,0:T(2,128)(2,1)S(1)}, u32[]{:S(2)}, u32[]{:S(2)}) async-start(bf16[128,2,1024]{2,1,0:T(2,128)(2,1)} %get-tuple-element.31), calls=%async_computation.5 | async-start | bytes 1048576 | tf_op jit(solution)/shard_map/all_to_all | solution.py:399
  124.1 1.0 copy-start.1

commit v6 on v5

--- a/solution.py
+++ b/solution.py
@@ -96,7 +96,9 @@
     return high, middle, rest - middle
 
 
-def fetch_kernel(incoming_ref, upper_ref, table_hbm, scale_hbm, out_ref, lower_ref, scale_ref, sems, scale_sem):
+def fetch_kernel(
+    incoming_ref, upper_ref, table_hbm, scale_hbm, out_hbm, lower_ref, scale_ref, out_ref, sems, scale_sem, out_sems
+):
     scale_load = pltpu.make_async_copy(scale_hbm, scale_ref, scale_sem)
     scale_load.start()
     upper, width = upper_ref.shape
@@ -123,11 +125,21 @@
     out_ref[:, :, width : width + 128] = pieces.astype(BF16).reshape(devices, CAPACITY, 128)
     for load in loads:
         load.wait()
+    stores = []
     for base in range(0, width, 256):
         columns = slice(base, base + 256)
         rows = nn_dot(hot[:, :upper], upper_ref[:, columns])
         rows += nn_dot(hot[:, upper:], lower_ref[:, columns])
         out_ref[:, :, columns] = rows.astype(BF16).reshape(devices, CAPACITY, 256)
+        columns = slice(base, base + 256 if base + 256 < width else width + 128)
+        stores.append(
+            pltpu.make_async_copy(
+                out_ref.at[:, :, columns], out_hbm.at[:, :, columns], out_sems.at[base // 256]
+            )
+        )
+        stores[-1].start()
+    for store in stores:
+        store.wait()
 
 
 def mix_kernel(cot_ref, weight_ref, out_ref):
@@ -304,11 +316,15 @@
 
 
 def finish_kernel(
-    back_ref, proj_ref, mixed_ref, gate_ref, slot_ref, embed_ref, cot_ref, weight_hbm, out_ref, gated_hbm, weight_ref, gated_ref, sems, sem
+    back_ref, proj_ref, mixed_ref, gate_ref, slot_ref, embed_ref, cot_ref, weight_hbm, out_hbm, gated_hbm, weight_ref, gated_ref, out_ref, sems, sem, out_sems
 ):
     heads = back_ref.shape[0]
     width = embed_ref.shape[1]
     loads = parts_of(weight_hbm, weight_ref, sems, 0, 1)
+    normed, inv_embed = normalize(embed_ref[...])
+    cotangent = cot_ref[...].astype(F32)
+    slots, rows = out_ref.shape[0] * out_ref.shape[1], slot_ref.shape[1]
+    place = jnp.where(slot_ref[...] == iota((slots, rows), 0), 1.0, 0.0).astype(BF16)
     total = 0.0
     for t in range(4):
         loads[t].wait()
@@ -326,14 +342,23 @@
             twice, active = silu_parts(0.5 * projected)
             slope = 0.5 * (twice + active * (2.0 - twice))
             total += nt_dot((grad_act * slope).astype(BF16), weight_ref[:, base : base + 256])
-    store = pltpu.make_async_copy(gated_ref, gated_hbm, sem)
-    store.start()
-    normed, inv_embed = normalize(embed_ref[...])
-    grad_embed = cot_ref[...].astype(F32) + normalize_back(total, normed, inv_embed)
-    slots, rows = out_ref.shape[0] * out_ref.shape[1], slot_ref.shape[1]
-    place = jnp.where(slot_ref[...] == iota((slots, rows), 0), 1.0, 0.0).astype(BF16)
-    out_ref[...] = nn_dot(place, grad_embed.astype(BF16)).astype(BF16).reshape(out_ref.shape)
-    store.wait()
+    stores = [pltpu.make_async_copy(gated_ref, gated_hbm, sem)]
+    stores[0].start()
+    grad_embed = cotangent + normalize_back(total, normed, inv_embed)
+    grad_embed = grad_embed.astype(BF16)
+    for n in range(out_sems.shape[0]):
+        step = width // out_sems.shape[0]
+        columns = slice(n * step, (n + 1) * step)
+        placed = nn_dot(place, grad_embed[:, columns]).astype(BF16)
+        out_ref[:, :, columns] = placed.reshape(out_ref.shape[0], out_ref.shape[1], step)
+        stores.append(
+            pltpu.make_async_copy(
+                out_ref.at[:, :, columns], out_hbm.at[:, :, columns], out_sems.at[n]
+            )
+        )
+        stores[-1].start()
+    for store in stores:
+        store.wait()
 
 
 def table_kernel(incoming_ref, arrived_ref, scale_ref, out_ref, buffer, sems):
@@ -425,20 +450,23 @@
     incoming = exchange(requests.reshape(devices, 1, 128), everyone).reshape(devices, 128)
 
     wide = width + 128
+    ahead = table_size * 5 // 8
     fetched = kernel(
         fetch_kernel,
         "fetch",
         [vmem, vmem, hbm, hbm],
-        vmem,
-        shape((devices, CAPACITY, wide), BF16),
+        hbm,
+        pltpu.HBM((devices, CAPACITY, wide), BF16),
         16,
         (
-            pltpu.VMEM((table_size // 2, width), BF16),
+            pltpu.VMEM((table_size - ahead, width), BF16),
             pltpu.VMEM((1, table_size), F32),
+            pltpu.VMEM((devices, CAPACITY, wide), BF16),
             dma((2,)),
             dma(()),
+            dma((width // 256,)),
         ),
-    )(incoming, near(table_rows[: table_size // 2]), far(table_rows), far(scale_line))
+    )(incoming, near(table_rows[:ahead]), far(table_rows), far(scale_line))
     returned = to_all(fetched)
 
     output_far = far(output_weight)
@@ -511,10 +539,17 @@
         finish_kernel,
         "finish",
         [vmem] * 7 + [hbm],
-        (vmem, hbm),
-        (shape((devices, CAPACITY, width), BF16), pltpu.HBM((rows, width), BF16)),
+        (hbm, hbm),
+        (pltpu.HBM((devices, CAPACITY, width), BF16), pltpu.HBM((rows, width), BF16)),
         24,
-        (near_weight[0], pltpu.VMEM((rows, width), BF16), near_weight[1], dma(())),
+        (
+            near_weight[0],
+            pltpu.VMEM((rows, width), BF16),
+            pltpu.VMEM((devices, CAPACITY, width), BF16),
+            near_weight[1],
+            dma(()),
+            dma((2,)),
+        ),
     )(back, projected, grad_mixed, gate, slot_line, embedded, cotangent, weight_far)
     arrived = to_all(outgoing)
     layer_out = kernel(

time: 142 us -> 141 us (level)
  transfers between devices with their start and end apart: 5 -> 5, of which waited for: 5 -> 5; matrix products, arithmetic and copies ran while one was open for 1% -> 2% of each run, Pallas kernels for 4% -> 4%
where the time goes in v6:
time: 141 us
  blocking collectives  45.5 us (32%)
  waiting for transfers between devices  33 us (23%)
  Pallas kernels  32.4 us (23%)
  starting transfers between devices  25.9 us (18%)
  local copies, waits for them, and re-layouts  3.08 us (2%)
    all_to_all x3, blocking collectives, exchange(): lax.all_to_all(values, axes, split_axis=0, concat_axis=0, tiled=True, **o...  45.5 us
    all_to_all x3, waiting for transfers between devices, exchange(): lax.all_to_all(values, axes, split_axis=0, concat_axis=0, tiled=True, **o...  29.2 us
    all_to_all x3, starting transfers between devices, exchange(): lax.all_to_all(values, axes, split_axis=0, concat_axis=0, tiled=True, **o...  21.7 us
    pallas_call x1, Pallas kernels, per_device(): kernel(finish_kernel, 'finish', [vmem] * 7 + [hbm], (hbm, hbm), (pltpu.HB...  5.85 us
    pallas_call x1, Pallas kernels, per_device(): kernel(project_kernel, 'project', [vmem] * 3 + [hbm], (vmem, vmem, vmem,...  4.54 us
    pallas_call x1, Pallas kernels, per_device(): kernel(backward_kernel, 'backward', [smem, vmem, vmem, vmem, vmem], (vmem...  4.21 us
    pallas_call x1, Pallas kernels, per_device(): kernel(table_kernel, 'table', [vmem] * 3, hbm, shape((table_size, width),...  3.69 us
    pallas_call x1, Pallas kernels, per_device(): kernel(fetch_kernel, 'fetch', [vmem, vmem, hbm, hbm], hbm, pltpu.HBM((dev...  3.55 us
  transfers between devices with their start and end apart: 5, of which 5 were waited for; matrix products, arithmetic and copies ran while one was open for 2% of the time, Pallas kernels for 4%

profile of v6, /device:TPU:1, one launch (start us, length us, event | category | flops | bytes accessed | tf_op | source)
XLA Modules:
  0.0 140.8 jit_solution(4658973305424564861)
XLA Ops:
  0.6 1.6 %request.1 = (s32[128,128]{1,0:T(8,128)}, s32[1,128]{1,0:T(1,128)}, s32[4]{0:T(128)}) custom-call(s32[1]{0:T(128)} %bitcast.core_ref, s32[1,3]{1,0:T(1,128)} %lengths_ref.1, s32[1,128]{1,0:T(1,128)} %bitcast.14, s32[1,128]{1,0:T(1,128)} %bitcast.15), custom_call_target="tpu_custom_call" | custom-call | tf_op jit(solution)/shard_map/request/pallas_call | solution.py:442
  2.2 11.5 %all-to-all-start = ((s32[128,1,128]{2,1,0:T(1,128)}), s32[128,1,128]{2,1,0:T(1,128)S(1)}, u32[]{:S(2)}, u32[]{:S(2)}) async-start(s32[128,1,128]{2,1,0:T(1,128)} %bitcast.13), calls=%async_computation | async-start | bytes 131072 | tf_op jit(solution)/shard_map/all_to_all | solution.py:424
  13.7 2.0 %slice.6.upper_ref = bf16[1280,1024]{1,0:T(8,128)(2,1)S(1)} slice(bf16[2048,1024]{1,0:T(8,128)(2,1)} %table_hbm.1), slice={[0:1280], [0:1024]} | slice | bytes 5242880 | tf_op jit(solution)/shard_map/slice | solution.py:469
  15.7 7.4 %all-to-all-done = s32[128,1,128]{2,1,0:T(1,128)S(1)} async-done(((s32[128,1,128]{2,1,0:T(1,128)}), s32[128,1,128]{2,1,0:T(1,128)S(1)}, u32[]{:S(2)}, u32[]{:S(2)}) %all-to-all-start) | async-done | bytes 65568 | tf_op jit(solution)/shard_map/all_to_all | solution.py:424
  23.1 3.6 %fetch.1 = bf16[128,2,1152]{2,1,0:T(2,128)(2,1)} custom-call(s32[128,128]{1,0:T(8,128)S(1)} %bitcast.9, bf16[1280,1024]{1,0:T(8,128)(2,1)S(1)} %slice.6.upper_ref, bf16[2048,1024]{1,0:T(8,128)(2,1)} %table_hbm.1, f32[1,2048]{1,0:T(1,128)} %bitcast.11), custom_call_target="tpu_custom_call" | custom-call | tf_op jit(solution)/shard_map/fetch/pallas_call | solution.py:454
  26.7 4.5 %all-to-all-start.1 = ((bf16[128,2,1152]{2,1,0:T(2,128)(2,1)}), bf16[128,2,1152]{2,1,0:T(2,128)(2,1)S(1)}, u32[]{:S(2)}, u32[]{:S(2)}) async-start(bf16[128,2,1152]{2,1,0:T(2,128)(2,1)} %fetch.1), calls=%async_computation.1 | async-start | bytes 1179648 | tf_op jit(solution)/shard_map/all_to_all | solution.py:424
  31.2 0.0 copy-done
  31.2 2.4 %mix.1.mixed_ref = f32[128,1024]{1,0:T(8,128)S(1)} custom-call(bf16[128,1024]{1,0:T(8,128)(2,1)S(1)} %copy-done, bf16[1024,1024]{1,0:T(8,128)(2,1)} %weight_ref.3), custom_call_target="tpu_custom_call" | custom-call | tf_op jit(solution)/shard_map/mix/pallas_call | solution.py:473
  33.7 12.0 %all-to-all-done.1.returned_ref = bf16[128,2,1152]{2,1,0:T(2,128)(2,1)S(1)} async-done(((bf16[128,2,1152]{2,1,0:T(2,128)(2,1)}), bf16[128,2,1152]{2,1,0:T(2,128)(2,1)S(1)}, u32[]{:S(2)}, u32[]{:S(2)}) %all-to-all-start.1) | async-done | bytes 589856 | tf_op jit(solution)/shard_map/all_to_all | solution.py:424
  45.6 0.0 copy-done.4
  45.6 4.5 %project.1 = (bf16[8,128,512]{2,1,0:T(8,128)(2,1)S(1)}, f32[128,4096]{1,0:T(8,128)S(1)}, f32[128,1024]{1,0:T(8,128)S(1)}, bf16[128,1024]{1,0:T(8,128)(2,1)S(1)}) custom-call(bf16[128,2,1152]{2,1,0:T(2,128)(2,1)S(1)} %all-to-all-done.1.returned_ref, s32[1,128]{1,0:T(1,128)S(1)} %copy-done.4, f32[128,1024]{1,0:T(8,128)S(1)} %mix.1.mixed_ref, ...), custom_call_target="tpu_custom_call" | custom-call | tf_op jit(solution)/shard_map/project/pallas_call | solution.py:478
  50.2 17.9 %all_to_all.30.x_ref = bf16[8,128,512]{2,1,0:T(8,128)(2,1)S(1)} all-to-all(bf16[8,128,512]{2,1,0:T(8,128)(2,1)S(1)} %get-tuple-element.21), channel_id=1, replica_groups={{0,2,4,6,8,10,12,14},{1,3,5,7,9,11,13,15},{16,18,20,22,24,26,28,30},{17..., dimensions={0} | all-to-all | bytes 2097152 | tf_op jit(solution)/shard_map/all_to_all | solution.py:424
  68.0 2.4 %collective-permute-start = (bf16[8,128,512]{2,1,0:T(8,128)(2,1)S(1)}, bf16[8,128,512]{2,1,0:T(8,128)(2,1)S(1)}, u32[]{:S(2)}, u32[]{:S(2)}) collective-permute-start(bf16[8,128,512]{2,1,0:T(8,128)(2,1)S(1)} %all_to_all.30.x_ref), channel_id=1, source_target_pairs={{0,1},{1,0},{2,3},{3,2},{4,5},{5,4},{6,7},{7,6},{8,9},{9,8},{10,11... | collective-permute-start | bytes 3145736 | tf_op jit(solution)/shard_map/ppermute | solution.py:494
  70.5 2.3 %collective-permute-done.received_ref = bf16[8,128,512]{2,1,0:T(8,128)(2,1)S(1)} collective-permute-done((bf16[8,128,512]{2,1,0:T(8,128)(2,1)S(1)}, bf16[8,128,512]{2,1,0:T(8,128)(2,1)S(1)}, u32[]{:S(2)}, u32[]{:S(2)}) %collective-permute-start) | collective-permute-done | bytes 1048608 | tf_op jit(solution)/shard_map/ppermute | solution.py:494
  72.8 0.0 copy-done.3
  72.8 3.0 %attend.1 = (bf16[1024,512]{1,0:T(8,128)(2,1)S(1)}, f32[128,1024]{1,0:T(8,128)S(1)}, bf16[128,1024]{1,0:T(8,128)(2,1)S(1)}, f32[8,4,1024]{2,1,0:T(4,128)S(1)}) custom-call(s32[4]{0:T(128)S(1)} %copy-done.3, bf16[8,128,512]{2,1,0:T(8,128)(2,1)S(1)} %all_to_all.30.x_ref, bf16[8,128,512]{2,1,0:T(8,128)(2,1)S(1)} %collective-permute-done.received_ref), custom_call_target="tpu_custom_call" | custom-call | tf_op jit(solution)/shard_map/attend/pallas_call | solution.py:495
  75.8 9.6 %all_to_all.31.stats_ref = f32[8,4,1024]{2,1,0:T(4,128)S(1)} all-to-all(f32[8,4,1024]{2,1,0:T(4,128)S(1)} %get-tuple-element.25), channel_id=1, replica_groups={{0,2,4,6,8,10,12,14},{1,3,5,7,9,11,13,15},{16,18,20,22,24,26,28,30},{17..., dimensions={0} | all-to-all | bytes 262144 | tf_op jit(solution)/shard_map/all_to_all | solution.py:424
  85.4 4.2 %backward.1 = (bf16[4,128,512]{2,1,0:T(8,128)(2,1)S(1)}, bf16[4,128,512]{2,1,0:T(8,128)(2,1)S(1)}) custom-call(s32[4]{0:T(128)S(1)} %copy-done.3, bf16[1024,512]{1,0:T(8,128)(2,1)S(1)} %get-tuple-element.22.y_ref, f32[128,1024]{1,0:T(8,128)S(1)} %get-tuple-element.23.att_ref, bf16[128,1024]{1,0:T(8,128)(2,1)S(1)} %get-tuple-element.24.gated_ref, ...), custom_call_target="tpu_custom_call" | custom-call | tf_op jit(solution)/shard_map/backward/pallas_call | solution.py:512
  89.6 1.7 %collective-permute-start.1 = (bf16[4,128,512]{2,1,0:T(8,128)(2,1)S(1)}, bf16[4,128,512]{2,1,0:T(8,128)(2,1)S(1)}, u32[]{:S(2)}, u32[]{:S(2)}) collective-permute-start(bf16[4,128,512]{2,1,0:T(8,128)(2,1)S(1)} %get-tuple-element.27), channel_id=1, source_target_pairs={{0,1},{1,0},{2,3},{3,2},{4,5},{5,4},{6,7},{7,6},{8,9},{9,8},{10,11... | collective-permute-start | bytes 1572872 | tf_op jit(solution)/shard_map/ppermute | solution.py:527
  91.3 1.5 %collective-permute-done.1.received_ref = bf16[4,128,512]{2,1,0:T(8,128)(2,1)S(1)} collective-permute-done((bf16[4,128,512]{2,1,0:T(8,128)(2,1)S(1)}, bf16[4,128,512]{2,1,0:T(8,128)(2,1)S(1)}, u32[]{:S(2)}, u32[]{:S(2)}) %collective-permute-start.1) | collective-permute-done | bytes 524320 | tf_op jit(solution)/shard_map/ppermute | solution.py:527
  92.9 0.8 join.1
  93.7 18.0 %all_to_all.32.back_ref = bf16[8,128,512]{2,1,0:T(8,128)(2,1)S(1)} all-to-all(bf16[8,128,512]{2,1,0:T(8,128)(2,1)S(1)} %join.1), channel_id=1, replica_groups={{0,2,4,6,8,10,12,14},{1,3,5,7,9,11,13,15},{16,18,20,22,24,26,28,30},{17..., dimensions={0} | all-to-all | bytes 2097152 | tf_op jit(solution)/shard_map/all_to_all | solution.py:424
  111.7 5.8 %finish.1 = (bf16[128,2,1024]{2,1,0:T(2,128)(2,1)}, bf16[128,1024]{1,0:T(8,128)(2,1)}) custom-call(bf16[8,128,512]{2,1,0:T(8,128)(2,1)S(1)} %all_to_all.32.back_ref, f32[128,4096]{1,0:T(8,128)S(1)} %get-tuple-element.28.proj_ref, f32[128,1024]{1,0:T(8,128)S(1)} %mix.1.mixed_ref, bf16[128,1024]{1,0:T(8,128)(2,1)S(1)} %get-tuple-element.29.gate_ref, ...), custom_call_target="tpu_custom_call" | custom-call | tf_op jit(solution)/shard_map/finish/pallas_call | solution.py:538
  117.6 0.0 copy-start.2
  117.6 5.7 %all-to-all-start.5 = ((bf16[128,2,1024]{2,1,0:T(2,128)(2,1)}), bf16[128,2,1024]{2,1,0:T(2,128)(2,1)S(1)}, u32[]{:S(2)}, u32[]{:S(2)}) async-start(bf16[128,2,1024]{2,1,0:T(2,128)(2,1)} %get-tuple-element.31), calls=%async_computation.5 | async-start | bytes 1048576 | tf_op jit(solution)/shard_map/all_to_all | solution.py:424
  123.3 0.1 reshape.31.incoming_ref
  123.5 0.0 copy-start.1
  123.5 0.9 copy-done.1
  124.4 2.7 %output.1 = bf16[128,1024]{1,0:T(8,128)(2,1)} custom-call(f32[128,1024]{1,0:T(8,128)S(1)} %get-tuple-element.19.embed_ref, bf16[128,1024]{1,0:T(8,128)(2,1)S(1)} %copy-done.1, bf16[1024,1024]{1,0:T(8,128)(2,1)} %weight_ref.3), custom_call_target="tpu_custom_call" | custom-call | tf_op jit(solution)/shard_map/output/pallas_call | solution.py:555
  127.2 9.8 %all-to-all-done.5.arrived_ref = bf16[128,2,1024]{2,1,0:T(2,128)(2,1)S(1)} async-done(((bf16[128,2,1024]{2,1,0:T(2,128)(2,1)}), bf16[128,2,1024]{2,1,0:T(2,128)(2,1)S(1)}, u32[]{:S(2)}, u32[]{:S(2)}) %all-to-all-start.5) | async-done | bytes 524320 | tf_op jit(solution)/shard_map/all_to_all | solution.py:424
  136.9 0.0 copy-done.2
  136.9 3.7 %table.1 = f32[2048,1024]{1,0:T(8,128)} custom-call(s32[1,256]{1,0:T(1,128)S(1)} %reshape.31.incoming_ref, bf16[128,2,1024]{2,1,0:T(2,128)(2,1)S(1)} %all-to-all-done.5.arrived_ref, f32[1,2048]{1,0:T(1,128)S(1)} %bitcast.12), custom_call_target="tpu_custom_call" | custom-call | tf_op jit(solution)/shard_map/table/pallas_call | solution.py:559
  (3 shorter events, 0.0 us)
Async XLA Ops:
  2.2 20.9 %all-to-all-start = ((s32[128,1,128]{2,1,0:T(1,128)}), s32[128,1,128]{2,1,0:T(1,128)S(1)}, u32[]{:S(2)}, u32[]{:S(2)}) async-start(s32[128,1,128]{2,1,0:T(1,128)} %bitcast.13), calls=%async_computation | async-start | bytes 131072 | tf_op jit(solution)/shard_map/all_to_all | solution.py:424
  23.1 8.1 %copy-start = (bf16[128,1024]{1,0:T(8,128)(2,1)S(1)}, bf16[128,1024]{1,0:T(8,128)(2,1)}, u32[]{:S(2)}) copy-start(bf16[128,1024]{1,0:T(8,128)(2,1)} %cot_ref.3) | copy-start | bytes 786436
  23.1 22.5 %copy-start.4 = (s32[1,128]{1,0:T(1,128)S(1)}, s32[1,128]{1,0:T(1,128)}, u32[]{:S(2)}) copy-start(s32[1,128]{1,0:T(1,128)} %get-tuple-element.18.slot_ref) | copy-start | bytes 1540
  26.7 18.9 %all-to-all-start.1 = ((bf16[128,2,1152]{2,1,0:T(2,128)(2,1)}), bf16[128,2,1152]{2,1,0:T(2,128)(2,1)S(1)}, u32[]{:S(2)}, u32[]{:S(2)}) async-start(bf16[128,2,1152]{2,1,0:T(2,128)(2,1)} %fetch.1), calls=%async_computation.1 | async-start | bytes 1179648 | tf_op jit(solution)/shard_map/all_to_all | solution.py:424
  45.6 27.2 %copy-start.3 = (s32[4]{0:T(128)S(1)}, s32[4]{0:T(128)}, u32[]{:S(2)}) copy-start(s32[4]{0:T(128)} %get-tuple-element.20.facts) | copy-start | bytes 52
  68.0 4.7 %collective-permute-start = (bf16[8,128,512]{2,1,0:T(8,128)(2,1)S(1)}, bf16[8,128,512]{2,1,0:T(8,128)(2,1)S(1)}, u32[]{:S(2)}, u32[]{:S(2)}) collective-permute-start(bf16[8,128,512]{2,1,0:T(8,128)(2,1)S(1)} %all_to_all.30.x_ref), channel_id=1, source_target_pairs={{0,1},{1,0},{2,3},{3,2},{4,5},{5,4},{6,7},{7,6},{8,9},{9,8},{10,11... | collective-permute-start | bytes 3145736 | tf_op jit(solution)/shard_map/ppermute | solution.py:494
  89.6 3.2 %collective-permute-start.1 = (bf16[4,128,512]{2,1,0:T(8,128)(2,1)S(1)}, bf16[4,128,512]{2,1,0:T(8,128)(2,1)S(1)}, u32[]{:S(2)}, u32[]{:S(2)}) collective-permute-start(bf16[4,128,512]{2,1,0:T(8,128)(2,1)S(1)} %get-tuple-element.27), channel_id=1, source_target_pairs={{0,1},{1,0},{2,3},{3,2},{4,5},{5,4},{6,7},{7,6},{8,9},{9,8},{10,11... | collective-permute-start | bytes 1572872 | tf_op jit(solution)/shard_map/ppermute | solution.py:527
  117.6 19.4 %copy-start.2 = (f32[2048]{0:T(1024)S(1)}, f32[2048]{0:T(1024)}, u32[]{:S(2)}) copy-start(f32[2048]{0:T(1024)} %param.9) | copy-start | bytes 24580
  117.6 19.4 %all-to-all-start.5 = ((bf16[128,2,1024]{2,1,0:T(2,128)(2,1)}), bf16[128,2,1024]{2,1,0:T(2,128)(2,1)S(1)}, u32[]{:S(2)}, u32[]{:S(2)}) async-start(bf16[128,2,1024]{2,1,0:T(2,128)(2,1)} %get-tuple-element.31), calls=%async_computation.5 | async-start | bytes 1048576 | tf_op jit(solution)/shard_map/all_to_all | solution.py:424
  123.5 1.0 copy-start.1

commit v7 on v6

--- a/solution.py
+++ b/solution.py
@@ -190,7 +190,7 @@
 
 
 def choose(mask, yes, no):
-    return jnp.where(mask, yes.astype(F32), no.astype(F32)).astype(BF16)
+    return jnp.where(mask, yes, no)
 
 
 def join_kernel(facts, mine_ref, received_ref, out_ref):
@@ -327,8 +327,9 @@
     place = jnp.where(slot_ref[...] == iota((slots, rows), 0), 1.0, 0.0).astype(BF16)
     total = 0.0
     for t in range(4):
-        loads[t].wait()
         for pair in range(heads // 2):
+            if pair % 2 == 0:
+                loads[2 * t + pair // 2].wait()
             columns = slice(pair * 256, (pair + 1) * 256)
             lanes = slice(t * 128, (t + 1) * 128)
             base = t * width + pair * 256
@@ -546,7 +547,7 @@
             near_weight[0],
             pltpu.VMEM((rows, width), BF16),
             pltpu.VMEM((devices, CAPACITY, width), BF16),
-            near_weight[1],
+            dma((8,)),
             dma(()),
             dma((2,)),
         ),

time: 141 us -> 141 us (level)
  no operation moved by 1% of the time
where the time goes in v7:
time: 141 us; the launch traced here: 140 us
  blocking collectives  45.5 us (32%)
  waiting for transfers between devices  33 us (23%)
  Pallas kernels  31.8 us (23%)
  starting transfers between devices  25.9 us (18%)
  local copies, waits for them, and re-layouts  3.08 us (2%)
    all_to_all x3, blocking collectives, exchange(): lax.all_to_all(values, axes, split_axis=0, concat_axis=0, tiled=True, **o...  45.5 us
    all_to_all x3, waiting for transfers between devices, exchange(): lax.all_to_all(values, axes, split_axis=0, concat_axis=0, tiled=True, **o...  29.2 us
    all_to_all x3, starting transfers between devices, exchange(): lax.all_to_all(values, axes, split_axis=0, concat_axis=0, tiled=True, **o...  21.7 us
    pallas_call x1, Pallas kernels, per_device(): kernel(finish_kernel, 'finish', [vmem] * 7 + [hbm], (hbm, hbm), (pltpu.HB...  5.68 us
    pallas_call x1, Pallas kernels, per_device(): kernel(project_kernel, 'project', [vmem] * 3 + [hbm], (vmem, vmem, vmem,...  4.54 us
    pallas_call x1, Pallas kernels, per_device(): kernel(backward_kernel, 'backward', [smem, vmem, vmem, vmem, vmem], (vmem...  4.21 us
    pallas_call x1, Pallas kernels, per_device(): kernel(table_kernel, 'table', [vmem] * 3, hbm, shape((table_size, width),...  3.69 us
    pallas_call x1, Pallas kernels, per_device(): kernel(fetch_kernel, 'fetch', [vmem, vmem, hbm, hbm], hbm, pltpu.HBM((dev...  3.55 us
  transfers between devices with their start and end apart: 5, of which 5 were waited for; matrix products, arithmetic and copies ran while one was open for 2% of the time, Pallas kernels for 4%

profile of v7, /device:TPU:1, one launch (start us, length us, event | category | flops | bytes accessed | tf_op | source)
XLA Modules:
  0.0 140.2 jit_solution(16752303203153029224)
XLA Ops:
  0.6 1.6 %request.1 = (s32[128,128]{1,0:T(8,128)}, s32[1,128]{1,0:T(1,128)}, s32[4]{0:T(128)}) custom-call(s32[1]{0:T(128)} %bitcast.core_ref, s32[1,3]{1,0:T(1,128)} %lengths_ref.1, s32[1,128]{1,0:T(1,128)} %bitcast.14, s32[1,128]{1,0:T(1,128)} %bitcast.15), custom_call_target="tpu_custom_call" | custom-call | tf_op jit(solution)/shard_map/request/pallas_call | solution.py:443
  2.2 11.5 %all-to-all-start = ((s32[128,1,128]{2,1,0:T(1,128)}), s32[128,1,128]{2,1,0:T(1,128)S(1)}, u32[]{:S(2)}, u32[]{:S(2)}) async-start(s32[128,1,128]{2,1,0:T(1,128)} %bitcast.13), calls=%async_computation | async-start | bytes 131072 | tf_op jit(solution)/shard_map/all_to_all | solution.py:425
  13.7 2.0 %slice.6.upper_ref = bf16[1280,1024]{1,0:T(8,128)(2,1)S(1)} slice(bf16[2048,1024]{1,0:T(8,128)(2,1)} %table_hbm.1), slice={[0:1280], [0:1024]} | slice | bytes 5242880 | tf_op jit(solution)/shard_map/slice | solution.py:470
  15.7 7.4 %all-to-all-done = s32[128,1,128]{2,1,0:T(1,128)S(1)} async-done(((s32[128,1,128]{2,1,0:T(1,128)}), s32[128,1,128]{2,1,0:T(1,128)S(1)}, u32[]{:S(2)}, u32[]{:S(2)}) %all-to-all-start) | async-done | bytes 65568 | tf_op jit(solution)/shard_map/all_to_all | solution.py:425
  23.1 3.6 %fetch.1 = bf16[128,2,1152]{2,1,0:T(2,128)(2,1)} custom-call(s32[128,128]{1,0:T(8,128)S(1)} %bitcast.9, bf16[1280,1024]{1,0:T(8,128)(2,1)S(1)} %slice.6.upper_ref, bf16[2048,1024]{1,0:T(8,128)(2,1)} %table_hbm.1, f32[1,2048]{1,0:T(1,128)} %bitcast.11), custom_call_target="tpu_custom_call" | custom-call | tf_op jit(solution)/shard_map/fetch/pallas_call | solution.py:455
  26.7 4.5 %all-to-all-start.1 = ((bf16[128,2,1152]{2,1,0:T(2,128)(2,1)}), bf16[128,2,1152]{2,1,0:T(2,128)(2,1)S(1)}, u32[]{:S(2)}, u32[]{:S(2)}) async-start(bf16[128,2,1152]{2,1,0:T(2,128)(2,1)} %fetch.1), calls=%async_computation.1 | async-start | bytes 1179648 | tf_op jit(solution)/shard_map/all_to_all | solution.py:425
  31.2 0.0 copy-done
  31.2 2.4 %mix.1.mixed_ref = f32[128,1024]{1,0:T(8,128)S(1)} custom-call(bf16[128,1024]{1,0:T(8,128)(2,1)S(1)} %copy-done, bf16[1024,1024]{1,0:T(8,128)(2,1)} %weight_ref.3), custom_call_target="tpu_custom_call" | custom-call | tf_op jit(solution)/shard_map/mix/pallas_call | solution.py:474
  33.7 12.0 %all-to-all-done.1.returned_ref = bf16[128,2,1152]{2,1,0:T(2,128)(2,1)S(1)} async-done(((bf16[128,2,1152]{2,1,0:T(2,128)(2,1)}), bf16[128,2,1152]{2,1,0:T(2,128)(2,1)S(1)}, u32[]{:S(2)}, u32[]{:S(2)}) %all-to-all-start.1) | async-done | bytes 589856 | tf_op jit(solution)/shard_map/all_to_all | solution.py:425
  45.6 0.0 copy-done.4
  45.6 4.5 %project.1 = (bf16[8,128,512]{2,1,0:T(8,128)(2,1)S(1)}, f32[128,4096]{1,0:T(8,128)S(1)}, f32[128,1024]{1,0:T(8,128)S(1)}, bf16[128,1024]{1,0:T(8,128)(2,1)S(1)}) custom-call(bf16[128,2,1152]{2,1,0:T(2,128)(2,1)S(1)} %all-to-all-done.1.returned_ref, s32[1,128]{1,0:T(1,128)S(1)} %copy-done.4, f32[128,1024]{1,0:T(8,128)S(1)} %mix.1.mixed_ref, ...), custom_call_target="tpu_custom_call" | custom-call | tf_op jit(solution)/shard_map/project/pallas_call | solution.py:479
  50.2 17.9 %all_to_all.30.x_ref = bf16[8,128,512]{2,1,0:T(8,128)(2,1)S(1)} all-to-all(bf16[8,128,512]{2,1,0:T(8,128)(2,1)S(1)} %get-tuple-element.21), channel_id=1, replica_groups={{0,2,4,6,8,10,12,14},{1,3,5,7,9,11,13,15},{16,18,20,22,24,26,28,30},{17..., dimensions={0} | all-to-all | bytes 2097152 | tf_op jit(solution)/shard_map/all_to_all | solution.py:425
  68.0 2.4 %collective-permute-start = (bf16[8,128,512]{2,1,0:T(8,128)(2,1)S(1)}, bf16[8,128,512]{2,1,0:T(8,128)(2,1)S(1)}, u32[]{:S(2)}, u32[]{:S(2)}) collective-permute-start(bf16[8,128,512]{2,1,0:T(8,128)(2,1)S(1)} %all_to_all.30.x_ref), channel_id=1, source_target_pairs={{0,1},{1,0},{2,3},{3,2},{4,5},{5,4},{6,7},{7,6},{8,9},{9,8},{10,11... | collective-permute-start | bytes 3145736 | tf_op jit(solution)/shard_map/ppermute | solution.py:495
  70.5 2.3 %collective-permute-done.received_ref = bf16[8,128,512]{2,1,0:T(8,128)(2,1)S(1)} collective-permute-done((bf16[8,128,512]{2,1,0:T(8,128)(2,1)S(1)}, bf16[8,128,512]{2,1,0:T(8,128)(2,1)S(1)}, u32[]{:S(2)}, u32[]{:S(2)}) %collective-permute-start) | collective-permute-done | bytes 1048608 | tf_op jit(solution)/shard_map/ppermute | solution.py:495
  72.8 0.0 copy-done.3
  72.8 2.8 %attend.1 = (bf16[1024,512]{1,0:T(8,128)(2,1)S(1)}, f32[128,1024]{1,0:T(8,128)S(1)}, bf16[128,1024]{1,0:T(8,128)(2,1)S(1)}, f32[8,4,1024]{2,1,0:T(4,128)S(1)}) custom-call(s32[4]{0:T(128)S(1)} %copy-done.3, bf16[8,128,512]{2,1,0:T(8,128)(2,1)S(1)} %all_to_all.30.x_ref, bf16[8,128,512]{2,1,0:T(8,128)(2,1)S(1)} %collective-permute-done.received_ref), custom_call_target="tpu_custom_call" | custom-call | tf_op jit(solution)/shard_map/attend/pallas_call | solution.py:496
  75.5 9.6 %all_to_all.31.stats_ref = f32[8,4,1024]{2,1,0:T(4,128)S(1)} all-to-all(f32[8,4,1024]{2,1,0:T(4,128)S(1)} %get-tuple-element.25), channel_id=1, replica_groups={{0,2,4,6,8,10,12,14},{1,3,5,7,9,11,13,15},{16,18,20,22,24,26,28,30},{17..., dimensions={0} | all-to-all | bytes 262144 | tf_op jit(solution)/shard_map/all_to_all | solution.py:425
  85.2 4.2 %backward.1 = (bf16[4,128,512]{2,1,0:T(8,128)(2,1)S(1)}, bf16[4,128,512]{2,1,0:T(8,128)(2,1)S(1)}) custom-call(s32[4]{0:T(128)S(1)} %copy-done.3, bf16[1024,512]{1,0:T(8,128)(2,1)S(1)} %get-tuple-element.22.y_ref, f32[128,1024]{1,0:T(8,128)S(1)} %get-tuple-element.23.att_ref, bf16[128,1024]{1,0:T(8,128)(2,1)S(1)} %get-tuple-element.24.gated_ref, ...), custom_call_target="tpu_custom_call" | custom-call | tf_op jit(solution)/shard_map/backward/pallas_call | solution.py:513
  89.4 1.7 %collective-permute-start.1 = (bf16[4,128,512]{2,1,0:T(8,128)(2,1)S(1)}, bf16[4,128,512]{2,1,0:T(8,128)(2,1)S(1)}, u32[]{:S(2)}, u32[]{:S(2)}) collective-permute-start(bf16[4,128,512]{2,1,0:T(8,128)(2,1)S(1)} %get-tuple-element.27), channel_id=1, source_target_pairs={{0,1},{1,0},{2,3},{3,2},{4,5},{5,4},{6,7},{7,6},{8,9},{9,8},{10,11... | collective-permute-start | bytes 1572872 | tf_op jit(solution)/shard_map/ppermute | solution.py:528
  91.1 1.5 %collective-permute-done.1.received_ref = bf16[4,128,512]{2,1,0:T(8,128)(2,1)S(1)} collective-permute-done((bf16[4,128,512]{2,1,0:T(8,128)(2,1)S(1)}, bf16[4,128,512]{2,1,0:T(8,128)(2,1)S(1)}, u32[]{:S(2)}, u32[]{:S(2)}) %collective-permute-start.1) | collective-permute-done | bytes 524320 | tf_op jit(solution)/shard_map/ppermute | solution.py:528
  92.6 0.7 join.1
  93.3 18.0 %all_to_all.32.back_ref = bf16[8,128,512]{2,1,0:T(8,128)(2,1)S(1)} all-to-all(bf16[8,128,512]{2,1,0:T(8,128)(2,1)S(1)} %join.1), channel_id=1, replica_groups={{0,2,4,6,8,10,12,14},{1,3,5,7,9,11,13,15},{16,18,20,22,24,26,28,30},{17..., dimensions={0} | all-to-all | bytes 2097152 | tf_op jit(solution)/shard_map/all_to_all | solution.py:425
  111.3 5.7 %finish.1 = (bf16[128,2,1024]{2,1,0:T(2,128)(2,1)}, bf16[128,1024]{1,0:T(8,128)(2,1)}) custom-call(bf16[8,128,512]{2,1,0:T(8,128)(2,1)S(1)} %all_to_all.32.back_ref, f32[128,4096]{1,0:T(8,128)S(1)} %get-tuple-element.28.proj_ref, f32[128,1024]{1,0:T(8,128)S(1)} %mix.1.mixed_ref, bf16[128,1024]{1,0:T(8,128)(2,1)S(1)} %get-tuple-element.29.gate_ref, ...), custom_call_target="tpu_custom_call" | custom-call | tf_op jit(solution)/shard_map/finish/pallas_call | solution.py:539
  117.0 0.0 copy-start.2
  117.0 5.7 %all-to-all-start.5 = ((bf16[128,2,1024]{2,1,0:T(2,128)(2,1)}), bf16[128,2,1024]{2,1,0:T(2,128)(2,1)S(1)}, u32[]{:S(2)}, u32[]{:S(2)}) async-start(bf16[128,2,1024]{2,1,0:T(2,128)(2,1)} %get-tuple-element.31), calls=%async_computation.5 | async-start | bytes 1048576 | tf_op jit(solution)/shard_map/all_to_all | solution.py:425
  122.7 0.1 reshape.31.incoming_ref
  122.9 0.0 copy-start.1
  122.9 0.9 copy-done.1
  123.8 2.7 %output.1 = bf16[128,1024]{1,0:T(8,128)(2,1)} custom-call(f32[128,1024]{1,0:T(8,128)S(1)} %get-tuple-element.19.embed_ref, bf16[128,1024]{1,0:T(8,128)(2,1)S(1)} %copy-done.1, bf16[1024,1024]{1,0:T(8,128)(2,1)} %weight_ref.3), custom_call_target="tpu_custom_call" | custom-call | tf_op jit(solution)/shard_map/output/pallas_call | solution.py:556
  126.6 9.8 %all-to-all-done.5.arrived_ref = bf16[128,2,1024]{2,1,0:T(2,128)(2,1)S(1)} async-done(((bf16[128,2,1024]{2,1,0:T(2,128)(2,1)}), bf16[128,2,1024]{2,1,0:T(2,128)(2,1)S(1)}, u32[]{:S(2)}, u32[]{:S(2)}) %all-to-all-start.5) | async-done | bytes 524320 | tf_op jit(solution)/shard_map/all_to_all | solution.py:425
  136.3 0.0 copy-done.2
  136.3 3.7 %table.1 = f32[2048,1024]{1,0:T(8,128)} custom-call(s32[1,256]{1,0:T(1,128)S(1)} %reshape.31.incoming_ref, bf16[128,2,1024]{2,1,0:T(2,128)(2,1)S(1)} %all-to-all-done.5.arrived_ref, f32[1,2048]{1,0:T(1,128)S(1)} %bitcast.12), custom_call_target="tpu_custom_call" | custom-call | tf_op jit(solution)/shard_map/table/pallas_call | solution.py:560
  (3 shorter events, 0.0 us)
Async XLA Ops:
  2.2 20.9 %all-to-all-start = ((s32[128,1,128]{2,1,0:T(1,128)}), s32[128,1,128]{2,1,0:T(1,128)S(1)}, u32[]{:S(2)}, u32[]{:S(2)}) async-start(s32[128,1,128]{2,1,0:T(1,128)} %bitcast.13), calls=%async_computation | async-start | bytes 131072 | tf_op jit(solution)/shard_map/all_to_all | solution.py:425
  23.1 8.1 %copy-start = (bf16[128,1024]{1,0:T(8,128)(2,1)S(1)}, bf16[128,1024]{1,0:T(8,128)(2,1)}, u32[]{:S(2)}) copy-start(bf16[128,1024]{1,0:T(8,128)(2,1)} %cot_ref.3) | copy-start | bytes 786436
  23.1 22.5 %copy-start.4 = (s32[1,128]{1,0:T(1,128)S(1)}, s32[1,128]{1,0:T(1,128)}, u32[]{:S(2)}) copy-start(s32[1,128]{1,0:T(1,128)} %get-tuple-element.18.slot_ref) | copy-start | bytes 1540
  26.7 18.9 %all-to-all-start.1 = ((bf16[128,2,1152]{2,1,0:T(2,128)(2,1)}), bf16[128,2,1152]{2,1,0:T(2,128)(2,1)S(1)}, u32[]{:S(2)}, u32[]{:S(2)}) async-start(bf16[128,2,1152]{2,1,0:T(2,128)(2,1)} %fetch.1), calls=%async_computation.1 | async-start | bytes 1179648 | tf_op jit(solution)/shard_map/all_to_all | solution.py:425
  45.6 27.2 %copy-start.3 = (s32[4]{0:T(128)S(1)}, s32[4]{0:T(128)}, u32[]{:S(2)}) copy-start(s32[4]{0:T(128)} %get-tuple-element.20.facts) | copy-start | bytes 52
  68.0 4.7 %collective-permute-start = (bf16[8,128,512]{2,1,0:T(8,128)(2,1)S(1)}, bf16[8,128,512]{2,1,0:T(8,128)(2,1)S(1)}, u32[]{:S(2)}, u32[]{:S(2)}) collective-permute-start(bf16[8,128,512]{2,1,0:T(8,128)(2,1)S(1)} %all_to_all.30.x_ref), channel_id=1, source_target_pairs={{0,1},{1,0},{2,3},{3,2},{4,5},{5,4},{6,7},{7,6},{8,9},{9,8},{10,11... | collective-permute-start | bytes 3145736 | tf_op jit(solution)/shard_map/ppermute | solution.py:495
  89.4 3.2 %collective-permute-start.1 = (bf16[4,128,512]{2,1,0:T(8,128)(2,1)S(1)}, bf16[4,128,512]{2,1,0:T(8,128)(2,1)S(1)}, u32[]{:S(2)}, u32[]{:S(2)}) collective-permute-start(bf16[4,128,512]{2,1,0:T(8,128)(2,1)S(1)} %get-tuple-element.27), channel_id=1, source_target_pairs={{0,1},{1,0},{2,3},{3,2},{4,5},{5,4},{6,7},{7,6},{8,9},{9,8},{10,11... | collective-permute-start | bytes 1572872 | tf_op jit(solution)/shard_map/ppermute | solution.py:528
  117.0 19.4 %copy-start.2 = (f32[2048]{0:T(1024)S(1)}, f32[2048]{0:T(1024)}, u32[]{:S(2)}) copy-start(f32[2048]{0:T(1024)} %param.9) | copy-start | bytes 24580
  117.0 19.3 %all-to-all-start.5 = ((bf16[128,2,1024]{2,1,0:T(2,128)(2,1)}), bf16[128,2,1024]{2,1,0:T(2,128)(2,1)S(1)}, u32[]{:S(2)}, u32[]{:S(2)}) async-start(bf16[128,2,1024]{2,1,0:T(2,128)(2,1)} %get-tuple-element.31), calls=%async_computation.5 | async-start | bytes 1048576 | tf_op jit(solution)/shard_map/all_to_all | solution.py:425
  122.9 1.0 copy-start.1
